TPU v7x, 256 devices: a whole 4x4x8 slice. The times are simulated.
256 devices in a mesh: lat: 8 (over y, core), lon: 4 (over z_lo), ens: 8 (over x, z_hi).
Axes of the slice: x: 4, y: 4, z: 8 (z_hi: 2, z_lo: 4; z = z_hi * 4 + z_lo), core: 2. Of those that a mesh axis runs over, the one named last changes fastest.
Arguments:
- fields: bfloat16 [8, 96, 64, 640], P('ens', 'lat', 'lon'), may hold values from -6 to 6
- filter_basis: bfloat16 [96, 5, 4, 16], P(('lat', 'lon')), may hold values from -0.625 to 0.625
- lon_offsets: int32 [96, 5, 16], P(('lat', 'lon')), may hold values from -32 to 31, as said below
- conv_weight: bfloat16 [2560, 640], replicated, may hold values from -0.125 to 0.125
- weight_in: bfloat16 [640, 1280], replicated, may hold values from -0.25 to 0.25
- weight_out: bfloat16 [1280, 640], replicated, may hold values from -0.15625 to 0.15625
- cotangent: bfloat16 [8, 96, 64, 640], P('ens', 'lat', 'lon'), may hold values from -6 to 6
Outputs:
- block_out: bfloat16 [8, 96, 64, 640], P('ens', 'lat', 'lon')
- field_grad: bfloat16 [8, 96, 64, 640], P('ens', 'lat', 'lon')
- conv_weight_grad: float32 [2560, 640], P(('lat', 'lon', 'ens'))
- weight_in_grad: float32 [640, 1280], P(None, ('lat', 'lon', 'ens'))
- weight_out_grad: float32 [1280, 640], P(('lat', 'lon', 'ens'))
Inputs may be any that keep to these rules, and one draw needn't show every extreme that they name: `lon_offsets`: within one cycle and one cycle offset the 16 longitude offsets are distinct. In the 2 cycles nearest each pole they lie in -32 to 31; in every other cycle they lie in -16 to 15.
All inputs are finite; a program needn't handle non-finite values.
Results may differ from a plain program's by a relative error of at most 0.015.
Values may be sent and summed in bfloat16 or wider, within the bound.
No kernel may reach another device: no remote copies, remote signals or barrier semaphores. Data moves between devices by JAX's collectives and lax.ppermute only.
A program may use at most 128 MiB of HBM per device.

v0:
```python
import math

import jax
import jax.numpy as jnp
from jax import lax
from jax.experimental import pallas as pl
from jax.experimental.pallas import tpu as pltpu
from jax.sharding import Mesh, PartitionSpec as P


EMBED = 640
HIDDEN = 1280
BASIS = 4
SPAN = 5
NLON = 64
NLAT = 96
MEMBERS = 8
WIDE = BASIS * EMBED

CYCLES = 12
LON = 16
CELLS = CYCLES * LON
OWNED = 3
HALO = 2
RIM = HALO * LON
CONV_PART = EMBED + BASIS * 384
MLP_PART = 3 * EMBED

half_root = 0.7071067811865476
gauss_norm = 0.3989422804014327


LAT = ("y", "core")
bf16 = jnp.bfloat16
f32 = jnp.float32


def dot(a, b, dims):
    return lax.dot_general(a, b, (dims, ((), ())), preferred_element_type=f32)


def shift(block, axis, count, step):
    return lax.ppermute(block, axis, [(i, (i + step) % count) for i in range(count)])


def struct(shape, dtype):
    return jax.ShapeDtypeStruct(shape, dtype)


def fill_window(win, tile, left, right, top, bottom, left_halo, right_halo, far, lat):
    far_zero = jnp.zeros((LON, EMBED), bf16)
    for group, (inner, halo) in enumerate(
        ((left, left_halo), (tile, None), (right, right_halo))
    ):
        for row in range(CYCLES):
            at = (row + HALO) * NLON + group * LON
            win[at : at + LON, :] = inner[row * LON : (row + 1) * LON, :]
        for row in range(HALO):
            upper = top if halo is None else halo
            lower = bottom if halo is None else halo
            shift_rows = 0 if halo is None else bottom.shape[0]
            at = row * NLON + group * LON
            win[at : at + LON, :] = upper[row * LON : (row + 1) * LON, :]
            at = (row + HALO + CYCLES) * NLON + group * LON
            win[at : at + LON, :] = lower[
                shift_rows + row * LON : shift_rows + (row + 1) * LON, :
            ]
    for row in range(CYCLES + 2 * HALO):
        at = row * NLON + 3 * LON
        win[at : at + LON, :] = far_zero

    @pl.when(lat == 0)
    def _():
        for row in range(4):
            at = (row + HALO) * NLON + 3 * LON
            win[at : at + LON, :] = far[row * LON : (row + 1) * LON, :]

    @pl.when(lat == 7)
    def _():
        for row in range(4):
            at = (row + HALO + CYCLES - 4) * NLON + 3 * LON
            win[at : at + LON, :] = far[row * LON : (row + 1) * LON, :]


def set_rows(coef, at, rows):
    for d in range(SPAN):
        coef[d, at : at + rows.shape[0], :] = rows[:, d * 128 : (d + 1) * 128]


def band_rows(win, band, coef, cycle, row_of):
    low_half = lax.broadcasted_iota(jnp.int32, (LON, 2 * NLON), 1) < NLON
    for k in range(BASIS):
        rolled = []
        for d in range(SPAN):
            row, lane = row_of(d, k)
            values = coef[lane, pl.ds(row, 1), :]
            spread_row = jnp.broadcast_to(values, (LON, 2 * NLON))
            rolled.append(pltpu.roll(spread_row, LON, 1, stride=1, stride_axis=0))
        at = k * LON
        band[at : at + LON, 0:128] = jnp.where(low_half, rolled[0], rolled[1]).astype(bf16)
        band[at : at + LON, 128:256] = jnp.where(low_half, rolled[2], rolled[3]).astype(bf16)
        band[at : at + LON, 256:384] = rolled[4].astype(bf16)
    window = win[cycle * NLON : cycle * NLON + SPAN * NLON, :]
    return dot(band[:, 0 : SPAN * NLON], window, ((1,), (0,)))


def forward_kernel(
    place, tile, left, right, top, bottom, left_side, right_side, far, own_e,
    tangent, conv_hbm, in_hbm, out_hbm,
    out, blend_grad, mine, mine_mlp, theirs, theirs_mlp, to_up, to_down, to_far,
    win, band, coef, spread, conv_weight, weight_in, weight_out, sems
):
    lat = place[0]
    lon = place[1]
    core = place[2]
    loads = [
        pltpu.make_async_copy(source, target, sems.at[i])
        for i, (source, target) in enumerate(
            ((conv_hbm, conv_weight), (in_hbm, weight_in), (out_hbm, weight_out))
        )
    ]
    for load in loads:
        load.start()
    fill_window(win, tile, left, right, top, bottom, left_side, right_side, far, lat)
    set_rows(coef, 0, left_side[2 * RIM : 2 * RIM + 32, :].astype(f32))
    set_rows(coef, 32, own_e[...].astype(f32))
    set_rows(coef, 64, right_side[2 * RIM : 2 * RIM + 32, :].astype(f32))
    set_rows(coef, 96, far[4 * LON : 4 * LON + 32, :].astype(f32))

    def base(cycle):
        return lax.rem(cycle // OWNED - lon + 1 + 4, 4) * 32 + (cycle % OWNED) * BASIS

    for i in range(CYCLES):
        start = base(i)
        rows = band_rows(win, band.at[i % 2], coef, i, lambda d, k: (start + k, d))
        for k in range(BASIS):
            spread[i * LON : (i + 1) * LON, k * EMBED : (k + 1) * EMBED] = rows[
                k * LON : (k + 1) * LON, :
            ].astype(bf16)

    loads[0].wait()
    blended = (
        tile[...].astype(f32) + dot(spread[...], conv_weight[...], ((1,), (0,)))
    ).astype(bf16)
    loads[1].wait()
    preact = dot(blended, weight_in[...], ((1,), (0,)))
    cdf = 0.5 * (1.0 + lax.erf(preact * half_root))
    hidden = (preact * cdf).astype(bf16)
    loads[2].wait()
    out[...] = (
        blended.astype(f32) + dot(hidden, weight_out[...], ((1,), (0,)))
    ).astype(bf16)
    slope = cdf + preact * jnp.exp(-0.5 * preact * preact) * gauss_norm
    hidden_grad = dot(tangent[...], weight_out[...], ((1,), (1,)))
    preact_grad = (hidden_grad * slope).astype(bf16)
    grad = (
        tangent[...].astype(f32) + dot(preact_grad, weight_in[...], ((1,), (1,)))
    ).astype(bf16)
    blend_grad[...] = grad
    for side in (theirs, mine):
        side[:, 0:EMBED] = grad
    for side in (theirs_mlp, mine_mlp):
        side[:, 0:EMBED] = blended
    for c in range(2):

        def store(side, side_mlp):
            for k in range(BASIS):
                at = k * EMBED + c * 320
                to = EMBED + k * 384
                side[:, to : to + 320] = spread[:, at : at + 320]
                at = k * 320 + c * 160
                to = EMBED + k * 160
                side_mlp[:, to : to + 160] = hidden[:, at : at + 160]
                side_mlp[:, to + EMBED : to + EMBED + 160] = preact_grad[:, at : at + 160]

        @pl.when(core == c)
        def _():
            store(mine, mine_mlp)

        @pl.when(core != c)
        def _():
            store(theirs, theirs_mlp)

    edges = []
    for cycle in (0, 1, CYCLES - 2, CYCLES - 1):
        start = base(cycle) + 16
        for k in range(BASIS):
            edges.append(
                jnp.concatenate([coef[d, pl.ds(start + k, 1), :] for d in range(SPAN)], axis=1)
            )
    to_up[0:RIM, :] = grad[CELLS - RIM :, :]
    to_up[RIM : RIM + 8, :] = jnp.concatenate(edges[8:], axis=0).astype(bf16)
    to_down[0:RIM, :] = grad[:RIM, :]
    to_down[RIM : RIM + 8, :] = jnp.concatenate(edges[:8], axis=0).astype(bf16)
    to_far[...] = jnp.where(lat == 0, grad[: 4 * LON, :], grad[CELLS - 4 * LON :, :])


def mlp_grad_kernel(place, mine, other, tangent, other_tangent, order, o0, o1, o2, o3, acc):
    x = place[3]
    sides = []
    for side, cot in ((mine, tangent), (other, other_tangent)):
        hidden = dot(side[:, EMBED : 2 * EMBED], order[...], ((1,), (0,))).astype(bf16)
        grad = dot(side[:, 2 * EMBED : 3 * EMBED], order[...], ((1,), (0,))).astype(bf16)
        sides.append((hidden, grad, side[:, 0:EMBED], cot[...]))
    acc[0:EMBED, :] = dot(sides[0][1], sides[0][2], ((0,), (0,))) + dot(
        sides[1][1], sides[1][2], ((0,), (0,))
    )
    acc[EMBED : 2 * EMBED, :] = dot(sides[0][0], sides[0][3], ((0,), (0,))) + dot(
        sides[1][0], sides[1][3], ((0,), (0,))
    )
    for s, o in enumerate((o0, o1, o2, o3)):
        at = pl.multiple_of(lax.rem(x + s, 4) * 160, 160)
        o[0:160, :] = acc[pl.ds(at, 160), :].astype(o.dtype)
        o[160:320, :] = acc[pl.ds(at + EMBED, 160), :].astype(o.dtype)


def conv_grad_kernel(place, mine, other, o0, o1, o2, o3):
    y = place[4]
    for s, o in enumerate((o0, o1, o2, o3)):
        lanes = pl.ds(pl.multiple_of(lax.rem(y + s, 4) * 384 + EMBED, 128), 384)
        rows = dot(mine[:, lanes], mine[:, 0:EMBED], ((0,), (0,))) + dot(
            other[:, lanes], other[:, 0:EMBED], ((0,), (0,))
        )
        o[...] = rows[0:320, :].astype(o.dtype)


def mlp_sum_kernel(place, r0, r1, r2, r3, o0, o1, o2, o3, acc):
    y = place[4]
    acc[...] = r0[...] + r1[...].astype(f32) + r2[...].astype(f32) + r3[...].astype(f32)
    for s, o in enumerate((o0, o1, o2, o3)):
        at = pl.multiple_of(lax.rem(y + s, 4) * 40, 40)
        o[0:40, :] = acc[pl.ds(at, 40), :].astype(o.dtype)
        o[40:80, :] = acc[pl.ds(at + 160, 40), :].astype(o.dtype)


def conv_sum_kernel(place, r0, r1, r2, r3, o0, o1, o2, o3, acc):
    x = place[3]
    total = r0[...] + r1[...].astype(f32) + r2[...].astype(f32) + r3[...].astype(f32)
    for lon in range(4):
        for to in range(4):
            at = lon * 80 + to * 20
            acc[to * 80 + lon * 20 : to * 80 + lon * 20 + 20, :] = total[at : at + 20, :]
    for s, o in enumerate((o0, o1, o2, o3)):
        at = pl.multiple_of(lax.rem(x + s, 4) * 80, 80)
        o[...] = acc[pl.ds(at, 80), :].astype(o.dtype)


def pack_kernel(m0, m1, m2, m3, c0, c1, c2, c3, o):
    mlp = m0[...] + m1[...].astype(f32) + m2[...].astype(f32) + m3[...].astype(f32)
    conv = c0[...] + c1[...].astype(f32) + c2[...].astype(f32) + c3[...].astype(f32)
    for to in range(8):
        o[to, 0:10, :] = conv[to * 10 : to * 10 + 10, :].astype(bf16)
        o[to, 10:15, :] = mlp[to * 5 : to * 5 + 5, :].astype(bf16)
        o[to, 15:20, :] = mlp[40 + to * 5 : 45 + to * 5, :].astype(bf16)


def final_kernel(parts, conv, w_in, w_out):
    total = parts[0].astype(f32)
    for i in range(1, 8):
        total = total + parts[i].astype(f32)
    total = total * (1.0 / math.sqrt(MEMBERS * NLAT * NLON))
    conv[...] = total[0:10, :]
    w_in[...] = total[10:15, :]
    w_out[...] = total[15:20, :]


def field_grad_kernel(
    place, tile, left, right, top, bottom, left_halo, right_halo, far,
    own_e, left_e, right_e, far_e, conv_hbm, field_grad, win, band, coef, mixed,
    conv_weight, sem
):
    lat = place[0]
    lon = place[1]
    load = pltpu.make_async_copy(conv_hbm, conv_weight, sem)
    load.start()
    fill_window(win, tile, left, right, top, bottom, left_halo, right_halo, far, lat)
    set_rows(coef, 0, left_e[2 * RIM : 2 * RIM + 32, :].astype(f32))
    set_rows(coef, 32, own_e[...].astype(f32))
    set_rows(coef, 64, right_e[2 * RIM : 2 * RIM + 32, :].astype(f32))
    set_rows(coef, 96, far_e[4 * LON : 4 * LON + 32, :].astype(f32))
    set_rows(coef, 128, top[HALO * LON : HALO * LON + 8, :].astype(f32))
    set_rows(coef, 136, bottom[HALO * LON : HALO * LON + 8, :].astype(f32))

    def base(cycle):
        if cycle < 0:
            return 128 + (cycle + HALO) * BASIS
        if cycle >= CYCLES:
            return 136 + (cycle - CYCLES) * BASIS
        return (
            lax.rem(cycle // OWNED - lon + 1 + 4, 4) * 32 + 16 + (cycle % OWNED) * BASIS
        )

    for j in range(CYCLES):
        starts = [base(j + e - HALO) for e in range(SPAN)]
        rows = band_rows(
            win, band.at[j % 2], coef, j, lambda e, k: (starts[e] + k, SPAN - 1 - e)
        )
        for k in range(BASIS):
            mixed[j * LON : (j + 1) * LON, k * EMBED : (k + 1) * EMBED] = rows[
                k * LON : (k + 1) * LON, :
            ].astype(bf16)
    total = tile[...].astype(f32)
    load.wait()
    for k in range(BASIS):
        total = total + dot(
            mixed[:, k * EMBED : (k + 1) * EMBED],
            conv_weight[k * EMBED : (k + 1) * EMBED, :],
            ((1,), (1,)),
        )
    field_grad[...] = total.astype(bf16)


def call(kernel, outs, scratch, mib, place, *args, in_hbm=()):
    vmem, hbm = pl.BlockSpec(memory_space=pltpu.VMEM), pl.BlockSpec(memory_space=pltpu.HBM)
    in_specs = [vmem] * len(args) + [hbm] * len(in_hbm)
    args = args + tuple(pltpu.with_memory_space_constraint(a, pltpu.HBM) for a in in_hbm)
    if place is not None:
        in_specs = [pl.BlockSpec(memory_space=pltpu.SMEM)] + in_specs
        args = (place,) + args
    return pl.pallas_call(
        kernel,
        out_shape=outs,
        in_specs=in_specs,
        scratch_shapes=scratch,
        compiler_params=pltpu.CompilerParams(vmem_limit_bytes=mib * 1024 * 1024),
    )(*args)


def polar_rows(tile, lat):
    return jnp.where(lat == 0, tile[: 4 * LON], tile[CELLS - 4 * LON :])


def neighbours(tile, to_up, to_down):
    forward = [(i, i + 1) for i in range(7)]
    backward = [(i + 1, i) for i in range(7)]
    left = shift(tile, "zlo", 4, 1)
    right = shift(tile, "zlo", 4, 3)
    top = lax.ppermute(to_up, LAT, forward)
    bottom = lax.ppermute(to_down, LAT, backward)
    return left, right, top, bottom


def relay(side):
    left_side = shift(side, "zlo", 4, 1)
    right_side = shift(side, "zlo", 4, 3)
    return left_side, right_side


def spread_out(chunks, axis):
    parts = [chunks[0]]
    for s in (1, 2, 3):
        parts.append(shift(chunks[s], axis, 4, s))
    return tuple(parts)


def coefficients(filter_basis, lon_offsets):
    lanes = jnp.arange(2 * NLON, dtype=jnp.int32) % NLON
    values = filter_basis.astype(f32)
    sides = []
    for sign in (1, -1):
        where_to = (sign * lon_offsets) % NLON
        hit = lanes[None, None, None, :] == where_to[:, :, :, None]
        kept = jnp.where(hit[:, None], values.transpose(0, 2, 1, 3)[..., None], 0.0)
        rows = kept.sum(axis=3).astype(bf16).reshape(OWNED * BASIS, SPAN * 2 * NLON)
        sides.append(jnp.pad(rows, ((0, 16 - OWNED * BASIS), (0, 0))))
    return jnp.concatenate(sides, axis=0)


def block(fields, filter_basis, lon_offsets, conv_weight, weight_in, weight_out, cotangent):
    y = lax.axis_index("y")
    core = lax.axis_index("core")
    lon = lax.axis_index("zlo")
    x = lax.axis_index("x")
    lat = 2 * y + core
    place = jnp.stack([lat, lon, core, x, y]).astype(jnp.int32)
    tile = fields.reshape(CELLS, EMBED)
    tangent = cotangent.reshape(CELLS, EMBED)

    left, right, top, bottom = neighbours(tile, tile[CELLS - RIM :], tile[:RIM])
    own_e = coefficients(filter_basis, lon_offsets)
    to_far = jnp.concatenate([polar_rows(tile, lat), own_e], axis=0)
    far = shift(to_far, "zlo", 4, 2)
    left_side, right_side = relay(jnp.concatenate([top, bottom, own_e], axis=0))
    other_tangent = shift(tangent, "core", 2, 1)

    unit = jnp.arange(EMBED, dtype=jnp.int32)
    ux, uy, ul, ur = unit // 160, unit // 40 % 4, unit // 10 % 4, unit % 10
    source = uy * 160 + ul * 40 + ux * 10 + ur
    order = (unit[:, None] == source[None, :]).astype(bf16)

    far, other_tangent, order = lax.optimization_barrier((far, other_tangent, order))
    window = pltpu.VMEM(((CYCLES + 2 * HALO) * NLON, EMBED), bf16)
    band = pltpu.VMEM((2, BASIS * LON, 384), bf16)
    edge = struct((RIM + 8, EMBED), bf16)
    parts = (struct((CELLS, CONV_PART), bf16), struct((CELLS, MLP_PART), bf16))
    block_out, blend_grad, mine, mine_mlp, theirs, theirs_mlp, to_up, to_down, to_far = call(
        forward_kernel,
        (struct((CELLS, EMBED), bf16), struct((CELLS, EMBED), bf16))
        + parts
        + parts
        + (edge, edge, struct((4 * LON, EMBED), bf16)),
        [
            window,
            band,
            pltpu.VMEM((SPAN, 128, 2 * NLON), f32),
            pltpu.VMEM((CELLS, WIDE), bf16),
            pltpu.VMEM((WIDE, EMBED), bf16),
            pltpu.VMEM((EMBED, HIDDEN), bf16),
            pltpu.VMEM((HIDDEN, EMBED), bf16),
            pltpu.SemaphoreType.DMA((3,)),
        ],
        24, place, tile, left, right, top, bottom, left_side, right_side, far, own_e,
        tangent, in_hbm=(conv_weight, weight_in, weight_out),
    )
    other = shift(theirs, "core", 2, 1)
    other_mlp = shift(theirs_mlp, "core", 2, 1)
    g_left, g_right, g_top, g_bottom = neighbours(blend_grad, to_up, to_down)
    g_far = shift(to_far, "zlo", 4, 2)

    chunk = (struct((320, EMBED), f32),) + (struct((320, EMBED), bf16),) * 3
    c = call(conv_grad_kernel, chunk, [], 16, place, mine, other)
    c = spread_out(c, "y")
    m = call(
        mlp_grad_kernel, chunk, [pltpu.VMEM((2 * EMBED, EMBED), f32)],
        16, place, mine_mlp, other_mlp, tangent, other_tangent, order,
    )
    m = spread_out(m, "x")

    g_left_side, g_right_side = relay(jnp.concatenate([g_top, g_bottom], axis=0))
    piece = (struct((80, EMBED), f32),) + (struct((80, EMBED), bf16),) * 3
    total = pltpu.VMEM((320, EMBED), f32)
    c = call(conv_sum_kernel, piece, [total], 8, place, *c)
    c = spread_out(c, "x")
    m = call(mlp_sum_kernel, piece, [total], 8, place, *m)
    m = spread_out(m, "y")
    field_grad = call(
        field_grad_kernel,
        struct((CELLS, EMBED), bf16),
        [
            window,
            band,
            pltpu.VMEM((SPAN, 144, 2 * NLON), f32),
            pltpu.VMEM((CELLS, WIDE), bf16),
            pltpu.VMEM((WIDE, EMBED), bf16),
            pltpu.SemaphoreType.DMA,
        ],
        16, place, blend_grad, g_left, g_right, g_top, g_bottom, g_left_side, g_right_side,
        g_far, own_e, left_side, right_side, far, in_hbm=(conv_weight,),
    )
    m0, field_grad = lax.optimization_barrier((m[0], field_grad))
    packed = call(pack_kernel, struct((8, 20, EMBED), bf16), [], 4, None, m0, *m[1:], *c)
    parts = lax.all_to_all(packed, ("zlo", "zhi"), split_axis=0, concat_axis=0, tiled=True)
    conv_grad, in_grad, out_grad = call(
        final_kernel,
        (struct((10, EMBED), f32), struct((5, EMBED), f32), struct((5, EMBED), f32)),
        [], 4, None, parts,
    )
    return (
        block_out.reshape(fields.shape),
        field_grad.reshape(fields.shape),
        conv_grad,
        in_grad.T,
        out_grad,
    )


def solution(mesh):
    fine = Mesh(mesh.devices.reshape(4, 2, 4, 4, 2), ("y", "core", "zlo", "x", "zhi"))
    tile_spec = P(("x", "zhi"), LAT, "zlo", None)
    everyone = ("y", "core", "zlo", "x", "zhi")
    return jax.shard_map(
        block,
        mesh=fine,
        in_specs=(
            tile_spec,
            P(LAT + ("zlo",), None, None, None),
            P(LAT + ("zlo",), None, None),
            P(),
            P(),
            P(),
            tile_spec,
        ),
        out_specs=(
            tile_spec,
            tile_spec,
            P(everyone, None),
            P(None, everyone),
            P(everyone, None),
        ),
        check_vma=False,
    )
```

profile of v0, /device:TPU:8, one launch (start us, length us, event | category | flops | bytes accessed | tf_op | source)
XLA Modules:
  0.0 118.2 jit_solution(13926167638105652719)
XLA Ops:
  0.7 0.9 fusion.22
  1.5 1.9 %collective-permute-start.2 = (bf16[32,640]{1,0:T(8,128)(2,1)S(1)}, bf16[32,640]{1,0:T(8,128)(2,1)S(1)}, u32[]{:S(2)}, u32[]{:S(2)}) collective-permute-start(bf16[32,640]{1,0:T(8,128)(2,1)S(1)} %bitcast.38), channel_id=1, source_target_pairs={{0,32},{32,64},{64,96},{96,128},{128,160},{160,192},{192,224},{1,3... | collective-permute-start | bytes 122888 | tf_op jit(solution)/shard_map/ppermute | solution.py:338
  3.4 3.6 %collective-permute-start.3 = (bf16[32,640]{1,0:T(8,128)(2,1)S(1)}, bf16[32,640]{1,0:T(8,128)(2,1)S(1)}, u32[]{:S(2)}, u32[]{:S(2)}) collective-permute-start(bf16[32,640]{1,0:T(8,128)(2,1)S(1)} %bitcast.37), channel_id=1, source_target_pairs={{32,0},{64,32},{96,64},{128,96},{160,128},{192,160},{224,192},{33,... | collective-permute-start | bytes 122888 | tf_op jit(solution)/shard_map/ppermute | solution.py:339
  7.1 0.7 add_select_fusion
  7.9 0.7 convert_bitcast_fusion
  8.6 0.9 slice_select_fusion
  9.7 0.3 select_reduce_fusion.1
  10.1 3.4 %collective-permute-start.6 = (bf16[96,640]{1,0:T(8,128)(2,1)S(1)}, bf16[96,640]{1,0:T(8,128)(2,1)S(1)}, u32[]{:S(2)}, u32[]{:S(2)}) collective-permute-start(bf16[96,640]{1,0:T(8,128)(2,1)S(1)} %get-tuple-element.75), channel_id=1, source_target_pairs={{0,16},{8,24},{16,0},{24,8},{1,17},{9,25},{17,1},{25,9},{2,18},{10... | collective-permute-start | bytes 368648 | tf_op jit(solution)/shard_map/ppermute | solution.py:43
  13.5 1.5 %collective-permute-start.1 = (bf16[192,640]{1,0:T(8,128)(2,1)S(1)}, bf16[192,640]{1,0:T(8,128)(2,1)S(1)}, u32[]{:S(2)}, u32[]{:S(2)}) collective-permute-start(bf16[192,640]{1,0:T(8,128)(2,1)S(1)} %bitcast.23), channel_id=1, source_target_pairs={{0,24},{8,0},{16,8},{24,16},{1,25},{9,1},{17,9},{25,17},{2,26},{10... | collective-permute-start | bytes 737288 | tf_op jit(solution)/shard_map/ppermute | solution.py:43
  15.0 0.6 collective-permute-start
  15.6 3.3 %collective-permute-start.5 = (bf16[96,640]{1,0:T(8,128)(2,1)S(1)}, bf16[96,640]{1,0:T(8,128)(2,1)S(1)}, u32[]{:S(2)}, u32[]{:S(2)}) collective-permute-start(bf16[96,640]{1,0:T(8,128)(2,1)S(1)} %get-tuple-element.76), channel_id=1, source_target_pairs={{0,24},{8,0},{16,8},{24,16},{1,25},{9,1},{17,9},{25,17},{2,26},{10... | collective-permute-start | bytes 368648 | tf_op jit(solution)/shard_map/ppermute | solution.py:43
  18.9 1.4 %collective-permute-done.6.far.far_e = bf16[96,640]{1,0:T(8,128)(2,1)S(1)} collective-permute-done((bf16[96,640]{1,0:T(8,128)(2,1)S(1)}, bf16[96,640]{1,0:T(8,128)(2,1)S(1)}, u32[]{:S(2)}, u32[]{:S(2)}) %collective-permute-start.6) | collective-permute-done | bytes 122912 | tf_op jit(solution)/shard_map/ppermute | solution.py:43
  20.3 5.7 %collective-permute-start.4 = (bf16[96,640]{1,0:T(8,128)(2,1)S(1)}, bf16[96,640]{1,0:T(8,128)(2,1)S(1)}, u32[]{:S(2)}, u32[]{:S(2)}) collective-permute-start(bf16[96,640]{1,0:T(8,128)(2,1)S(1)} %get-tuple-element.76), channel_id=1, source_target_pairs={{0,8},{8,16},{16,24},{24,0},{1,9},{9,17},{17,25},{25,1},{2,10},{10... | collective-permute-start | bytes 368648 | tf_op jit(solution)/shard_map/ppermute | solution.py:43
  26.0 0.2 fusion.order
  26.4 4.3 %collective-permute-done.5.right_side.right_e = bf16[96,640]{1,0:T(8,128)(2,1)S(1)} collective-permute-done((bf16[96,640]{1,0:T(8,128)(2,1)S(1)}, bf16[96,640]{1,0:T(8,128)(2,1)S(1)}, u32[]{:S(2)}, u32[]{:S(2)}) %collective-permute-start.5) | collective-permute-done | bytes 122912 | tf_op jit(solution)/shard_map/ppermute | solution.py:43
  30.7 4.0 %collective-permute-done.4.left_side.left_e = bf16[96,640]{1,0:T(8,128)(2,1)S(1)} collective-permute-done((bf16[96,640]{1,0:T(8,128)(2,1)S(1)}, bf16[96,640]{1,0:T(8,128)(2,1)S(1)}, u32[]{:S(2)}, u32[]{:S(2)}) %collective-permute-start.4) | collective-permute-done | bytes 122912 | tf_op jit(solution)/shard_map/ppermute | solution.py:43
  34.7 7.2 %shard_map.110 = (bf16[192,640]{1,0:T(8,128)(2,1)}, bf16[192,640]{1,0:T(8,128)(2,1)S(1)}, bf16[192,2176]{1,0:T(8,128)(2,1)S(1)}, bf16[192,1920]{1,0:T(8,128)(2,1...) custom-call(s32[5]{0:T(128)S(1)} %stack.23.place, ...), custom_call_target="tpu_custom_call" | custom-call | tf_op jit(solution)/shard_map/pallas_call | solution.py:320
  41.9 0.5 collective-permute-start.22
  42.4 1.7 %collective-permute-done.8.other = bf16[192,1920]{1,0:T(8,128)(2,1)S(1)} collective-permute-done((bf16[192,1920]{1,0:T(8,128)(2,1)S(1)}, bf16[192,1920]{1,0:T(8,128)(2,1)S(1)}, u32[]{:S(2)}, u32[]{:S(2)}) %collective-permute-start.8) | collective-permute-done | bytes 737312 | tf_op jit(solution)/shard_map/ppermute | solution.py:43
  44.1 3.2 %shard_map.111 = (f32[320,640]{1,0:T(8,128)S(1)}, bf16[320,640]{1,0:T(8,128)(2,1)S(1)}, bf16[320,640]{1,0:T(8,128)(2,1)S(1)}, bf16[320,640]{1,0:T(8,128)(2,1)S(1)}) custom-call(s32[5]{0:T(128)S(1)} %stack.23.place, bf16[192,1920]{1,0:T(8,128)(2,1)S(1)} %get-tuple-element.40.mine, bf16[192,1920]{1,0:T(8,128)(2,1)S(1)} %collective-permute-done.8.other, ...), custom_call_target="tpu_custom_call" | custom-call | tf_op jit(solution)/shard_map/pallas_call | solution.py:320
  47.3 1.6 %collective-permute-start.9 = (bf16[320,640]{1,0:T(8,128)(2,1)S(1)}, bf16[320,640]{1,0:T(8,128)(2,1)S(1)}, u32[]{:S(2)}, u32[]{:S(2)}) collective-permute-start(bf16[320,640]{1,0:T(8,128)(2,1)S(1)} %get-tuple-element.45), channel_id=1, source_target_pairs={{0,2},{2,4},{4,6},{6,0},{1,3},{3,5},{5,7},{7,1},{8,10},{10,12},{12... | collective-permute-start | bytes 1228808 | tf_op jit(solution)/shard_map/ppermute | solution.py:43
  48.9 2.7 %collective-permute-start.10 = (bf16[320,640]{1,0:T(8,128)(2,1)S(1)}, bf16[320,640]{1,0:T(8,128)(2,1)S(1)}, u32[]{:S(2)}, u32[]{:S(2)}) collective-permute-start(bf16[320,640]{1,0:T(8,128)(2,1)S(1)} %get-tuple-element.46), channel_id=1, source_target_pairs={{0,4},{2,6},{4,0},{6,2},{1,5},{3,7},{5,1},{7,3},{8,12},{10,14},{12... | collective-permute-start | bytes 1228808 | tf_op jit(solution)/shard_map/ppermute | solution.py:43
  51.6 1.4 %collective-permute-start.11 = (bf16[320,640]{1,0:T(8,128)(2,1)S(1)}, bf16[320,640]{1,0:T(8,128)(2,1)S(1)}, u32[]{:S(2)}, u32[]{:S(2)}) collective-permute-start(bf16[320,640]{1,0:T(8,128)(2,1)S(1)} %get-tuple-element.47), channel_id=1, source_target_pairs={{0,6},{2,0},{4,2},{6,4},{1,7},{3,1},{5,3},{7,5},{8,14},{10,8},{12,... | collective-permute-start | bytes 1228808 | tf_op jit(solution)/shard_map/ppermute | solution.py:43
  53.0 1.9 %collective-permute-start.14 = (bf16[40,640]{1,0:T(8,128)(2,1)S(1)}, bf16[40,640]{1,0:T(8,128)(2,1)S(1)}, u32[]{:S(2)}, u32[]{:S(2)}) collective-permute-start(bf16[40,640]{1,0:T(8,128)(2,1)S(1)} %get-tuple-element.50), channel_id=1, source_target_pairs={{0,32},{32,64},{64,96},{96,128},{128,160},{160,192},{192,224},{1,3... | collective-permute-start | bytes 153608 | tf_op jit(solution)/shard_map/ppermute | solution.py:338
  55.0 3.5 %collective-permute-done.14.top = bf16[40,640]{1,0:T(8,128)(2,1)S(1)} collective-permute-done((bf16[40,640]{1,0:T(8,128)(2,1)S(1)}, bf16[40,640]{1,0:T(8,128)(2,1)S(1)}, u32[]{:S(2)}, u32[]{:S(2)}) %collective-permute-start.14) | collective-permute-done | bytes 51232 | tf_op jit(solution)/shard_map/ppermute | solution.py:338
  58.5 3.8 %collective-permute-start.18 = (bf16[64,640]{1,0:T(8,128)(2,1)S(1)}, bf16[64,640]{1,0:T(8,128)(2,1)S(1)}, u32[]{:S(2)}, u32[]{:S(2)}) collective-permute-start(bf16[64,640]{1,0:T(8,128)(2,1)S(1)} %get-tuple-element.52), channel_id=1, source_target_pairs={{0,16},{8,24},{16,0},{24,8},{1,17},{9,25},{17,1},{25,9},{2,18},{10... | collective-permute-start | bytes 245768 | tf_op jit(solution)/shard_map/ppermute | solution.py:43
  62.3 1.9 %collective-permute-start.15 = (bf16[40,640]{1,0:T(8,128)(2,1)S(1)}, bf16[40,640]{1,0:T(8,128)(2,1)S(1)}, u32[]{:S(2)}, u32[]{:S(2)}) collective-permute-start(bf16[40,640]{1,0:T(8,128)(2,1)S(1)} %get-tuple-element.51), channel_id=1, source_target_pairs={{32,0},{64,32},{96,64},{128,96},{160,128},{192,160},{224,192},{33,... | collective-permute-start | bytes 153608 | tf_op jit(solution)/shard_map/ppermute | solution.py:339
  64.2 2.0 %shard_map.114 = (f32[320,640]{1,0:T(8,128)S(1)}, bf16[320,640]{1,0:T(8,128)(2,1)S(1)}, bf16[320,640]{1,0:T(8,128)(2,1)S(1)}, bf16[320,640]{1,0:T(8,128)(2,1)S(1)}) custom-call(s32[5]{0:T(128)S(1)} %stack.23.place, bf16[192,2176]{1,0:T(8,128)(2,1)S(1)} %get-tuple-element.58.mine, bf16[192,2176]{1,0:T(8,128)(2,1)S(1)} %collective-permute-done.22.other), custom_call_target="tpu_custom_call" | custom-call | tf_op jit(solution)/shard_map/pallas_call | solution.py:320
  66.2 1.4 %collective-permute-start.23 = (bf16[320,640]{1,0:T(8,128)(2,1)S(1)}, bf16[320,640]{1,0:T(8,128)(2,1)S(1)}, u32[]{:S(2)}, u32[]{:S(2)}) collective-permute-start(bf16[320,640]{1,0:T(8,128)(2,1)S(1)} %get-tuple-element.61), channel_id=1, source_target_pairs={{0,64},{64,128},{128,192},{192,0},{1,65},{65,129},{129,193},{193,1... | collective-permute-start | bytes 1228808 | tf_op jit(solution)/shard_map/ppermute | solution.py:43
  67.5 2.2 %collective-permute-start.25 = (bf16[320,640]{1,0:T(8,128)(2,1)S(1)}, bf16[320,640]{1,0:T(8,128)(2,1)S(1)}, u32[]{:S(2)}, u32[]{:S(2)}) collective-permute-start(bf16[320,640]{1,0:T(8,128)(2,1)S(1)} %get-tuple-element.63), channel_id=1, source_target_pairs={{0,192},{64,0},{128,64},{192,128},{1,193},{65,1},{129,65},{193,129... | collective-permute-start | bytes 1228808 | tf_op jit(solution)/shard_map/ppermute | solution.py:43
  69.7 0.2 collective-permute-done.10.r2
  69.9 2.7 %collective-permute-start.13 = (bf16[192,640]{1,0:T(8,128)(2,1)S(1)}, bf16[192,640]{1,0:T(8,128)(2,1)S(1)}, u32[]{:S(2)}, u32[]{:S(2)}) collective-permute-start(bf16[192,640]{1,0:T(8,128)(2,1)S(1)} %get-tuple-element.49.tile), channel_id=1, source_target_pairs={{0,24},{8,0},{16,8},{24,16},{1,25},{9,1},{17,9},{25,17},{2,26},{10... | collective-permute-start | bytes 737288 | tf_op jit(solution)/shard_map/ppermute | solution.py:43
  72.6 5.6 %collective-permute-done.23.r1 = bf16[320,640]{1,0:T(8,128)(2,1)S(1)} collective-permute-done((bf16[320,640]{1,0:T(8,128)(2,1)S(1)}, bf16[320,640]{1,0:T(8,128)(2,1)S(1)}, u32[]{:S(2)}, u32[]{:S(2)}) %collective-permute-start.23) | collective-permute-done | bytes 409632 | tf_op jit(solution)/shard_map/ppermute | solution.py:43
  78.2 0.5 collective-permute-start.17
  78.7 2.8 %collective-permute-done.24.r2 = bf16[320,640]{1,0:T(8,128)(2,1)S(1)} collective-permute-done((bf16[320,640]{1,0:T(8,128)(2,1)S(1)}, bf16[320,640]{1,0:T(8,128)(2,1)S(1)}, u32[]{:S(2)}, u32[]{:S(2)}) %collective-permute-start.24) | collective-permute-done | bytes 409632 | tf_op jit(solution)/shard_map/ppermute | solution.py:43
  81.4 0.9 shard_map.112
  82.4 5.8 %collective-permute-done.25.r3 = bf16[320,640]{1,0:T(8,128)(2,1)S(1)} collective-permute-done((bf16[320,640]{1,0:T(8,128)(2,1)S(1)}, bf16[320,640]{1,0:T(8,128)(2,1)S(1)}, u32[]{:S(2)}, u32[]{:S(2)}) %collective-permute-start.25) | collective-permute-done | bytes 409632 | tf_op jit(solution)/shard_map/ppermute | solution.py:43
  88.2 1.8 %collective-permute-start.19 = (bf16[80,640]{1,0:T(8,128)(2,1)S(1)}, bf16[80,640]{1,0:T(8,128)(2,1)S(1)}, u32[]{:S(2)}, u32[]{:S(2)}) collective-permute-start(bf16[80,640]{1,0:T(8,128)(2,1)S(1)} %get-tuple-element.55), channel_id=1, source_target_pairs={{0,64},{64,128},{128,192},{192,0},{1,65},{65,129},{129,193},{193,1... | collective-permute-start | bytes 307208 | tf_op jit(solution)/shard_map/ppermute | solution.py:43
  90.0 1.0 shard_map.115
  91.0 1.9 %collective-permute-start.20 = (bf16[80,640]{1,0:T(8,128)(2,1)S(1)}, bf16[80,640]{1,0:T(8,128)(2,1)S(1)}, u32[]{:S(2)}, u32[]{:S(2)}) collective-permute-start(bf16[80,640]{1,0:T(8,128)(2,1)S(1)} %get-tuple-element.56), channel_id=1, source_target_pairs={{0,128},{64,192},{128,0},{192,64},{1,129},{65,193},{129,1},{193,65... | collective-permute-start | bytes 307208 | tf_op jit(solution)/shard_map/ppermute | solution.py:43
  92.9 2.1 %collective-permute-start.21 = (bf16[80,640]{1,0:T(8,128)(2,1)S(1)}, bf16[80,640]{1,0:T(8,128)(2,1)S(1)}, u32[]{:S(2)}, u32[]{:S(2)}) collective-permute-start(bf16[80,640]{1,0:T(8,128)(2,1)S(1)} %get-tuple-element.57), channel_id=1, source_target_pairs={{0,192},{64,0},{128,64},{192,128},{1,193},{65,1},{129,65},{193,129... | collective-permute-start | bytes 307208 | tf_op jit(solution)/shard_map/ppermute | solution.py:43
  95.0 0.6 collective-permute-start.26
  95.6 0.9 collective-permute-start.27
  96.5 1.9 %collective-permute-start.28 = (bf16[80,640]{1,0:T(8,128)(2,1)S(1)}, bf16[80,640]{1,0:T(8,128)(2,1)S(1)}, u32[]{:S(2)}, u32[]{:S(2)}) collective-permute-start(bf16[80,640]{1,0:T(8,128)(2,1)S(1)} %get-tuple-element.67), channel_id=1, source_target_pairs={{0,6},{2,0},{4,2},{6,4},{1,7},{3,1},{5,3},{7,5},{8,14},{10,8},{12,... | collective-permute-start | bytes 307208 | tf_op jit(solution)/shard_map/ppermute | solution.py:43
  98.4 4.5 %shard_map.113 = bf16[192,640]{1,0:T(8,128)(2,1)} custom-call(s32[5]{0:T(128)S(1)} %stack.23.place, bf16[192,640]{1,0:T(8,128)(2,1)S(1)} %get-tuple-element.49.tile, bf16[192,640]{1,0:T(8,128)(2,1)S(1)} %collective-permute-done.12.left, bf16[192,640]{1,0:T(8,128)(2,1)S(1)} %collective-permute-done.13.right, bf16[40,640]{1,0:T(8,128)(2,1)S(1)} %collective-permute-done.14.top, ...), custom_call_target="tpu_custom_call" | custom-call | tf_op jit(solution)/shard_map/pallas_call | solution.py:320
  102.9 0.2 shard_map.116
  103.1 14.4 %all_to_all.5.parts = bf16[8,20,640]{2,1,0:T(8,128)(2,1)S(1)} all-to-all(bf16[8,20,640]{2,1,0:T(8,128)(2,1)S(1)} %shard_map.116), channel_id=1, replica_groups=mesh['y'=4,'core'=2,'zlo'=4,'x'=4,'zhi'=2] {'zlo','zhi'}, dimensions={0} | all-to-all | bytes 409600 | tf_op jit(solution)/shard_map/all_to_all | solution.py:452
  117.5 0.6 shard_map.117
  (46 shorter events, 0.5 us)
Async XLA Ops:
  0.6 12.9 %copy-start = (bf16[1,12,16,640]{3,2,1,0:T(8,128)(2,1)S(1)}, bf16[1,12,16,640]{3,2,1,0:T(8,128)(2,1)}, u32[]{:S(2)}) copy-start(bf16[1,12,16,640]{3,2,1,0:T(8,128)(2,1)} %param.7) | copy-start | bytes 737284
  0.6 14.9 %copy-start.1 = (bf16[1,12,16,640]{3,2,1,0:T(8,128)(2,1)S(1)}, bf16[1,12,16,640]{3,2,1,0:T(8,128)(2,1)}, u32[]{:S(2)}) copy-start(bf16[1,12,16,640]{3,2,1,0:T(8,128)(2,1)} %param.13) | copy-start | bytes 737284
  1.5 8.6 %collective-permute-start.2 = (bf16[32,640]{1,0:T(8,128)(2,1)S(1)}, bf16[32,640]{1,0:T(8,128)(2,1)S(1)}, u32[]{:S(2)}, u32[]{:S(2)}) collective-permute-start(bf16[32,640]{1,0:T(8,128)(2,1)S(1)} %bitcast.38), channel_id=1, source_target_pairs={{0,32},{32,64},{64,96},{96,128},{128,160},{160,192},{192,224},{1,3... | collective-permute-start | bytes 122888 | tf_op jit(solution)/shard_map/ppermute | solution.py:338
  3.4 6.7 %collective-permute-start.3 = (bf16[32,640]{1,0:T(8,128)(2,1)S(1)}, bf16[32,640]{1,0:T(8,128)(2,1)S(1)}, u32[]{:S(2)}, u32[]{:S(2)}) collective-permute-start(bf16[32,640]{1,0:T(8,128)(2,1)S(1)} %bitcast.37), channel_id=1, source_target_pairs={{32,0},{64,32},{96,64},{128,96},{160,128},{192,160},{224,192},{33,... | collective-permute-start | bytes 122888 | tf_op jit(solution)/shard_map/ppermute | solution.py:339
  10.1 10.2 %collective-permute-start.6 = (bf16[96,640]{1,0:T(8,128)(2,1)S(1)}, bf16[96,640]{1,0:T(8,128)(2,1)S(1)}, u32[]{:S(2)}, u32[]{:S(2)}) collective-permute-start(bf16[96,640]{1,0:T(8,128)(2,1)S(1)} %get-tuple-element.75), channel_id=1, source_target_pairs={{0,16},{8,24},{16,0},{24,8},{1,17},{9,25},{17,1},{25,9},{2,18},{10... | collective-permute-start | bytes 368648 | tf_op jit(solution)/shard_map/ppermute | solution.py:43
  13.5 21.1 %collective-permute-start.1 = (bf16[192,640]{1,0:T(8,128)(2,1)S(1)}, bf16[192,640]{1,0:T(8,128)(2,1)S(1)}, u32[]{:S(2)}, u32[]{:S(2)}) collective-permute-start(bf16[192,640]{1,0:T(8,128)(2,1)S(1)} %bitcast.23), channel_id=1, source_target_pairs={{0,24},{8,0},{16,8},{24,16},{1,25},{9,1},{17,9},{25,17},{2,26},{10... | collective-permute-start | bytes 737288 | tf_op jit(solution)/shard_map/ppermute | solution.py:43
  15.0 19.7 %collective-permute-start = (bf16[192,640]{1,0:T(8,128)(2,1)S(1)}, bf16[192,640]{1,0:T(8,128)(2,1)S(1)}, u32[]{:S(2)}, u32[]{:S(2)}) collective-permute-start(bf16[192,640]{1,0:T(8,128)(2,1)S(1)} %bitcast.24), channel_id=1, source_target_pairs={{0,8},{8,16},{16,24},{24,0},{1,9},{9,17},{17,25},{25,1},{2,10},{10... | collective-permute-start | bytes 737288 | tf_op jit(solution)/shard_map/ppermute | solution.py:43
  15.5 10.8 %collective-permute-start.7 = (bf16[192,640]{1,0:T(8,128)(2,1)S(1)}, bf16[192,640]{1,0:T(8,128)(2,1)S(1)}, u32[]{:S(2)}, u32[]{:S(2)}) collective-permute-start(bf16[192,640]{1,0:T(8,128)(2,1)S(1)} %bitcast.26), channel_id=1, source_target_pairs={{0,32},{32,0},{1,33},{33,1},{2,34},{34,2},{3,35},{35,3},{4,36},{36... | collective-permute-start | bytes 737288 | tf_op jit(solution)/shard_map/ppermute | solution.py:43
  15.6 15.1 %collective-permute-start.5 = (bf16[96,640]{1,0:T(8,128)(2,1)S(1)}, bf16[96,640]{1,0:T(8,128)(2,1)S(1)}, u32[]{:S(2)}, u32[]{:S(2)}) collective-permute-start(bf16[96,640]{1,0:T(8,128)(2,1)S(1)} %get-tuple-element.76), channel_id=1, source_target_pairs={{0,24},{8,0},{16,8},{24,16},{1,25},{9,1},{17,9},{25,17},{2,26},{10... | collective-permute-start | bytes 368648 | tf_op jit(solution)/shard_map/ppermute | solution.py:43
  20.3 14.3 %collective-permute-start.4 = (bf16[96,640]{1,0:T(8,128)(2,1)S(1)}, bf16[96,640]{1,0:T(8,128)(2,1)S(1)}, u32[]{:S(2)}, u32[]{:S(2)}) collective-permute-start(bf16[96,640]{1,0:T(8,128)(2,1)S(1)} %get-tuple-element.76), channel_id=1, source_target_pairs={{0,8},{8,16},{16,24},{24,0},{1,9},{9,17},{17,25},{25,1},{2,10},{10... | collective-permute-start | bytes 368648 | tf_op jit(solution)/shard_map/ppermute | solution.py:43
  41.8 2.3 %collective-permute-start.8 = (bf16[192,1920]{1,0:T(8,128)(2,1)S(1)}, bf16[192,1920]{1,0:T(8,128)(2,1)S(1)}, u32[]{:S(2)}, u32[]{:S(2)}) collective-permute-start(bf16[192,1920]{1,0:T(8,128)(2,1)S(1)} %get-tuple-element.41), channel_id=1, source_target_pairs={{0,32},{32,0},{1,33},{33,1},{2,34},{34,2},{3,35},{35,3},{4,36},{36... | collective-permute-start | bytes 2211848 | tf_op jit(solution)/shard_map/ppermute | solution.py:43
  41.9 20.3 %collective-permute-start.22 = (bf16[192,2176]{1,0:T(8,128)(2,1)S(1)}, bf16[192,2176]{1,0:T(8,128)(2,1)S(1)}, u32[]{:S(2)}, u32[]{:S(2)}) collective-permute-start(bf16[192,2176]{1,0:T(8,128)(2,1)S(1)} %get-tuple-element.59), channel_id=1, source_target_pairs={{0,32},{32,0},{1,33},{33,1},{2,34},{34,2},{3,35},{35,3},{4,36},{36... | collective-permute-start | bytes 2506760 | tf_op jit(solution)/shard_map/ppermute | solution.py:43
  47.3 20.2 %collective-permute-start.9 = (bf16[320,640]{1,0:T(8,128)(2,1)S(1)}, bf16[320,640]{1,0:T(8,128)(2,1)S(1)}, u32[]{:S(2)}, u32[]{:S(2)}) collective-permute-start(bf16[320,640]{1,0:T(8,128)(2,1)S(1)} %get-tuple-element.45), channel_id=1, source_target_pairs={{0,2},{2,4},{4,6},{6,0},{1,3},{3,5},{5,7},{7,1},{8,10},{10,12},{12... | collective-permute-start | bytes 1228808 | tf_op jit(solution)/shard_map/ppermute | solution.py:43
  48.9 21.0 %collective-permute-start.10 = (bf16[320,640]{1,0:T(8,128)(2,1)S(1)}, bf16[320,640]{1,0:T(8,128)(2,1)S(1)}, u32[]{:S(2)}, u32[]{:S(2)}) collective-permute-start(bf16[320,640]{1,0:T(8,128)(2,1)S(1)} %get-tuple-element.46), channel_id=1, source_target_pairs={{0,4},{2,6},{4,0},{6,2},{1,5},{3,7},{5,1},{7,3},{8,12},{10,14},{12... | collective-permute-start | bytes 1228808 | tf_op jit(solution)/shard_map/ppermute | solution.py:43
  51.6 21.0 %collective-permute-start.11 = (bf16[320,640]{1,0:T(8,128)(2,1)S(1)}, bf16[320,640]{1,0:T(8,128)(2,1)S(1)}, u32[]{:S(2)}, u32[]{:S(2)}) collective-permute-start(bf16[320,640]{1,0:T(8,128)(2,1)S(1)} %get-tuple-element.47), channel_id=1, source_target_pairs={{0,6},{2,0},{4,2},{6,4},{1,7},{3,1},{5,3},{7,5},{8,14},{10,8},{12,... | collective-permute-start | bytes 1228808 | tf_op jit(solution)/shard_map/ppermute | solution.py:43
  53.0 5.4 %collective-permute-start.14 = (bf16[40,640]{1,0:T(8,128)(2,1)S(1)}, bf16[40,640]{1,0:T(8,128)(2,1)S(1)}, u32[]{:S(2)}, u32[]{:S(2)}) collective-permute-start(bf16[40,640]{1,0:T(8,128)(2,1)S(1)} %get-tuple-element.50), channel_id=1, source_target_pairs={{0,32},{32,64},{64,96},{96,128},{128,160},{160,192},{192,224},{1,3... | collective-permute-start | bytes 153608 | tf_op jit(solution)/shard_map/ppermute | solution.py:338
  58.5 9.1 %collective-permute-start.18 = (bf16[64,640]{1,0:T(8,128)(2,1)S(1)}, bf16[64,640]{1,0:T(8,128)(2,1)S(1)}, u32[]{:S(2)}, u32[]{:S(2)}) collective-permute-start(bf16[64,640]{1,0:T(8,128)(2,1)S(1)} %get-tuple-element.52), channel_id=1, source_target_pairs={{0,16},{8,24},{16,0},{24,8},{1,17},{9,25},{17,1},{25,9},{2,18},{10... | collective-permute-start | bytes 245768 | tf_op jit(solution)/shard_map/ppermute | solution.py:43
  62.3 3.9 %collective-permute-start.15 = (bf16[40,640]{1,0:T(8,128)(2,1)S(1)}, bf16[40,640]{1,0:T(8,128)(2,1)S(1)}, u32[]{:S(2)}, u32[]{:S(2)}) collective-permute-start(bf16[40,640]{1,0:T(8,128)(2,1)S(1)} %get-tuple-element.51), channel_id=1, source_target_pairs={{32,0},{64,32},{96,64},{128,96},{160,128},{192,160},{224,192},{33,... | collective-permute-start | bytes 153608 | tf_op jit(solution)/shard_map/ppermute | solution.py:339
  66.2 12.0 %collective-permute-start.23 = (bf16[320,640]{1,0:T(8,128)(2,1)S(1)}, bf16[320,640]{1,0:T(8,128)(2,1)S(1)}, u32[]{:S(2)}, u32[]{:S(2)}) collective-permute-start(bf16[320,640]{1,0:T(8,128)(2,1)S(1)} %get-tuple-element.61), channel_id=1, source_target_pairs={{0,64},{64,128},{128,192},{192,0},{1,65},{65,129},{129,193},{193,1... | collective-permute-start | bytes 1228808 | tf_op jit(solution)/shard_map/ppermute | solution.py:43
  67.5 13.9 %collective-permute-start.24 = (bf16[320,640]{1,0:T(8,128)(2,1)S(1)}, bf16[320,640]{1,0:T(8,128)(2,1)S(1)}, u32[]{:S(2)}, u32[]{:S(2)}) collective-permute-start(bf16[320,640]{1,0:T(8,128)(2,1)S(1)} %get-tuple-element.62), channel_id=1, source_target_pairs={{0,128},{64,192},{128,0},{192,64},{1,129},{65,193},{129,1},{193,65... | collective-permute-start | bytes 1228808 | tf_op jit(solution)/shard_map/ppermute | solution.py:43
  67.5 20.6 %collective-permute-start.25 = (bf16[320,640]{1,0:T(8,128)(2,1)S(1)}, bf16[320,640]{1,0:T(8,128)(2,1)S(1)}, u32[]{:S(2)}, u32[]{:S(2)}) collective-permute-start(bf16[320,640]{1,0:T(8,128)(2,1)S(1)} %get-tuple-element.63), channel_id=1, source_target_pairs={{0,192},{64,0},{128,64},{192,128},{1,193},{65,1},{129,65},{193,129... | collective-permute-start | bytes 1228808 | tf_op jit(solution)/shard_map/ppermute | solution.py:43
  69.9 25.1 %collective-permute-start.13 = (bf16[192,640]{1,0:T(8,128)(2,1)S(1)}, bf16[192,640]{1,0:T(8,128)(2,1)S(1)}, u32[]{:S(2)}, u32[]{:S(2)}) collective-permute-start(bf16[192,640]{1,0:T(8,128)(2,1)S(1)} %get-tuple-element.49.tile), channel_id=1, source_target_pairs={{0,24},{8,0},{16,8},{24,16},{1,25},{9,1},{17,9},{25,17},{2,26},{10... | collective-permute-start | bytes 737288 | tf_op jit(solution)/shard_map/ppermute | solution.py:43
  72.6 23.0 %collective-permute-start.12 = (bf16[192,640]{1,0:T(8,128)(2,1)S(1)}, bf16[192,640]{1,0:T(8,128)(2,1)S(1)}, u32[]{:S(2)}, u32[]{:S(2)}) collective-permute-start(bf16[192,640]{1,0:T(8,128)(2,1)S(1)} %get-tuple-element.49.tile), channel_id=1, source_target_pairs={{0,8},{8,16},{16,24},{24,0},{1,9},{9,17},{17,25},{25,1},{2,10},{10... | collective-permute-start | bytes 737288 | tf_op jit(solution)/shard_map/ppermute | solution.py:43
  78.2 12.8 %collective-permute-start.17 = (bf16[80,640]{1,0:T(8,128)(2,1)S(1)}, bf16[80,640]{1,0:T(8,128)(2,1)S(1)}, u32[]{:S(2)}, u32[]{:S(2)}) collective-permute-start(bf16[80,640]{1,0:T(8,128)(2,1)S(1)} %constant_dynamic-update-slice_fusion), channel_id=1, source_target_pairs={{0,24},{8,0},{16,8},{24,16},{1,25},{9,1},{17,9},{25,17},{2,26},{10... | collective-permute-start | bytes 307208 | tf_op jit(solution)/shard_map/ppermute | solution.py:43
  81.4 11.4 %collective-permute-start.16 = (bf16[80,640]{1,0:T(8,128)(2,1)S(1)}, bf16[80,640]{1,0:T(8,128)(2,1)S(1)}, u32[]{:S(2)}, u32[]{:S(2)}) collective-permute-start(bf16[80,640]{1,0:T(8,128)(2,1)S(1)} %constant_dynamic-update-slice_fusion), channel_id=1, source_target_pairs={{0,8},{8,16},{16,24},{24,0},{1,9},{9,17},{17,25},{25,1},{2,10},{10... | collective-permute-start | bytes 307208 | tf_op jit(solution)/shard_map/ppermute | solution.py:43
  88.2 8.3 %collective-permute-start.19 = (bf16[80,640]{1,0:T(8,128)(2,1)S(1)}, bf16[80,640]{1,0:T(8,128)(2,1)S(1)}, u32[]{:S(2)}, u32[]{:S(2)}) collective-permute-start(bf16[80,640]{1,0:T(8,128)(2,1)S(1)} %get-tuple-element.55), channel_id=1, source_target_pairs={{0,64},{64,128},{128,192},{192,0},{1,65},{65,129},{129,193},{193,1... | collective-permute-start | bytes 307208 | tf_op jit(solution)/shard_map/ppermute | solution.py:43
  91.0 11.9 %collective-permute-start.20 = (bf16[80,640]{1,0:T(8,128)(2,1)S(1)}, bf16[80,640]{1,0:T(8,128)(2,1)S(1)}, u32[]{:S(2)}, u32[]{:S(2)}) collective-permute-start(bf16[80,640]{1,0:T(8,128)(2,1)S(1)} %get-tuple-element.56), channel_id=1, source_target_pairs={{0,128},{64,192},{128,0},{192,64},{1,129},{65,193},{129,1},{193,65... | collective-permute-start | bytes 307208 | tf_op jit(solution)/shard_map/ppermute | solution.py:43
  92.9 10.0 %collective-permute-start.21 = (bf16[80,640]{1,0:T(8,128)(2,1)S(1)}, bf16[80,640]{1,0:T(8,128)(2,1)S(1)}, u32[]{:S(2)}, u32[]{:S(2)}) collective-permute-start(bf16[80,640]{1,0:T(8,128)(2,1)S(1)} %get-tuple-element.57), channel_id=1, source_target_pairs={{0,192},{64,0},{128,64},{192,128},{1,193},{65,1},{129,65},{193,129... | collective-permute-start | bytes 307208 | tf_op jit(solution)/shard_map/ppermute | solution.py:43
  95.0 7.9 %collective-permute-start.26 = (bf16[80,640]{1,0:T(8,128)(2,1)S(1)}, bf16[80,640]{1,0:T(8,128)(2,1)S(1)}, u32[]{:S(2)}, u32[]{:S(2)}) collective-permute-start(bf16[80,640]{1,0:T(8,128)(2,1)S(1)} %get-tuple-element.65), channel_id=1, source_target_pairs={{0,2},{2,4},{4,6},{6,0},{1,3},{3,5},{5,7},{7,1},{8,10},{10,12},{12... | collective-permute-start | bytes 307208 | tf_op jit(solution)/shard_map/ppermute | solution.py:43
  95.6 7.3 %collective-permute-start.27 = (bf16[80,640]{1,0:T(8,128)(2,1)S(1)}, bf16[80,640]{1,0:T(8,128)(2,1)S(1)}, u32[]{:S(2)}, u32[]{:S(2)}) collective-permute-start(bf16[80,640]{1,0:T(8,128)(2,1)S(1)} %get-tuple-element.66), channel_id=1, source_target_pairs={{0,4},{2,6},{4,0},{6,2},{1,5},{3,7},{5,1},{7,3},{8,12},{10,14},{12... | collective-permute-start | bytes 307208 | tf_op jit(solution)/shard_map/ppermute | solution.py:43
  96.5 6.4 %collective-permute-start.28 = (bf16[80,640]{1,0:T(8,128)(2,1)S(1)}, bf16[80,640]{1,0:T(8,128)(2,1)S(1)}, u32[]{:S(2)}, u32[]{:S(2)}) collective-permute-start(bf16[80,640]{1,0:T(8,128)(2,1)S(1)} %get-tuple-element.67), channel_id=1, source_target_pairs={{0,6},{2,0},{4,2},{6,4},{1,7},{3,1},{5,3},{7,5},{8,14},{10,8},{12,... | collective-permute-start | bytes 307208 | tf_op jit(solution)/shard_map/ppermute | solution.py:43
where the time goes:
time: 120 us; the launch traced here: 118 us
  starting transfers between devices  49.8 us (42%)
  waiting for transfers between devices  29.3 us (24%)
  Pallas kernels  19.5 us (16%)
  blocking collectives  14.4 us (12%)
  other arithmetic  3.14 us (3%)
    ppermute x25, starting transfers between devices, shift(): lax.ppermute(block, axis, [(i, (i + step) % count) for i in range(count)])  40.4 us
    ppermute x25, waiting for transfers between devices, shift(): lax.ppermute(block, axis, [(i, (i + step) % count) for i in range(count)])  25.8 us
    pallas_call x8, Pallas kernels, call(): pl.pallas_call(kernel, out_shape=outs, in_specs=in_specs, scratch_shapes=...  19.5 us
    all_to_all x1, blocking collectives, block(): lax.all_to_all(packed, ('zlo', 'zhi'), split_axis=0, concat_axis=0, tiled...  14.4 us
    ppermute x2, starting transfers between devices, neighbours(): bottom = lax.ppermute(to_down, LAT, backward)  5.55 us
    ppermute x2, starting transfers between devices, neighbours(): top = lax.ppermute(to_up, LAT, forward)  3.82 us
    ppermute x2, waiting for transfers between devices, neighbours(): top = lax.ppermute(to_up, LAT, forward)  3.51 us
  transfers between devices with their start and end apart: 29, of which 9 were waited for; matrix products, arithmetic and copies ran while one was open for 3% of the time, Pallas kernels for 10%

commit v1 on v0

--- a/solution.py
+++ b/solution.py
@@ -47,39 +47,61 @@
     return jax.ShapeDtypeStruct(shape, dtype)
 
 
-def fill_window(win, tile, left, right, top, bottom, left_halo, right_halo, far, lat):
-    far_zero = jnp.zeros((LON, EMBED), bf16)
-    for group, (inner, halo) in enumerate(
-        ((left, left_halo), (tile, None), (right, right_halo))
+def fill_window(win, tile, left, right, top, bottom, left_side, right_side, lat):
+    zero = jnp.zeros((LON, EMBED), bf16)
+
+    def put(cycle, group, rows):
+        at = (cycle + HALO) * NLON + group * LON
+        win[at : at + LON, :] = rows
+
+    for group, (inner, side) in enumerate(
+        ((left, left_side), (tile, None), (right, right_side))
     ):
         for row in range(CYCLES):
-            at = (row + HALO) * NLON + group * LON
-            win[at : at + LON, :] = inner[row * LON : (row + 1) * LON, :]
+            put(row, group, inner[row * LON : (row + 1) * LON, :])
         for row in range(HALO):
-            upper = top if halo is None else halo
-            lower = bottom if halo is None else halo
-            shift_rows = 0 if halo is None else bottom.shape[0]
-            at = row * NLON + group * LON
-            win[at : at + LON, :] = upper[row * LON : (row + 1) * LON, :]
-            at = (row + HALO + CYCLES) * NLON + group * LON
-            win[at : at + LON, :] = lower[
-                shift_rows + row * LON : shift_rows + (row + 1) * LON, :
-            ]
-    for row in range(CYCLES + 2 * HALO):
-        at = row * NLON + 3 * LON
-        win[at : at + LON, :] = far_zero
+            upper, lower = (top, bottom) if side is None else (side, side)
+            skip = 0 if side is None else RIM
+            put(row - HALO, group, upper[row * LON : (row + 1) * LON, :])
+            put(row + CYCLES, group, lower[skip + row * LON : skip + (row + 1) * LON, :])
+    for row in range(-HALO, CYCLES + HALO):
+        put(row, 3, zero)
+
+    def polar(first, skip, missing):
+        for row in range(HALO):
+            rows = slice(skip + row * LON, skip + (row + 1) * LON)
+            put(first + row, 3, left_side[rows, :])
+            put(first + HALO + row, 3, right_side[rows, :])
+            put(missing + row, 0, zero)
+            put(missing + row, 2, zero)
 
     @pl.when(lat == 0)
     def _():
-        for row in range(4):
-            at = (row + HALO) * NLON + 3 * LON
-            win[at : at + LON, :] = far[row * LON : (row + 1) * LON, :]
+        polar(0, 0, -HALO)
 
     @pl.when(lat == 7)
     def _():
-        for row in range(4):
-            at = (row + HALO + CYCLES - 4) * NLON + 3 * LON
-            win[at : at + LON, :] = far[row * LON : (row + 1) * LON, :]
+        polar(CYCLES - 4, RIM, CYCLES)
+
+
+def side_kernel(place, left, right, top, bottom, *rest):
+    *extra, to_right, to_left = rest
+    lat = place[0]
+    for to in (to_right, to_left):
+        to[0:RIM, :] = top[0:RIM, :]
+        to[RIM : 2 * RIM, :] = bottom[0:RIM, :]
+        if extra:
+            to[2 * RIM :, :] = extra[0][...]
+
+    @pl.when(lat == 0)
+    def _():
+        to_right[0:RIM, :] = left[0:RIM, :]
+        to_left[0:RIM, :] = right[RIM : 2 * RIM, :]
+
+    @pl.when(lat == 7)
+    def _():
+        to_right[RIM : 2 * RIM, :] = left[CELLS - 2 * RIM : CELLS - RIM, :]
+        to_left[RIM : 2 * RIM, :] = right[CELLS - RIM :, :]
 
 
 def set_rows(coef, at, rows):
@@ -105,9 +127,9 @@
 
 
 def forward_kernel(
-    place, tile, left, right, top, bottom, left_side, right_side, far, own_e,
+    place, tile, left, right, top, bottom, left_side, right_side, far_e, own_e,
     tangent, conv_hbm, in_hbm, out_hbm,
-    out, blend_grad, mine, mine_mlp, theirs, theirs_mlp, to_up, to_down, to_far,
+    out, blend_grad, mine, mine_mlp, theirs, theirs_mlp, to_up, to_down,
     win, band, coef, spread, conv_weight, weight_in, weight_out, sems
 ):
     lat = place[0]
@@ -121,14 +143,14 @@
     ]
     for load in loads:
         load.start()
-    fill_window(win, tile, left, right, top, bottom, left_side, right_side, far, lat)
-    set_rows(coef, 0, left_side[2 * RIM : 2 * RIM + 32, :].astype(f32))
-    set_rows(coef, 32, own_e[...].astype(f32))
-    set_rows(coef, 64, right_side[2 * RIM : 2 * RIM + 32, :].astype(f32))
-    set_rows(coef, 96, far[4 * LON : 4 * LON + 32, :].astype(f32))
+    fill_window(win, tile, left, right, top, bottom, left_side, right_side, lat)
+    set_rows(coef, 0, left_side[2 * RIM :, :].astype(f32))
+    set_rows(coef, 16, own_e[...].astype(f32))
+    set_rows(coef, 32, right_side[2 * RIM :, :].astype(f32))
+    set_rows(coef, 48, far_e[...].astype(f32))
 
     def base(cycle):
-        return lax.rem(cycle // OWNED - lon + 1 + 4, 4) * 32 + (cycle % OWNED) * BASIS
+        return lax.rem(cycle // OWNED - lon + 1 + 4, 4) * 16 + (cycle % OWNED) * BASIS
 
     for i in range(CYCLES):
         start = base(i)
@@ -183,7 +205,7 @@
 
     edges = []
     for cycle in (0, 1, CYCLES - 2, CYCLES - 1):
-        start = base(cycle) + 16
+        start = base(cycle)
         for k in range(BASIS):
             edges.append(
                 jnp.concatenate([coef[d, pl.ds(start + k, 1), :] for d in range(SPAN)], axis=1)
@@ -192,7 +214,6 @@
     to_up[RIM : RIM + 8, :] = jnp.concatenate(edges[8:], axis=0).astype(bf16)
     to_down[0:RIM, :] = grad[:RIM, :]
     to_down[RIM : RIM + 8, :] = jnp.concatenate(edges[:8], axis=0).astype(bf16)
-    to_far[...] = jnp.where(lat == 0, grad[: 4 * LON, :], grad[CELLS - 4 * LON :, :])
 
 
 def mlp_grad_kernel(place, mine, other, tangent, other_tangent, order, o0, o1, o2, o3, acc):
@@ -265,7 +286,7 @@
 
 
 def field_grad_kernel(
-    place, tile, left, right, top, bottom, left_halo, right_halo, far,
+    place, tile, left, right, top, bottom, left_side, right_side,
     own_e, left_e, right_e, far_e, conv_hbm, field_grad, win, band, coef, mixed,
     conv_weight, sem
 ):
@@ -273,22 +294,26 @@
     lon = place[1]
     load = pltpu.make_async_copy(conv_hbm, conv_weight, sem)
     load.start()
-    fill_window(win, tile, left, right, top, bottom, left_halo, right_halo, far, lat)
-    set_rows(coef, 0, left_e[2 * RIM : 2 * RIM + 32, :].astype(f32))
-    set_rows(coef, 32, own_e[...].astype(f32))
-    set_rows(coef, 64, right_e[2 * RIM : 2 * RIM + 32, :].astype(f32))
-    set_rows(coef, 96, far_e[4 * LON : 4 * LON + 32, :].astype(f32))
-    set_rows(coef, 128, top[HALO * LON : HALO * LON + 8, :].astype(f32))
-    set_rows(coef, 136, bottom[HALO * LON : HALO * LON + 8, :].astype(f32))
+    fill_window(win, tile, left, right, top, bottom, left_side, right_side, lat)
+    rows = jnp.concatenate(
+        [
+            left_e[2 * RIM :, :], own_e[...], right_e[2 * RIM :, :], far_e[...],
+            top[RIM:, :], bottom[RIM:, :],
+        ],
+        axis=0,
+    )
+    lane = lax.broadcasted_iota(jnp.int32, (2 * NLON, 2 * NLON), 0)
+    to = lax.broadcasted_iota(jnp.int32, (2 * NLON, 2 * NLON), 1)
+    flip = (lax.rem(lane + to, 2 * NLON) == 0).astype(f32).astype(bf16)
+    for d in range(SPAN):
+        coef[d, :, :] = dot(rows[:, d * 128 : (d + 1) * 128], flip, ((1,), (0,)))
 
     def base(cycle):
         if cycle < 0:
-            return 128 + (cycle + HALO) * BASIS
+            return 64 + (cycle + HALO) * BASIS
         if cycle >= CYCLES:
-            return 136 + (cycle - CYCLES) * BASIS
-        return (
-            lax.rem(cycle // OWNED - lon + 1 + 4, 4) * 32 + 16 + (cycle % OWNED) * BASIS
-        )
+            return 72 + (cycle - CYCLES) * BASIS
+        return lax.rem(cycle // OWNED - lon + 1 + 4, 4) * 16 + (cycle % OWNED) * BASIS
 
     for j in range(CYCLES):
         starts = [base(j + e - HALO) for e in range(SPAN)]
@@ -326,10 +351,6 @@
     )(*args)
 
 
-def polar_rows(tile, lat):
-    return jnp.where(lat == 0, tile[: 4 * LON], tile[CELLS - 4 * LON :])
-
-
 def neighbours(tile, to_up, to_down):
     forward = [(i, i + 1) for i in range(7)]
     backward = [(i + 1, i) for i in range(7)]
@@ -340,9 +361,14 @@
     return left, right, top, bottom
 
 
-def relay(side):
-    left_side = shift(side, "zlo", 4, 1)
-    right_side = shift(side, "zlo", 4, 3)
+def relay(place, left, right, top, bottom, *extra):
+    rows = 2 * RIM + sum(e.shape[0] for e in extra)
+    to_right, to_left = call(
+        side_kernel, (struct((rows, EMBED), bf16),) * 2, [], 4, place,
+        left, right, top, bottom, *extra,
+    )
+    left_side = shift(to_right, "zlo", 4, 1)
+    right_side = shift(to_left, "zlo", 4, 3)
     return left_side, right_side
 
 
@@ -355,15 +381,11 @@
 
 def coefficients(filter_basis, lon_offsets):
     lanes = jnp.arange(2 * NLON, dtype=jnp.int32) % NLON
-    values = filter_basis.astype(f32)
-    sides = []
-    for sign in (1, -1):
-        where_to = (sign * lon_offsets) % NLON
-        hit = lanes[None, None, None, :] == where_to[:, :, :, None]
-        kept = jnp.where(hit[:, None], values.transpose(0, 2, 1, 3)[..., None], 0.0)
-        rows = kept.sum(axis=3).astype(bf16).reshape(OWNED * BASIS, SPAN * 2 * NLON)
-        sides.append(jnp.pad(rows, ((0, 16 - OWNED * BASIS), (0, 0))))
-    return jnp.concatenate(sides, axis=0)
+    values = filter_basis.astype(f32).transpose(0, 2, 1, 3)
+    hit = lanes[None, None, None, :] == (lon_offsets % NLON)[:, :, :, None]
+    kept = jnp.where(hit[:, None], values[..., None], 0.0)
+    rows = kept.sum(axis=3).astype(bf16).reshape(OWNED * BASIS, SPAN * 2 * NLON)
+    return jnp.pad(rows, ((0, 16 - OWNED * BASIS), (0, 0)))
 
 
 def block(fields, filter_basis, lon_offsets, conv_weight, weight_in, weight_out, cotangent):
@@ -378,9 +400,8 @@
 
     left, right, top, bottom = neighbours(tile, tile[CELLS - RIM :], tile[:RIM])
     own_e = coefficients(filter_basis, lon_offsets)
-    to_far = jnp.concatenate([polar_rows(tile, lat), own_e], axis=0)
-    far = shift(to_far, "zlo", 4, 2)
-    left_side, right_side = relay(jnp.concatenate([top, bottom, own_e], axis=0))
+    far_e = shift(own_e, "zlo", 4, 2)
+    left_side, right_side = relay(place, left, right, top, bottom, own_e)
     other_tangent = shift(tangent, "core", 2, 1)
 
     unit = jnp.arange(EMBED, dtype=jnp.int32)
@@ -388,34 +409,33 @@
     source = uy * 160 + ul * 40 + ux * 10 + ur
     order = (unit[:, None] == source[None, :]).astype(bf16)
 
-    far, other_tangent, order = lax.optimization_barrier((far, other_tangent, order))
+    far_e, other_tangent, order = lax.optimization_barrier((far_e, other_tangent, order))
     window = pltpu.VMEM(((CYCLES + 2 * HALO) * NLON, EMBED), bf16)
     band = pltpu.VMEM((2, BASIS * LON, 384), bf16)
     edge = struct((RIM + 8, EMBED), bf16)
     parts = (struct((CELLS, CONV_PART), bf16), struct((CELLS, MLP_PART), bf16))
-    block_out, blend_grad, mine, mine_mlp, theirs, theirs_mlp, to_up, to_down, to_far = call(
+    block_out, blend_grad, mine, mine_mlp, theirs, theirs_mlp, to_up, to_down = call(
         forward_kernel,
         (struct((CELLS, EMBED), bf16), struct((CELLS, EMBED), bf16))
         + parts
         + parts
-        + (edge, edge, struct((4 * LON, EMBED), bf16)),
+        + (edge, edge),
         [
             window,
             band,
-            pltpu.VMEM((SPAN, 128, 2 * NLON), f32),
+            pltpu.VMEM((SPAN, 64, 2 * NLON), f32),
             pltpu.VMEM((CELLS, WIDE), bf16),
             pltpu.VMEM((WIDE, EMBED), bf16),
             pltpu.VMEM((EMBED, HIDDEN), bf16),
             pltpu.VMEM((HIDDEN, EMBED), bf16),
             pltpu.SemaphoreType.DMA((3,)),
         ],
-        24, place, tile, left, right, top, bottom, left_side, right_side, far, own_e,
+        24, place, tile, left, right, top, bottom, left_side, right_side, far_e, own_e,
         tangent, in_hbm=(conv_weight, weight_in, weight_out),
     )
     other = shift(theirs, "core", 2, 1)
     other_mlp = shift(theirs_mlp, "core", 2, 1)
     g_left, g_right, g_top, g_bottom = neighbours(blend_grad, to_up, to_down)
-    g_far = shift(to_far, "zlo", 4, 2)
 
     chunk = (struct((320, EMBED), f32),) + (struct((320, EMBED), bf16),) * 3
     c = call(conv_grad_kernel, chunk, [], 16, place, mine, other)
@@ -426,7 +446,7 @@
     )
     m = spread_out(m, "x")
 
-    g_left_side, g_right_side = relay(jnp.concatenate([g_top, g_bottom], axis=0))
+    g_left_side, g_right_side = relay(place, g_left, g_right, g_top, g_bottom)
     piece = (struct((80, EMBED), f32),) + (struct((80, EMBED), bf16),) * 3
     total = pltpu.VMEM((320, EMBED), f32)
     c = call(conv_sum_kernel, piece, [total], 8, place, *c)
@@ -439,13 +459,13 @@
         [
             window,
             band,
-            pltpu.VMEM((SPAN, 144, 2 * NLON), f32),
+            pltpu.VMEM((SPAN, 80, 2 * NLON), f32),
             pltpu.VMEM((CELLS, WIDE), bf16),
             pltpu.VMEM((WIDE, EMBED), bf16),
             pltpu.SemaphoreType.DMA,
         ],
         16, place, blend_grad, g_left, g_right, g_top, g_bottom, g_left_side, g_right_side,
-        g_far, own_e, left_side, right_side, far, in_hbm=(conv_weight,),
+        own_e, left_side, right_side, far_e, in_hbm=(conv_weight,),
     )
     m0, field_grad = lax.optimization_barrier((m[0], field_grad))
     packed = call(pack_kernel, struct((8, 20, EMBED), bf16), [], 4, None, m0, *m[1:], *c)

time: 120 us -> 108 us (0.900)
  waiting for transfers between devices: 29.3 us -> 20.5 us
  starting transfers between devices: 49.8 us -> 46.7 us
    ppermute x25 -> x24, waiting for transfers between devices: 25.8 us -> 18.8 us  [shift(): lax.ppermute(block, axis, [(i, (i + step) % count) for i in range(count)])]
    ppermute x25 -> x24, starting transfers between devices: 40.4 us -> 35.8 us  [shift(): lax.ppermute(block, axis, [(i, (i + step) % count) for i in range(count)])]
    ppermute x2, waiting for transfers between devices: 3.51 us -> 0.01 us  [neighbours(): top = lax.ppermute(to_up, LAT, forward)]
    ppermute x2, waiting for transfers between devices: 0.01 us -> 1.75 us  [neighbours(): bottom = lax.ppermute(to_down, LAT, backward)]
    ppermute x2, starting transfers between devices: 5.55 us -> 6.99 us  [neighbours(): bottom = lax.ppermute(to_down, LAT, backward)]
    pallas_call x8 -> x10, Pallas kernels: 19.5 us -> 20.6 us  [call(): pl.pallas_call(kernel, out_shape=outs, in_specs=in_specs, scratch_shapes=...]
  transfers between devices with their start and end apart: 29 -> 28, of which waited for: 9 -> 8; matrix products, arithmetic and copies ran while one was open for 3% -> 3% of each run, Pallas kernels for 10% -> 12%
where the time goes in v1:
time: 108 us; the launch traced here: 106 us
  starting transfers between devices  46.7 us (43%)
  Pallas kernels  20.6 us (19%)
  waiting for transfers between devices  20.5 us (19%)
  blocking collectives  14.3 us (13%)
  other arithmetic  2.04 us (2%)
    ppermute x24, starting transfers between devices, shift(): lax.ppermute(block, axis, [(i, (i + step) % count) for i in range(count)])  35.8 us
    pallas_call x10, Pallas kernels, call(): pl.pallas_call(kernel, out_shape=outs, in_specs=in_specs, scratch_shapes=...  20.6 us
    ppermute x24, waiting for transfers between devices, shift(): lax.ppermute(block, axis, [(i, (i + step) % count) for i in range(count)])  18.8 us
    all_to_all x1, blocking collectives, block(): lax.all_to_all(packed, ('zlo', 'zhi'), split_axis=0, concat_axis=0, tiled...  14.3 us
    ppermute x2, starting transfers between devices, neighbours(): bottom = lax.ppermute(to_down, LAT, backward)  6.99 us
    ppermute x2, starting transfers between devices, neighbours(): top = lax.ppermute(to_up, LAT, forward)  3.83 us
  transfers between devices with their start and end apart: 28, of which 8 were waited for; matrix products, arithmetic and copies ran while one was open for 3% of the time, Pallas kernels for 12%

profile of v1, /device:TPU:8, one launch (start us, length us, event | category | flops | bytes accessed | tf_op | source)
XLA Modules:
  0.0 106.1 jit_solution(3753207442039523052)
XLA Ops:
  0.7 4.7 %collective-permute-start.1 = (bf16[192,640]{1,0:T(8,128)(2,1)}, bf16[192,640]{1,0:T(8,128)(2,1)S(1)}, u32[]{:S(2)}, u32[]{:S(2)}) collective-permute-start(bf16[192,640]{1,0:T(8,128)(2,1)} %bitcast.21), channel_id=1, source_target_pairs={{0,24},{8,0},{16,8},{24,16},{1,25},{9,1},{17,9},{25,17},{2,26},{10... | collective-permute-start | bytes 737288 | tf_op jit(solution)/shard_map/ppermute | solution.py:43
  5.4 0.9 fusion.21
  6.2 1.9 %collective-permute-start.2 = (bf16[32,640]{1,0:T(8,128)(2,1)S(1)}, bf16[32,640]{1,0:T(8,128)(2,1)S(1)}, u32[]{:S(2)}, u32[]{:S(2)}) collective-permute-start(bf16[32,640]{1,0:T(8,128)(2,1)S(1)} %bitcast.29), channel_id=1, source_target_pairs={{0,32},{32,64},{64,96},{96,128},{128,160},{160,192},{192,224},{1,3... | collective-permute-start | bytes 122888 | tf_op jit(solution)/shard_map/ppermute | solution.py:359
  8.1 3.6 %collective-permute-start.3 = (bf16[32,640]{1,0:T(8,128)(2,1)S(1)}, bf16[32,640]{1,0:T(8,128)(2,1)S(1)}, u32[]{:S(2)}, u32[]{:S(2)}) collective-permute-start(bf16[32,640]{1,0:T(8,128)(2,1)S(1)} %bitcast.28), channel_id=1, source_target_pairs={{32,0},{64,32},{96,64},{128,96},{160,128},{192,160},{224,192},{33,... | collective-permute-start | bytes 122888 | tf_op jit(solution)/shard_map/ppermute | solution.py:360
  11.9 0.7 add_select_fusion
  12.6 0.7 convert_bitcast_fusion
  13.4 0.1 broadcast_compare_fusion
  13.5 0.2 select_reduce_fusion
  13.9 0.7 collective-permute-start.6
  14.6 2.2 %collective-permute-done.left = bf16[192,640]{1,0:T(8,128)(2,1)S(1)} collective-permute-done((bf16[192,640]{1,0:T(8,128)(2,1)}, bf16[192,640]{1,0:T(8,128)(2,1)S(1)}, u32[]{:S(2)}, u32[]{:S(2)}) %collective-permute-start) | collective-permute-done | bytes 245792 | tf_op jit(solution)/shard_map/ppermute | solution.py:43
  16.8 0.6 shard_map.110
  17.4 2.1 %collective-permute-start.4 = (bf16[80,640]{1,0:T(8,128)(2,1)S(1)}, bf16[80,640]{1,0:T(8,128)(2,1)S(1)}, u32[]{:S(2)}, u32[]{:S(2)}) collective-permute-start(bf16[80,640]{1,0:T(8,128)(2,1)S(1)} %get-tuple-element.41), channel_id=1, source_target_pairs={{0,8},{8,16},{16,24},{24,0},{1,9},{9,17},{17,25},{25,1},{2,10},{10... | collective-permute-start | bytes 307208 | tf_op jit(solution)/shard_map/ppermute | solution.py:43
  19.4 1.8 %collective-permute-start.5 = (bf16[80,640]{1,0:T(8,128)(2,1)S(1)}, bf16[80,640]{1,0:T(8,128)(2,1)S(1)}, u32[]{:S(2)}, u32[]{:S(2)}) collective-permute-start(bf16[80,640]{1,0:T(8,128)(2,1)S(1)} %get-tuple-element.42), channel_id=1, source_target_pairs={{0,24},{8,0},{16,8},{24,16},{1,25},{9,1},{17,9},{25,17},{2,26},{10... | collective-permute-start | bytes 307208 | tf_op jit(solution)/shard_map/ppermute | solution.py:43
  21.3 0.2 fusion.order
  21.5 2.8 %collective-permute-done.4.left_side.left_e = bf16[80,640]{1,0:T(8,128)(2,1)S(1)} collective-permute-done((bf16[80,640]{1,0:T(8,128)(2,1)S(1)}, bf16[80,640]{1,0:T(8,128)(2,1)S(1)}, u32[]{:S(2)}, u32[]{:S(2)}) %collective-permute-start.4) | collective-permute-done | bytes 102432 | tf_op jit(solution)/shard_map/ppermute | solution.py:43
  24.4 1.0 collective-permute-done.5.right_side.right_e
  25.4 7.1 %shard_map.111 = (bf16[192,640]{1,0:T(8,128)(2,1)}, bf16[192,640]{1,0:T(8,128)(2,1)S(1)}, bf16[192,2176]{1,0:T(8,128)(2,1)S(1)}, bf16[192,1920]{1,0:T(8,128)(2,1...) custom-call(s32[5]{0:T(128)S(1)} %stack.23.place, ...), custom_call_target="tpu_custom_call" | custom-call | tf_op jit(solution)/shard_map/pallas_call | solution.py:345
  32.6 0.5 collective-permute-start.21
  33.1 1.7 %collective-permute-done.8.other = bf16[192,1920]{1,0:T(8,128)(2,1)S(1)} collective-permute-done((bf16[192,1920]{1,0:T(8,128)(2,1)S(1)}, bf16[192,1920]{1,0:T(8,128)(2,1)S(1)}, u32[]{:S(2)}, u32[]{:S(2)}) %collective-permute-start.8) | collective-permute-done | bytes 737312 | tf_op jit(solution)/shard_map/ppermute | solution.py:43
  34.8 3.2 %shard_map.112 = (f32[320,640]{1,0:T(8,128)S(1)}, bf16[320,640]{1,0:T(8,128)(2,1)S(1)}, bf16[320,640]{1,0:T(8,128)(2,1)S(1)}, bf16[320,640]{1,0:T(8,128)(2,1)S(1)}) custom-call(s32[5]{0:T(128)S(1)} %stack.23.place, bf16[192,1920]{1,0:T(8,128)(2,1)S(1)} %get-tuple-element.45.mine, bf16[192,1920]{1,0:T(8,128)(2,1)S(1)} %collective-permute-done.8.other, ...), custom_call_target="tpu_custom_call" | custom-call | tf_op jit(solution)/shard_map/pallas_call | solution.py:345
  38.0 1.6 %collective-permute-start.9 = (bf16[320,640]{1,0:T(8,128)(2,1)S(1)}, bf16[320,640]{1,0:T(8,128)(2,1)S(1)}, u32[]{:S(2)}, u32[]{:S(2)}) collective-permute-start(bf16[320,640]{1,0:T(8,128)(2,1)S(1)} %get-tuple-element.50), channel_id=1, source_target_pairs={{0,2},{2,4},{4,6},{6,0},{1,3},{3,5},{5,7},{7,1},{8,10},{10,12},{12... | collective-permute-start | bytes 1228808 | tf_op jit(solution)/shard_map/ppermute | solution.py:43
  39.6 2.7 %collective-permute-start.10 = (bf16[320,640]{1,0:T(8,128)(2,1)S(1)}, bf16[320,640]{1,0:T(8,128)(2,1)S(1)}, u32[]{:S(2)}, u32[]{:S(2)}) collective-permute-start(bf16[320,640]{1,0:T(8,128)(2,1)S(1)} %get-tuple-element.51), channel_id=1, source_target_pairs={{0,4},{2,6},{4,0},{6,2},{1,5},{3,7},{5,1},{7,3},{8,12},{10,14},{12... | collective-permute-start | bytes 1228808 | tf_op jit(solution)/shard_map/ppermute | solution.py:43
  42.3 1.4 %collective-permute-start.11 = (bf16[320,640]{1,0:T(8,128)(2,1)S(1)}, bf16[320,640]{1,0:T(8,128)(2,1)S(1)}, u32[]{:S(2)}, u32[]{:S(2)}) collective-permute-start(bf16[320,640]{1,0:T(8,128)(2,1)S(1)} %get-tuple-element.52), channel_id=1, source_target_pairs={{0,6},{2,0},{4,2},{6,4},{1,7},{3,1},{5,3},{7,5},{8,14},{10,8},{12,... | collective-permute-start | bytes 1228808 | tf_op jit(solution)/shard_map/ppermute | solution.py:43
  43.8 1.9 %collective-permute-start.14 = (bf16[40,640]{1,0:T(8,128)(2,1)S(1)}, bf16[40,640]{1,0:T(8,128)(2,1)S(1)}, u32[]{:S(2)}, u32[]{:S(2)}) collective-permute-start(bf16[40,640]{1,0:T(8,128)(2,1)S(1)} %get-tuple-element.55), channel_id=1, source_target_pairs={{0,32},{32,64},{64,96},{96,128},{128,160},{160,192},{192,224},{1,3... | collective-permute-start | bytes 153608 | tf_op jit(solution)/shard_map/ppermute | solution.py:359
  45.7 2.0 %shard_map.116 = (f32[320,640]{1,0:T(8,128)S(1)}, bf16[320,640]{1,0:T(8,128)(2,1)S(1)}, bf16[320,640]{1,0:T(8,128)(2,1)S(1)}, bf16[320,640]{1,0:T(8,128)(2,1)S(1)}) custom-call(s32[5]{0:T(128)S(1)} %stack.23.place, bf16[192,2176]{1,0:T(8,128)(2,1)S(1)} %get-tuple-element.64.mine, bf16[192,2176]{1,0:T(8,128)(2,1)S(1)} %collective-permute-done.21.other), custom_call_target="tpu_custom_call" | custom-call | tf_op jit(solution)/shard_map/pallas_call | solution.py:345
  47.7 1.7 %collective-permute-start.22 = (bf16[320,640]{1,0:T(8,128)(2,1)S(1)}, bf16[320,640]{1,0:T(8,128)(2,1)S(1)}, u32[]{:S(2)}, u32[]{:S(2)}) collective-permute-start(bf16[320,640]{1,0:T(8,128)(2,1)S(1)} %get-tuple-element.67), channel_id=1, source_target_pairs={{0,64},{64,128},{128,192},{192,0},{1,65},{65,129},{129,193},{193,1... | collective-permute-start | bytes 1228808 | tf_op jit(solution)/shard_map/ppermute | solution.py:43
  49.3 3.4 %collective-permute-start.15 = (bf16[40,640]{1,0:T(8,128)(2,1)S(1)}, bf16[40,640]{1,0:T(8,128)(2,1)S(1)}, u32[]{:S(2)}, u32[]{:S(2)}) collective-permute-start(bf16[40,640]{1,0:T(8,128)(2,1)S(1)} %get-tuple-element.56), channel_id=1, source_target_pairs={{32,0},{64,32},{96,64},{128,96},{160,128},{192,160},{224,192},{33,... | collective-permute-start | bytes 153608 | tf_op jit(solution)/shard_map/ppermute | solution.py:360
  52.7 1.7 %collective-permute-done.15.bottom = bf16[40,640]{1,0:T(8,128)(2,1)S(1)} collective-permute-done((bf16[40,640]{1,0:T(8,128)(2,1)S(1)}, bf16[40,640]{1,0:T(8,128)(2,1)S(1)}, u32[]{:S(2)}, u32[]{:S(2)}) %collective-permute-start.15) | collective-permute-done | bytes 51232 | tf_op jit(solution)/shard_map/ppermute | solution.py:360
  54.4 1.0 collective-permute-start.23
  55.5 2.3 %collective-permute-start.24 = (bf16[320,640]{1,0:T(8,128)(2,1)S(1)}, bf16[320,640]{1,0:T(8,128)(2,1)S(1)}, u32[]{:S(2)}, u32[]{:S(2)}) collective-permute-start(bf16[320,640]{1,0:T(8,128)(2,1)S(1)} %get-tuple-element.69), channel_id=1, source_target_pairs={{0,192},{64,0},{128,64},{192,128},{1,193},{65,1},{129,65},{193,129... | collective-permute-start | bytes 1228808 | tf_op jit(solution)/shard_map/ppermute | solution.py:43
  57.8 2.8 %collective-permute-done.10.r2 = bf16[320,640]{1,0:T(8,128)(2,1)S(1)} collective-permute-done((bf16[320,640]{1,0:T(8,128)(2,1)S(1)}, bf16[320,640]{1,0:T(8,128)(2,1)S(1)}, u32[]{:S(2)}, u32[]{:S(2)}) %collective-permute-start.10) | collective-permute-done | bytes 409632 | tf_op jit(solution)/shard_map/ppermute | solution.py:43
  60.6 2.5 %collective-permute-start.13 = (bf16[192,640]{1,0:T(8,128)(2,1)S(1)}, bf16[192,640]{1,0:T(8,128)(2,1)S(1)}, u32[]{:S(2)}, u32[]{:S(2)}) collective-permute-start(bf16[192,640]{1,0:T(8,128)(2,1)S(1)} %get-tuple-element.54.tile), channel_id=1, source_target_pairs={{0,24},{8,0},{16,8},{24,16},{1,25},{9,1},{17,9},{25,17},{2,26},{10... | collective-permute-start | bytes 737288 | tf_op jit(solution)/shard_map/ppermute | solution.py:43
  63.1 0.9 shard_map.113
  64.0 5.4 %collective-permute-done.13.right = bf16[192,640]{1,0:T(8,128)(2,1)S(1)} collective-permute-done((bf16[192,640]{1,0:T(8,128)(2,1)S(1)}, bf16[192,640]{1,0:T(8,128)(2,1)S(1)}, u32[]{:S(2)}, u32[]{:S(2)}) %collective-permute-start.13) | collective-permute-done | bytes 245792 | tf_op jit(solution)/shard_map/ppermute | solution.py:43
  69.5 1.6 %collective-permute-start.18 = (bf16[80,640]{1,0:T(8,128)(2,1)S(1)}, bf16[80,640]{1,0:T(8,128)(2,1)S(1)}, u32[]{:S(2)}, u32[]{:S(2)}) collective-permute-start(bf16[80,640]{1,0:T(8,128)(2,1)S(1)} %get-tuple-element.61), channel_id=1, source_target_pairs={{0,64},{64,128},{128,192},{192,0},{1,65},{65,129},{129,193},{193,1... | collective-permute-start | bytes 307208 | tf_op jit(solution)/shard_map/ppermute | solution.py:43
  71.0 2.7 %collective-permute-done.12.left = bf16[192,640]{1,0:T(8,128)(2,1)S(1)} collective-permute-done((bf16[192,640]{1,0:T(8,128)(2,1)S(1)}, bf16[192,640]{1,0:T(8,128)(2,1)S(1)}, u32[]{:S(2)}, u32[]{:S(2)}) %collective-permute-start.12) | collective-permute-done | bytes 245792 | tf_op jit(solution)/shard_map/ppermute | solution.py:43
  73.8 0.6 shard_map.114
  74.3 1.9 %collective-permute-start.16 = (bf16[64,640]{1,0:T(8,128)(2,1)S(1)}, bf16[64,640]{1,0:T(8,128)(2,1)S(1)}, u32[]{:S(2)}, u32[]{:S(2)}) collective-permute-start(bf16[64,640]{1,0:T(8,128)(2,1)S(1)} %get-tuple-element.57), channel_id=1, source_target_pairs={{0,8},{8,16},{16,24},{24,0},{1,9},{9,17},{17,25},{25,1},{2,10},{10... | collective-permute-start | bytes 245768 | tf_op jit(solution)/shard_map/ppermute | solution.py:43
  76.2 2.0 %collective-permute-start.17 = (bf16[64,640]{1,0:T(8,128)(2,1)S(1)}, bf16[64,640]{1,0:T(8,128)(2,1)S(1)}, u32[]{:S(2)}, u32[]{:S(2)}) collective-permute-start(bf16[64,640]{1,0:T(8,128)(2,1)S(1)} %get-tuple-element.58), channel_id=1, source_target_pairs={{0,24},{8,0},{16,8},{24,16},{1,25},{9,1},{17,9},{25,17},{2,26},{10... | collective-permute-start | bytes 245768 | tf_op jit(solution)/shard_map/ppermute | solution.py:43
  78.2 2.3 %collective-permute-start.19 = (bf16[80,640]{1,0:T(8,128)(2,1)S(1)}, bf16[80,640]{1,0:T(8,128)(2,1)S(1)}, u32[]{:S(2)}, u32[]{:S(2)}) collective-permute-start(bf16[80,640]{1,0:T(8,128)(2,1)S(1)} %get-tuple-element.62), channel_id=1, source_target_pairs={{0,128},{64,192},{128,0},{192,64},{1,129},{65,193},{129,1},{193,65... | collective-permute-start | bytes 307208 | tf_op jit(solution)/shard_map/ppermute | solution.py:43
  80.6 1.3 %collective-permute-start.20 = (bf16[80,640]{1,0:T(8,128)(2,1)S(1)}, bf16[80,640]{1,0:T(8,128)(2,1)S(1)}, u32[]{:S(2)}, u32[]{:S(2)}) collective-permute-start(bf16[80,640]{1,0:T(8,128)(2,1)S(1)} %get-tuple-element.63), channel_id=1, source_target_pairs={{0,192},{64,0},{128,64},{192,128},{1,193},{65,1},{129,65},{193,129... | collective-permute-start | bytes 307208 | tf_op jit(solution)/shard_map/ppermute | solution.py:43
  81.9 1.0 shard_map.117
  83.0 0.9 collective-permute-start.26
  83.9 2.5 %collective-permute-start.27 = (bf16[80,640]{1,0:T(8,128)(2,1)S(1)}, bf16[80,640]{1,0:T(8,128)(2,1)S(1)}, u32[]{:S(2)}, u32[]{:S(2)}) collective-permute-start(bf16[80,640]{1,0:T(8,128)(2,1)S(1)} %get-tuple-element.73), channel_id=1, source_target_pairs={{0,6},{2,0},{4,2},{6,4},{1,7},{3,1},{5,3},{7,5},{8,14},{10,8},{12,... | collective-permute-start | bytes 307208 | tf_op jit(solution)/shard_map/ppermute | solution.py:43
  86.4 4.5 %shard_map.115 = bf16[192,640]{1,0:T(8,128)(2,1)} custom-call(s32[5]{0:T(128)S(1)} %stack.23.place, bf16[192,640]{1,0:T(8,128)(2,1)S(1)} %get-tuple-element.54.tile, bf16[192,640]{1,0:T(8,128)(2,1)S(1)} %collective-permute-done.12.left, bf16[192,640]{1,0:T(8,128)(2,1)S(1)} %collective-permute-done.13.right, bf16[40,640]{1,0:T(8,128)(2,1)S(1)} %collective-permute-done.14.top, ...), custom_call_target="tpu_custom_call" | custom-call | tf_op jit(solution)/shard_map/pallas_call | solution.py:345
  90.9 0.2 shard_map.118
  91.1 14.3 %all_to_all.5.parts = bf16[8,20,640]{2,1,0:T(8,128)(2,1)S(1)} all-to-all(bf16[8,20,640]{2,1,0:T(8,128)(2,1)S(1)} %shard_map.118), channel_id=1, replica_groups=mesh['y'=4,'core'=2,'zlo'=4,'x'=4,'zhi'=2] {'zlo','zhi'}, dimensions={0} | all-to-all | bytes 409600 | tf_op jit(solution)/shard_map/all_to_all | solution.py:472
  105.4 0.6 shard_map.119
  (37 shorter events, 0.5 us)
Async XLA Ops:
  0.6 24.8 %copy-start.1 = (bf16[1,12,16,640]{3,2,1,0:T(8,128)(2,1)S(1)}, bf16[1,12,16,640]{3,2,1,0:T(8,128)(2,1)}, u32[]{:S(2)}) copy-start(bf16[1,12,16,640]{3,2,1,0:T(8,128)(2,1)} %param.7) | copy-start | bytes 737284
  0.6 24.7 %copy-start = (bf16[1,12,16,640]{3,2,1,0:T(8,128)(2,1)S(1)}, bf16[1,12,16,640]{3,2,1,0:T(8,128)(2,1)}, u32[]{:S(2)}) copy-start(bf16[1,12,16,640]{3,2,1,0:T(8,128)(2,1)} %param.13) | copy-start | bytes 737284
  0.7 13.9 %collective-permute-start.1 = (bf16[192,640]{1,0:T(8,128)(2,1)}, bf16[192,640]{1,0:T(8,128)(2,1)S(1)}, u32[]{:S(2)}, u32[]{:S(2)}) collective-permute-start(bf16[192,640]{1,0:T(8,128)(2,1)} %bitcast.21), channel_id=1, source_target_pairs={{0,24},{8,0},{16,8},{24,16},{1,25},{9,1},{17,9},{25,17},{2,26},{10... | collective-permute-start | bytes 737288 | tf_op jit(solution)/shard_map/ppermute | solution.py:43
  5.4 11.4 %collective-permute-start = (bf16[192,640]{1,0:T(8,128)(2,1)}, bf16[192,640]{1,0:T(8,128)(2,1)S(1)}, u32[]{:S(2)}, u32[]{:S(2)}) collective-permute-start(bf16[192,640]{1,0:T(8,128)(2,1)} %bitcast.22), channel_id=1, source_target_pairs={{0,8},{8,16},{16,24},{24,0},{1,9},{9,17},{17,25},{25,1},{2,10},{10... | collective-permute-start | bytes 737288 | tf_op jit(solution)/shard_map/ppermute | solution.py:43
  6.2 7.7 %collective-permute-start.2 = (bf16[32,640]{1,0:T(8,128)(2,1)S(1)}, bf16[32,640]{1,0:T(8,128)(2,1)S(1)}, u32[]{:S(2)}, u32[]{:S(2)}) collective-permute-start(bf16[32,640]{1,0:T(8,128)(2,1)S(1)} %bitcast.29), channel_id=1, source_target_pairs={{0,32},{32,64},{64,96},{96,128},{128,160},{160,192},{192,224},{1,3... | collective-permute-start | bytes 122888 | tf_op jit(solution)/shard_map/ppermute | solution.py:359
  8.1 6.4 %collective-permute-start.3 = (bf16[32,640]{1,0:T(8,128)(2,1)S(1)}, bf16[32,640]{1,0:T(8,128)(2,1)S(1)}, u32[]{:S(2)}, u32[]{:S(2)}) collective-permute-start(bf16[32,640]{1,0:T(8,128)(2,1)S(1)} %bitcast.28), channel_id=1, source_target_pairs={{32,0},{64,32},{96,64},{128,96},{160,128},{192,160},{224,192},{33,... | collective-permute-start | bytes 122888 | tf_op jit(solution)/shard_map/ppermute | solution.py:360
  11.8 9.7 %collective-permute-start.7 = (bf16[192,640]{1,0:T(8,128)(2,1)}, bf16[192,640]{1,0:T(8,128)(2,1)S(1)}, u32[]{:S(2)}, u32[]{:S(2)}) collective-permute-start(bf16[192,640]{1,0:T(8,128)(2,1)} %bitcast.18), channel_id=1, source_target_pairs={{0,32},{32,0},{1,33},{33,1},{2,34},{34,2},{3,35},{35,3},{4,36},{36... | collective-permute-start | bytes 737288 | tf_op jit(solution)/shard_map/ppermute | solution.py:43
  13.9 7.6 %collective-permute-start.6 = (bf16[16,640]{1,0:T(8,128)(2,1)S(1)}, bf16[16,640]{1,0:T(8,128)(2,1)S(1)}, u32[]{:S(2)}, u32[]{:S(2)}) collective-permute-start(bf16[16,640]{1,0:T(8,128)(2,1)S(1)} %pad.4.rest_0_.own_e), channel_id=1, source_target_pairs={{0,16},{8,24},{16,0},{24,8},{1,17},{9,25},{17,1},{25,9},{2,18},{10... | collective-permute-start | bytes 61448 | tf_op jit(solution)/shard_map/ppermute | solution.py:43
  17.4 7.0 %collective-permute-start.4 = (bf16[80,640]{1,0:T(8,128)(2,1)S(1)}, bf16[80,640]{1,0:T(8,128)(2,1)S(1)}, u32[]{:S(2)}, u32[]{:S(2)}) collective-permute-start(bf16[80,640]{1,0:T(8,128)(2,1)S(1)} %get-tuple-element.41), channel_id=1, source_target_pairs={{0,8},{8,16},{16,24},{24,0},{1,9},{9,17},{17,25},{25,1},{2,10},{10... | collective-permute-start | bytes 307208 | tf_op jit(solution)/shard_map/ppermute | solution.py:43
  19.4 5.9 %collective-permute-start.5 = (bf16[80,640]{1,0:T(8,128)(2,1)S(1)}, bf16[80,640]{1,0:T(8,128)(2,1)S(1)}, u32[]{:S(2)}, u32[]{:S(2)}) collective-permute-start(bf16[80,640]{1,0:T(8,128)(2,1)S(1)} %get-tuple-element.42), channel_id=1, source_target_pairs={{0,24},{8,0},{16,8},{24,16},{1,25},{9,1},{17,9},{25,17},{2,26},{10... | collective-permute-start | bytes 307208 | tf_op jit(solution)/shard_map/ppermute | solution.py:43
  32.5 2.3 %collective-permute-start.8 = (bf16[192,1920]{1,0:T(8,128)(2,1)S(1)}, bf16[192,1920]{1,0:T(8,128)(2,1)S(1)}, u32[]{:S(2)}, u32[]{:S(2)}) collective-permute-start(bf16[192,1920]{1,0:T(8,128)(2,1)S(1)} %get-tuple-element.46), channel_id=1, source_target_pairs={{0,32},{32,0},{1,33},{33,1},{2,34},{34,2},{3,35},{35,3},{4,36},{36... | collective-permute-start | bytes 2211848 | tf_op jit(solution)/shard_map/ppermute | solution.py:43
  32.6 13.0 %collective-permute-start.21 = (bf16[192,2176]{1,0:T(8,128)(2,1)S(1)}, bf16[192,2176]{1,0:T(8,128)(2,1)S(1)}, u32[]{:S(2)}, u32[]{:S(2)}) collective-permute-start(bf16[192,2176]{1,0:T(8,128)(2,1)S(1)} %get-tuple-element.65), channel_id=1, source_target_pairs={{0,32},{32,0},{1,33},{33,1},{2,34},{34,2},{3,35},{35,3},{4,36},{36... | collective-permute-start | bytes 2506760 | tf_op jit(solution)/shard_map/ppermute | solution.py:43
  38.0 17.5 %collective-permute-start.9 = (bf16[320,640]{1,0:T(8,128)(2,1)S(1)}, bf16[320,640]{1,0:T(8,128)(2,1)S(1)}, u32[]{:S(2)}, u32[]{:S(2)}) collective-permute-start(bf16[320,640]{1,0:T(8,128)(2,1)S(1)} %get-tuple-element.50), channel_id=1, source_target_pairs={{0,2},{2,4},{4,6},{6,0},{1,3},{3,5},{5,7},{7,1},{8,10},{10,12},{12... | collective-permute-start | bytes 1228808 | tf_op jit(solution)/shard_map/ppermute | solution.py:43
  39.6 21.0 %collective-permute-start.10 = (bf16[320,640]{1,0:T(8,128)(2,1)S(1)}, bf16[320,640]{1,0:T(8,128)(2,1)S(1)}, u32[]{:S(2)}, u32[]{:S(2)}) collective-permute-start(bf16[320,640]{1,0:T(8,128)(2,1)S(1)} %get-tuple-element.51), channel_id=1, source_target_pairs={{0,4},{2,6},{4,0},{6,2},{1,5},{3,7},{5,1},{7,3},{8,12},{10,14},{12... | collective-permute-start | bytes 1228808 | tf_op jit(solution)/shard_map/ppermute | solution.py:43
  42.3 20.8 %collective-permute-start.11 = (bf16[320,640]{1,0:T(8,128)(2,1)S(1)}, bf16[320,640]{1,0:T(8,128)(2,1)S(1)}, u32[]{:S(2)}, u32[]{:S(2)}) collective-permute-start(bf16[320,640]{1,0:T(8,128)(2,1)S(1)} %get-tuple-element.52), channel_id=1, source_target_pairs={{0,6},{2,0},{4,2},{6,4},{1,7},{3,1},{5,3},{7,5},{8,14},{10,8},{12,... | collective-permute-start | bytes 1228808 | tf_op jit(solution)/shard_map/ppermute | solution.py:43
  43.8 5.6 %collective-permute-start.14 = (bf16[40,640]{1,0:T(8,128)(2,1)S(1)}, bf16[40,640]{1,0:T(8,128)(2,1)S(1)}, u32[]{:S(2)}, u32[]{:S(2)}) collective-permute-start(bf16[40,640]{1,0:T(8,128)(2,1)S(1)} %get-tuple-element.55), channel_id=1, source_target_pairs={{0,32},{32,64},{64,96},{96,128},{128,160},{160,192},{192,224},{1,3... | collective-permute-start | bytes 153608 | tf_op jit(solution)/shard_map/ppermute | solution.py:359
  47.7 28.5 %collective-permute-start.22 = (bf16[320,640]{1,0:T(8,128)(2,1)S(1)}, bf16[320,640]{1,0:T(8,128)(2,1)S(1)}, u32[]{:S(2)}, u32[]{:S(2)}) collective-permute-start(bf16[320,640]{1,0:T(8,128)(2,1)S(1)} %get-tuple-element.67), channel_id=1, source_target_pairs={{0,64},{64,128},{128,192},{192,0},{1,65},{65,129},{129,193},{193,1... | collective-permute-start | bytes 1228808 | tf_op jit(solution)/shard_map/ppermute | solution.py:43
  49.3 5.1 %collective-permute-start.15 = (bf16[40,640]{1,0:T(8,128)(2,1)S(1)}, bf16[40,640]{1,0:T(8,128)(2,1)S(1)}, u32[]{:S(2)}, u32[]{:S(2)}) collective-permute-start(bf16[40,640]{1,0:T(8,128)(2,1)S(1)} %get-tuple-element.56), channel_id=1, source_target_pairs={{32,0},{64,32},{96,64},{128,96},{160,128},{192,160},{224,192},{33,... | collective-permute-start | bytes 153608 | tf_op jit(solution)/shard_map/ppermute | solution.py:360
  54.4 23.8 %collective-permute-start.23 = (bf16[320,640]{1,0:T(8,128)(2,1)S(1)}, bf16[320,640]{1,0:T(8,128)(2,1)S(1)}, u32[]{:S(2)}, u32[]{:S(2)}) collective-permute-start(bf16[320,640]{1,0:T(8,128)(2,1)S(1)} %get-tuple-element.68), channel_id=1, source_target_pairs={{0,128},{64,192},{128,0},{192,64},{1,129},{65,193},{129,1},{193,65... | collective-permute-start | bytes 1228808 | tf_op jit(solution)/shard_map/ppermute | solution.py:43
  55.5 25.1 %collective-permute-start.24 = (bf16[320,640]{1,0:T(8,128)(2,1)S(1)}, bf16[320,640]{1,0:T(8,128)(2,1)S(1)}, u32[]{:S(2)}, u32[]{:S(2)}) collective-permute-start(bf16[320,640]{1,0:T(8,128)(2,1)S(1)} %get-tuple-element.69), channel_id=1, source_target_pairs={{0,192},{64,0},{128,64},{192,128},{1,193},{65,1},{129,65},{193,129... | collective-permute-start | bytes 1228808 | tf_op jit(solution)/shard_map/ppermute | solution.py:43
  60.6 8.9 %collective-permute-start.13 = (bf16[192,640]{1,0:T(8,128)(2,1)S(1)}, bf16[192,640]{1,0:T(8,128)(2,1)S(1)}, u32[]{:S(2)}, u32[]{:S(2)}) collective-permute-start(bf16[192,640]{1,0:T(8,128)(2,1)S(1)} %get-tuple-element.54.tile), channel_id=1, source_target_pairs={{0,24},{8,0},{16,8},{24,16},{1,25},{9,1},{17,9},{25,17},{2,26},{10... | collective-permute-start | bytes 737288 | tf_op jit(solution)/shard_map/ppermute | solution.py:43
  63.1 10.7 %collective-permute-start.12 = (bf16[192,640]{1,0:T(8,128)(2,1)S(1)}, bf16[192,640]{1,0:T(8,128)(2,1)S(1)}, u32[]{:S(2)}, u32[]{:S(2)}) collective-permute-start(bf16[192,640]{1,0:T(8,128)(2,1)S(1)} %get-tuple-element.54.tile), channel_id=1, source_target_pairs={{0,8},{8,16},{16,24},{24,0},{1,9},{9,17},{17,25},{25,1},{2,10},{10... | collective-permute-start | bytes 737288 | tf_op jit(solution)/shard_map/ppermute | solution.py:43
  69.5 14.4 %collective-permute-start.18 = (bf16[80,640]{1,0:T(8,128)(2,1)S(1)}, bf16[80,640]{1,0:T(8,128)(2,1)S(1)}, u32[]{:S(2)}, u32[]{:S(2)}) collective-permute-start(bf16[80,640]{1,0:T(8,128)(2,1)S(1)} %get-tuple-element.61), channel_id=1, source_target_pairs={{0,64},{64,128},{128,192},{192,0},{1,65},{65,129},{129,193},{193,1... | collective-permute-start | bytes 307208 | tf_op jit(solution)/shard_map/ppermute | solution.py:43
  74.3 8.5 %collective-permute-start.16 = (bf16[64,640]{1,0:T(8,128)(2,1)S(1)}, bf16[64,640]{1,0:T(8,128)(2,1)S(1)}, u32[]{:S(2)}, u32[]{:S(2)}) collective-permute-start(bf16[64,640]{1,0:T(8,128)(2,1)S(1)} %get-tuple-element.57), channel_id=1, source_target_pairs={{0,8},{8,16},{16,24},{24,0},{1,9},{9,17},{17,25},{25,1},{2,10},{10... | collective-permute-start | bytes 245768 | tf_op jit(solution)/shard_map/ppermute | solution.py:43
  76.2 6.8 %collective-permute-start.17 = (bf16[64,640]{1,0:T(8,128)(2,1)S(1)}, bf16[64,640]{1,0:T(8,128)(2,1)S(1)}, u32[]{:S(2)}, u32[]{:S(2)}) collective-permute-start(bf16[64,640]{1,0:T(8,128)(2,1)S(1)} %get-tuple-element.58), channel_id=1, source_target_pairs={{0,24},{8,0},{16,8},{24,16},{1,25},{9,1},{17,9},{25,17},{2,26},{10... | collective-permute-start | bytes 245768 | tf_op jit(solution)/shard_map/ppermute | solution.py:43
  78.2 12.6 %collective-permute-start.19 = (bf16[80,640]{1,0:T(8,128)(2,1)S(1)}, bf16[80,640]{1,0:T(8,128)(2,1)S(1)}, u32[]{:S(2)}, u32[]{:S(2)}) collective-permute-start(bf16[80,640]{1,0:T(8,128)(2,1)S(1)} %get-tuple-element.62), channel_id=1, source_target_pairs={{0,128},{64,192},{128,0},{192,64},{1,129},{65,193},{129,1},{193,65... | collective-permute-start | bytes 307208 | tf_op jit(solution)/shard_map/ppermute | solution.py:43
  80.6 10.3 %collective-permute-start.20 = (bf16[80,640]{1,0:T(8,128)(2,1)S(1)}, bf16[80,640]{1,0:T(8,128)(2,1)S(1)}, u32[]{:S(2)}, u32[]{:S(2)}) collective-permute-start(bf16[80,640]{1,0:T(8,128)(2,1)S(1)} %get-tuple-element.63), channel_id=1, source_target_pairs={{0,192},{64,0},{128,64},{192,128},{1,193},{65,1},{129,65},{193,129... | collective-permute-start | bytes 307208 | tf_op jit(solution)/shard_map/ppermute | solution.py:43
  82.9 8.0 %collective-permute-start.25 = (bf16[80,640]{1,0:T(8,128)(2,1)S(1)}, bf16[80,640]{1,0:T(8,128)(2,1)S(1)}, u32[]{:S(2)}, u32[]{:S(2)}) collective-permute-start(bf16[80,640]{1,0:T(8,128)(2,1)S(1)} %get-tuple-element.71), channel_id=1, source_target_pairs={{0,2},{2,4},{4,6},{6,0},{1,3},{3,5},{5,7},{7,1},{8,10},{10,12},{12... | collective-permute-start | bytes 307208 | tf_op jit(solution)/shard_map/ppermute | solution.py:43
  83.0 7.9 %collective-permute-start.26 = (bf16[80,640]{1,0:T(8,128)(2,1)S(1)}, bf16[80,640]{1,0:T(8,128)(2,1)S(1)}, u32[]{:S(2)}, u32[]{:S(2)}) collective-permute-start(bf16[80,640]{1,0:T(8,128)(2,1)S(1)} %get-tuple-element.72), channel_id=1, source_target_pairs={{0,4},{2,6},{4,0},{6,2},{1,5},{3,7},{5,1},{7,3},{8,12},{10,14},{12... | collective-permute-start | bytes 307208 | tf_op jit(solution)/shard_map/ppermute | solution.py:43
  83.9 7.0 %collective-permute-start.27 = (bf16[80,640]{1,0:T(8,128)(2,1)S(1)}, bf16[80,640]{1,0:T(8,128)(2,1)S(1)}, u32[]{:S(2)}, u32[]{:S(2)}) collective-permute-start(bf16[80,640]{1,0:T(8,128)(2,1)S(1)} %get-tuple-element.73), channel_id=1, source_target_pairs={{0,6},{2,0},{4,2},{6,4},{1,7},{3,1},{5,3},{7,5},{8,14},{10,8},{12,... | collective-permute-start | bytes 307208 | tf_op jit(solution)/shard_map/ppermute | solution.py:43

commit v2 on v1

--- a/solution.py
+++ b/solution.py
@@ -84,14 +84,11 @@
         polar(CYCLES - 4, RIM, CYCLES)
 
 
-def side_kernel(place, left, right, top, bottom, *rest):
-    *extra, to_right, to_left = rest
+def side_kernel(place, left, right, top, bottom, to_right, to_left):
     lat = place[0]
     for to in (to_right, to_left):
         to[0:RIM, :] = top[0:RIM, :]
         to[RIM : 2 * RIM, :] = bottom[0:RIM, :]
-        if extra:
-            to[2 * RIM :, :] = extra[0][...]
 
     @pl.when(lat == 0)
     def _():
@@ -109,31 +106,67 @@
         coef[d, at : at + rows.shape[0], :] = rows[:, d * 128 : (d + 1) * 128]
 
 
-def band_rows(win, band, coef, cycle, row_of):
+def fill_band(band, coef, row_of):
     low_half = lax.broadcasted_iota(jnp.int32, (LON, 2 * NLON), 1) < NLON
     for k in range(BASIS):
         rolled = []
         for d in range(SPAN):
             row, lane = row_of(d, k)
-            values = coef[lane, pl.ds(row, 1), :]
-            spread_row = jnp.broadcast_to(values, (LON, 2 * NLON))
-            rolled.append(pltpu.roll(spread_row, LON, 1, stride=1, stride_axis=0))
+            values = jnp.broadcast_to(coef[lane, pl.ds(row, 1), :], (LON, 2 * NLON))
+            rolled.append(pltpu.roll(values, LON, 1, stride=1, stride_axis=0))
         at = k * LON
         band[at : at + LON, 0:128] = jnp.where(low_half, rolled[0], rolled[1]).astype(bf16)
         band[at : at + LON, 128:256] = jnp.where(low_half, rolled[2], rolled[3]).astype(bf16)
         band[at : at + LON, 256:384] = rolled[4].astype(bf16)
+
+
+def apply_band(band, win, cycle, out):
     window = win[cycle * NLON : cycle * NLON + SPAN * NLON, :]
-    return dot(band[:, 0 : SPAN * NLON], window, ((1,), (0,)))
+    rows = dot(band[:, 0 : SPAN * NLON], window, ((1,), (0,)))
+    for k in range(BASIS):
+        out[cycle * LON : (cycle + 1) * LON, k * EMBED : (k + 1) * EMBED] = rows[
+            k * LON : (k + 1) * LON, :
+        ].astype(bf16)
+
+
+def first_row(cycle, lon):
+    return lax.rem(cycle // OWNED - lon + 1 + 4, 4) * 16 + (cycle % OWNED) * BASIS
+
+
+def band_kernel(
+    place, left_e, own_e, right_e, far_e, tangent, out_hbm,
+    bands, hidden_grad, edge_down, edge_up, coef, weight_out, sem
+):
+    lon = place[1]
+    load = pltpu.make_async_copy(out_hbm, weight_out, sem)
+    load.start()
+    for group, e in enumerate((left_e, own_e, right_e, far_e)):
+        set_rows(coef, group * 16, e[...].astype(f32))
+    for i in range(CYCLES):
+        start = first_row(i, lon)
+        fill_band(
+            bands.at[i * BASIS * LON : (i + 1) * BASIS * LON], coef, lambda d, k: (start + k, d)
+        )
+    for edge, first in ((edge_down, 0), (edge_up, CYCLES - HALO)):
+        rows = []
+        for cycle in range(first, first + HALO):
+            start = first_row(cycle, lon)
+            for k in range(BASIS):
+                rows.append(
+                    jnp.concatenate([coef[d, pl.ds(start + k, 1), :] for d in range(SPAN)], axis=1)
+                )
+        edge[...] = jnp.concatenate(rows, axis=0).astype(bf16)
+    load.wait()
+    hidden_grad[...] = dot(tangent[...], weight_out[...], ((1,), (1,)))
 
 
 def forward_kernel(
-    place, tile, left, right, top, bottom, left_side, right_side, far_e, own_e,
-    tangent, conv_hbm, in_hbm, out_hbm,
+    place, tile, left, right, top, bottom, left_side, right_side, bands, hidden_grad,
+    edge_down, edge_up, tangent, conv_hbm, in_hbm, out_hbm,
     out, blend_grad, mine, mine_mlp, theirs, theirs_mlp, to_up, to_down,
-    win, band, coef, spread, conv_weight, weight_in, weight_out, sems
+    win, spread, conv_weight, weight_in, weight_out, sems
 ):
     lat = place[0]
-    lon = place[1]
     core = place[2]
     loads = [
         pltpu.make_async_copy(source, target, sems.at[i])
@@ -144,21 +177,8 @@
     for load in loads:
         load.start()
     fill_window(win, tile, left, right, top, bottom, left_side, right_side, lat)
-    set_rows(coef, 0, left_side[2 * RIM :, :].astype(f32))
-    set_rows(coef, 16, own_e[...].astype(f32))
-    set_rows(coef, 32, right_side[2 * RIM :, :].astype(f32))
-    set_rows(coef, 48, far_e[...].astype(f32))
-
-    def base(cycle):
-        return lax.rem(cycle // OWNED - lon + 1 + 4, 4) * 16 + (cycle % OWNED) * BASIS
-
     for i in range(CYCLES):
-        start = base(i)
-        rows = band_rows(win, band.at[i % 2], coef, i, lambda d, k: (start + k, d))
-        for k in range(BASIS):
-            spread[i * LON : (i + 1) * LON, k * EMBED : (k + 1) * EMBED] = rows[
-                k * LON : (k + 1) * LON, :
-            ].astype(bf16)
+        apply_band(bands.at[i * BASIS * LON : (i + 1) * BASIS * LON], win, i, spread)
 
     loads[0].wait()
     blended = (
@@ -173,8 +193,7 @@
         blended.astype(f32) + dot(hidden, weight_out[...], ((1,), (0,)))
     ).astype(bf16)
     slope = cdf + preact * jnp.exp(-0.5 * preact * preact) * gauss_norm
-    hidden_grad = dot(tangent[...], weight_out[...], ((1,), (1,)))
-    preact_grad = (hidden_grad * slope).astype(bf16)
+    preact_grad = (hidden_grad[...] * slope).astype(bf16)
     grad = (
         tangent[...].astype(f32) + dot(preact_grad, weight_in[...], ((1,), (1,)))
     ).astype(bf16)
@@ -203,17 +222,10 @@
         def _():
             store(theirs, theirs_mlp)
 
-    edges = []
-    for cycle in (0, 1, CYCLES - 2, CYCLES - 1):
-        start = base(cycle)
-        for k in range(BASIS):
-            edges.append(
-                jnp.concatenate([coef[d, pl.ds(start + k, 1), :] for d in range(SPAN)], axis=1)
-            )
     to_up[0:RIM, :] = grad[CELLS - RIM :, :]
-    to_up[RIM : RIM + 8, :] = jnp.concatenate(edges[8:], axis=0).astype(bf16)
+    to_up[RIM:, :] = edge_up[...]
     to_down[0:RIM, :] = grad[:RIM, :]
-    to_down[RIM : RIM + 8, :] = jnp.concatenate(edges[:8], axis=0).astype(bf16)
+    to_down[RIM:, :] = edge_down[...]
 
 
 def mlp_grad_kernel(place, mine, other, tangent, other_tangent, order, o0, o1, o2, o3, acc):
@@ -296,10 +308,7 @@
     load.start()
     fill_window(win, tile, left, right, top, bottom, left_side, right_side, lat)
     rows = jnp.concatenate(
-        [
-            left_e[2 * RIM :, :], own_e[...], right_e[2 * RIM :, :], far_e[...],
-            top[RIM:, :], bottom[RIM:, :],
-        ],
+        [left_e[...], own_e[...], right_e[...], far_e[...], top[RIM:, :], bottom[RIM:, :]],
         axis=0,
     )
     lane = lax.broadcasted_iota(jnp.int32, (2 * NLON, 2 * NLON), 0)
@@ -313,17 +322,12 @@
             return 64 + (cycle + HALO) * BASIS
         if cycle >= CYCLES:
             return 72 + (cycle - CYCLES) * BASIS
-        return lax.rem(cycle // OWNED - lon + 1 + 4, 4) * 16 + (cycle % OWNED) * BASIS
+        return first_row(cycle, lon)
 
     for j in range(CYCLES):
         starts = [base(j + e - HALO) for e in range(SPAN)]
-        rows = band_rows(
-            win, band.at[j % 2], coef, j, lambda e, k: (starts[e] + k, SPAN - 1 - e)
-        )
-        for k in range(BASIS):
-            mixed[j * LON : (j + 1) * LON, k * EMBED : (k + 1) * EMBED] = rows[
-                k * LON : (k + 1) * LON, :
-            ].astype(bf16)
+        fill_band(band.at[j % 2], coef, lambda e, k: (starts[e] + k, SPAN - 1 - e))
+        apply_band(band.at[j % 2], win, j, mixed)
     total = tile[...].astype(f32)
     load.wait()
     for k in range(BASIS):
@@ -361,11 +365,10 @@
     return left, right, top, bottom
 
 
-def relay(place, left, right, top, bottom, *extra):
-    rows = 2 * RIM + sum(e.shape[0] for e in extra)
+def relay(place, left, right, top, bottom):
     to_right, to_left = call(
-        side_kernel, (struct((rows, EMBED), bf16),) * 2, [], 4, place,
-        left, right, top, bottom, *extra,
+        side_kernel, (struct((2 * RIM, EMBED), bf16),) * 2, [], 4, place,
+        left, right, top, bottom,
     )
     left_side = shift(to_right, "zlo", 4, 1)
     right_side = shift(to_left, "zlo", 4, 3)
@@ -400,8 +403,10 @@
 
     left, right, top, bottom = neighbours(tile, tile[CELLS - RIM :], tile[:RIM])
     own_e = coefficients(filter_basis, lon_offsets)
+    left_e = shift(own_e, "zlo", 4, 1)
+    right_e = shift(own_e, "zlo", 4, 3)
     far_e = shift(own_e, "zlo", 4, 2)
-    left_side, right_side = relay(place, left, right, top, bottom, own_e)
+    left_side, right_side = relay(place, left, right, top, bottom)
     other_tangent = shift(tangent, "core", 2, 1)
 
     unit = jnp.arange(EMBED, dtype=jnp.int32)
@@ -409,29 +414,37 @@
     source = uy * 160 + ul * 40 + ux * 10 + ur
     order = (unit[:, None] == source[None, :]).astype(bf16)
 
-    far_e, other_tangent, order = lax.optimization_barrier((far_e, other_tangent, order))
     window = pltpu.VMEM(((CYCLES + 2 * HALO) * NLON, EMBED), bf16)
-    band = pltpu.VMEM((2, BASIS * LON, 384), bf16)
-    edge = struct((RIM + 8, EMBED), bf16)
+    edge = struct((8, EMBED), bf16)
+    bands, hidden_grad, edge_down, edge_up = call(
+        band_kernel,
+        (struct((CELLS * BASIS, 384), bf16), struct((CELLS, HIDDEN), f32), edge, edge),
+        [
+            pltpu.VMEM((SPAN, 64, 2 * NLON), f32),
+            pltpu.VMEM((HIDDEN, EMBED), bf16),
+            pltpu.SemaphoreType.DMA,
+        ],
+        12, place, left_e, own_e, right_e, far_e, tangent, in_hbm=(weight_out,),
+    )
+    bands, other_tangent, order = lax.optimization_barrier((bands, other_tangent, order))
+    edge_rows = struct((RIM + 8, EMBED), bf16)
     parts = (struct((CELLS, CONV_PART), bf16), struct((CELLS, MLP_PART), bf16))
     block_out, blend_grad, mine, mine_mlp, theirs, theirs_mlp, to_up, to_down = call(
         forward_kernel,
         (struct((CELLS, EMBED), bf16), struct((CELLS, EMBED), bf16))
         + parts
         + parts
-        + (edge, edge),
+        + (edge_rows, edge_rows),
         [
             window,
-            band,
-            pltpu.VMEM((SPAN, 64, 2 * NLON), f32),
             pltpu.VMEM((CELLS, WIDE), bf16),
             pltpu.VMEM((WIDE, EMBED), bf16),
             pltpu.VMEM((EMBED, HIDDEN), bf16),
             pltpu.VMEM((HIDDEN, EMBED), bf16),
             pltpu.SemaphoreType.DMA((3,)),
         ],
-        24, place, tile, left, right, top, bottom, left_side, right_side, far_e, own_e,
-        tangent, in_hbm=(conv_weight, weight_in, weight_out),
+        24, place, tile, left, right, top, bottom, left_side, right_side, bands,
+        hidden_grad, edge_down, edge_up, tangent, in_hbm=(conv_weight, weight_in, weight_out),
     )
     other = shift(theirs, "core", 2, 1)
     other_mlp = shift(theirs_mlp, "core", 2, 1)
@@ -458,14 +471,14 @@
         struct((CELLS, EMBED), bf16),
         [
             window,
-            band,
+            pltpu.VMEM((2, BASIS * LON, 384), bf16),
             pltpu.VMEM((SPAN, 80, 2 * NLON), f32),
             pltpu.VMEM((CELLS, WIDE), bf16),
             pltpu.VMEM((WIDE, EMBED), bf16),
             pltpu.SemaphoreType.DMA,
         ],
         16, place, blend_grad, g_left, g_right, g_top, g_bottom, g_left_side, g_right_side,
-        own_e, left_side, right_side, far_e, in_hbm=(conv_weight,),
+        own_e, left_e, right_e, far_e, in_hbm=(conv_weight,),
     )
     m0, field_grad = lax.optimization_barrier((m[0], field_grad))
     packed = call(pack_kernel, struct((8, 20, EMBED), bf16), [], 4, None, m0, *m[1:], *c)

time: 108 us -> 110 us (1.019)
  Pallas kernels: 20.6 us -> 22.8 us
  starting transfers between devices: 46.7 us -> 48.9 us
  waiting for transfers between devices: 20.5 us -> 19.1 us
    ppermute x24 -> x26, waiting for transfers between devices: 18.8 us -> 15.9 us  [shift(): lax.ppermute(block, axis, [(i, (i + step) % count) for i in range(count)])]
    ppermute x24 -> x26, starting transfers between devices: 35.8 us -> 38.1 us  [shift(): lax.ppermute(block, axis, [(i, (i + step) % count) for i in range(count)])]
    pallas_call x10 -> x11, Pallas kernels: 20.6 us -> 22.8 us  [call(): pl.pallas_call(kernel, out_shape=outs, in_specs=in_specs, scratch_shapes=...]
    ppermute x2, waiting for transfers between devices: 1.75 us -> 3.17 us  [neighbours(): bottom = lax.ppermute(to_down, LAT, backward)]
  transfers between devices with their start and end apart: 28 -> 30, of which waited for: 8 -> 8; matrix products, arithmetic and copies ran while one was open for 3% -> 3% of each run, Pallas kernels for 12% -> 14%
where the time goes in v2:
time: 110 us; the launch traced here: 109 us
  starting transfers between devices  48.9 us (44%)
  Pallas kernels  22.8 us (21%)
  waiting for transfers between devices  19.1 us (17%)
  blocking collectives  13.9 us (13%)
  other arithmetic  2.04 us (2%)
    ppermute x26, starting transfers between devices, shift(): lax.ppermute(block, axis, [(i, (i + step) % count) for i in range(count)])  38.1 us
    pallas_call x11, Pallas kernels, call(): pl.pallas_call(kernel, out_shape=outs, in_specs=in_specs, scratch_shapes=...  22.8 us
    ppermute x26, waiting for transfers between devices, shift(): lax.ppermute(block, axis, [(i, (i + step) % count) for i in range(count)])  15.9 us
    all_to_all x1, blocking collectives, block(): lax.all_to_all(packed, ('zlo', 'zhi'), split_axis=0, concat_axis=0, tiled...  13.9 us
    ppermute x2, starting transfers between devices, neighbours(): bottom = lax.ppermute(to_down, LAT, backward)  6.95 us
    ppermute x2, starting transfers between devices, neighbours(): top = lax.ppermute(to_up, LAT, forward)  3.82 us
    ppermute x2, waiting for transfers between devices, neighbours(): bottom = lax.ppermute(to_down, LAT, backward)  3.17 us
  transfers between devices with their start and end apart: 30, of which 8 were waited for; matrix products, arithmetic and copies ran while one was open for 3% of the time, Pallas kernels for 14%

profile of v2, /device:TPU:8, one launch (start us, length us, event | category | flops | bytes accessed | tf_op | source)
XLA Modules:
  0.0 108.6 jit_solution(1402640401831871379)
XLA Ops:
  0.6 4.7 %collective-permute-start.1 = (bf16[192,640]{1,0:T(8,128)(2,1)}, bf16[192,640]{1,0:T(8,128)(2,1)S(1)}, u32[]{:S(2)}, u32[]{:S(2)}) collective-permute-start(bf16[192,640]{1,0:T(8,128)(2,1)} %bitcast.22), channel_id=1, source_target_pairs={{0,24},{8,0},{16,8},{24,16},{1,25},{9,1},{17,9},{25,17},{2,26},{10... | collective-permute-start | bytes 737288 | tf_op jit(solution)/shard_map/ppermute | solution.py:43
  5.4 0.7 add_select_fusion
  6.1 0.7 convert_bitcast_fusion
  7.2 0.8 collective-permute-start.8
  8.0 0.8 fusion.21
  8.8 1.9 %collective-permute-start.2 = (bf16[32,640]{1,0:T(8,128)(2,1)S(1)}, bf16[32,640]{1,0:T(8,128)(2,1)S(1)}, u32[]{:S(2)}, u32[]{:S(2)}) collective-permute-start(bf16[32,640]{1,0:T(8,128)(2,1)S(1)} %bitcast.30), channel_id=1, source_target_pairs={{0,32},{32,64},{64,96},{96,128},{128,160},{160,192},{192,224},{1,3... | collective-permute-start | bytes 122888 | tf_op jit(solution)/shard_map/ppermute | solution.py:363
  10.7 3.6 %collective-permute-start.3 = (bf16[32,640]{1,0:T(8,128)(2,1)S(1)}, bf16[32,640]{1,0:T(8,128)(2,1)S(1)}, u32[]{:S(2)}, u32[]{:S(2)}) collective-permute-start(bf16[32,640]{1,0:T(8,128)(2,1)S(1)} %bitcast.29), channel_id=1, source_target_pairs={{32,0},{64,32},{96,64},{128,96},{160,128},{192,160},{224,192},{33,... | collective-permute-start | bytes 122888 | tf_op jit(solution)/shard_map/ppermute | solution.py:364
  14.6 1.4 %collective-permute-done.3.bottom = bf16[32,640]{1,0:T(8,128)(2,1)S(1)} collective-permute-done((bf16[32,640]{1,0:T(8,128)(2,1)S(1)}, bf16[32,640]{1,0:T(8,128)(2,1)S(1)}, u32[]{:S(2)}, u32[]{:S(2)}) %collective-permute-start.3) | collective-permute-done | bytes 40992 | tf_op jit(solution)/shard_map/ppermute | solution.py:364
  16.0 3.2 %collective-permute-start.7 = (bf16[16,640]{1,0:T(8,128)(2,1)S(1)}, bf16[16,640]{1,0:T(8,128)(2,1)S(1)}, u32[]{:S(2)}, u32[]{:S(2)}) collective-permute-start(bf16[16,640]{1,0:T(8,128)(2,1)S(1)} %pad.4.own_e), channel_id=1, source_target_pairs={{0,24},{8,0},{16,8},{24,16},{1,25},{9,1},{17,9},{25,17},{2,26},{10... | collective-permute-start | bytes 61448 | tf_op jit(solution)/shard_map/ppermute | solution.py:43
  19.1 0.6 collective-permute-start.6
  19.7 0.6 shard_map.110
  20.3 2.1 %collective-permute-start.4 = (bf16[64,640]{1,0:T(8,128)(2,1)S(1)}, bf16[64,640]{1,0:T(8,128)(2,1)S(1)}, u32[]{:S(2)}, u32[]{:S(2)}) collective-permute-start(bf16[64,640]{1,0:T(8,128)(2,1)S(1)} %get-tuple-element.45), channel_id=1, source_target_pairs={{0,8},{8,16},{16,24},{24,0},{1,9},{9,17},{17,25},{25,1},{2,10},{10... | collective-permute-start | bytes 245768 | tf_op jit(solution)/shard_map/ppermute | solution.py:43
  22.4 1.8 %collective-permute-start.5 = (bf16[64,640]{1,0:T(8,128)(2,1)S(1)}, bf16[64,640]{1,0:T(8,128)(2,1)S(1)}, u32[]{:S(2)}, u32[]{:S(2)}) collective-permute-start(bf16[64,640]{1,0:T(8,128)(2,1)S(1)} %get-tuple-element.46), channel_id=1, source_target_pairs={{0,24},{8,0},{16,8},{24,16},{1,25},{9,1},{17,9},{25,17},{2,26},{10... | collective-permute-start | bytes 245768 | tf_op jit(solution)/shard_map/ppermute | solution.py:43
  24.2 0.2 fusion.order
  24.4 0.3 collective-permute-done.6.left_e
  24.7 2.7 %shard_map.111 = (bf16[768,384]{1,0:T(8,128)(2,1)S(1)}, f32[192,1280]{1,0:T(8,128)S(1)}, bf16[8,640]{1,0:T(8,128)(2,1)S(1)}, bf16[8,640]{1,0:T(8,128)(2,1)S(1)}) custom-call(s32[5]{0:T(128)S(1)} %stack.23.place, bf16[16,640]{1,0:T(8,128)(2,1)S(1)} %collective-permute-done.6.left_e, bf16[16,640]{1,0:T(8,128)(2,1)S(1)} %pad.4.own_e, ...), custom_call_target="tpu_custom_call" | custom-call | tf_op jit(solution)/shard_map/pallas_call | solution.py:349
  27.5 1.8 %collective-permute-done.5.right_side = bf16[64,640]{1,0:T(8,128)(2,1)S(1)} collective-permute-done((bf16[64,640]{1,0:T(8,128)(2,1)S(1)}, bf16[64,640]{1,0:T(8,128)(2,1)S(1)}, u32[]{:S(2)}, u32[]{:S(2)}) %collective-permute-start.5) | collective-permute-done | bytes 81952 | tf_op jit(solution)/shard_map/ppermute | solution.py:43
  29.2 6.7 %shard_map.112 = (bf16[192,640]{1,0:T(8,128)(2,1)}, bf16[192,640]{1,0:T(8,128)(2,1)S(1)}, bf16[192,2176]{1,0:T(8,128)(2,1)S(1)}, bf16[192,1920]{1,0:T(8,128)(2,1...) custom-call(s32[5]{0:T(128)S(1)} %stack.23.place, ...), custom_call_target="tpu_custom_call" | custom-call | tf_op jit(solution)/shard_map/pallas_call | solution.py:349
  35.9 0.4 collective-permute-start.10
  36.3 0.4 collective-permute-start.23
  36.7 1.7 %collective-permute-done.10.other = bf16[192,1920]{1,0:T(8,128)(2,1)S(1)} collective-permute-done((bf16[192,1920]{1,0:T(8,128)(2,1)S(1)}, bf16[192,1920]{1,0:T(8,128)(2,1)S(1)}, u32[]{:S(2)}, u32[]{:S(2)}) %collective-permute-start.10) | collective-permute-done | bytes 737312 | tf_op jit(solution)/shard_map/ppermute | solution.py:43
  38.4 3.2 %shard_map.113 = (f32[320,640]{1,0:T(8,128)S(1)}, bf16[320,640]{1,0:T(8,128)(2,1)S(1)}, bf16[320,640]{1,0:T(8,128)(2,1)S(1)}, bf16[320,640]{1,0:T(8,128)(2,1)S(1)}) custom-call(s32[5]{0:T(128)S(1)} %stack.23.place, bf16[192,1920]{1,0:T(8,128)(2,1)S(1)} %get-tuple-element.53.mine, bf16[192,1920]{1,0:T(8,128)(2,1)S(1)} %collective-permute-done.10.other, ...), custom_call_target="tpu_custom_call" | custom-call | tf_op jit(solution)/shard_map/pallas_call | solution.py:349
  41.6 1.6 %collective-permute-start.11 = (bf16[320,640]{1,0:T(8,128)(2,1)S(1)}, bf16[320,640]{1,0:T(8,128)(2,1)S(1)}, u32[]{:S(2)}, u32[]{:S(2)}) collective-permute-start(bf16[320,640]{1,0:T(8,128)(2,1)S(1)} %get-tuple-element.58), channel_id=1, source_target_pairs={{0,2},{2,4},{4,6},{6,0},{1,3},{3,5},{5,7},{7,1},{8,10},{10,12},{12... | collective-permute-start | bytes 1228808 | tf_op jit(solution)/shard_map/ppermute | solution.py:43
  43.1 2.7 %collective-permute-start.12 = (bf16[320,640]{1,0:T(8,128)(2,1)S(1)}, bf16[320,640]{1,0:T(8,128)(2,1)S(1)}, u32[]{:S(2)}, u32[]{:S(2)}) collective-permute-start(bf16[320,640]{1,0:T(8,128)(2,1)S(1)} %get-tuple-element.59), channel_id=1, source_target_pairs={{0,4},{2,6},{4,0},{6,2},{1,5},{3,7},{5,1},{7,3},{8,12},{10,14},{12... | collective-permute-start | bytes 1228808 | tf_op jit(solution)/shard_map/ppermute | solution.py:43
  45.9 1.4 %collective-permute-start.13 = (bf16[320,640]{1,0:T(8,128)(2,1)S(1)}, bf16[320,640]{1,0:T(8,128)(2,1)S(1)}, u32[]{:S(2)}, u32[]{:S(2)}) collective-permute-start(bf16[320,640]{1,0:T(8,128)(2,1)S(1)} %get-tuple-element.60), channel_id=1, source_target_pairs={{0,6},{2,0},{4,2},{6,4},{1,7},{3,1},{5,3},{7,5},{8,14},{10,8},{12,... | collective-permute-start | bytes 1228808 | tf_op jit(solution)/shard_map/ppermute | solution.py:43
  47.3 1.9 %collective-permute-start.16 = (bf16[40,640]{1,0:T(8,128)(2,1)S(1)}, bf16[40,640]{1,0:T(8,128)(2,1)S(1)}, u32[]{:S(2)}, u32[]{:S(2)}) collective-permute-start(bf16[40,640]{1,0:T(8,128)(2,1)S(1)} %get-tuple-element.63), channel_id=1, source_target_pairs={{0,32},{32,64},{64,96},{96,128},{128,160},{160,192},{192,224},{1,3... | collective-permute-start | bytes 153608 | tf_op jit(solution)/shard_map/ppermute | solution.py:363
  49.2 2.0 %shard_map.117 = (f32[320,640]{1,0:T(8,128)S(1)}, bf16[320,640]{1,0:T(8,128)(2,1)S(1)}, bf16[320,640]{1,0:T(8,128)(2,1)S(1)}, bf16[320,640]{1,0:T(8,128)(2,1)S(1)}) custom-call(s32[5]{0:T(128)S(1)} %stack.23.place, bf16[192,2176]{1,0:T(8,128)(2,1)S(1)} %get-tuple-element.72.mine, bf16[192,2176]{1,0:T(8,128)(2,1)S(1)} %collective-permute-done.23.other), custom_call_target="tpu_custom_call" | custom-call | tf_op jit(solution)/shard_map/pallas_call | solution.py:349
  51.2 1.5 %collective-permute-start.24 = (bf16[320,640]{1,0:T(8,128)(2,1)S(1)}, bf16[320,640]{1,0:T(8,128)(2,1)S(1)}, u32[]{:S(2)}, u32[]{:S(2)}) collective-permute-start(bf16[320,640]{1,0:T(8,128)(2,1)S(1)} %get-tuple-element.75), channel_id=1, source_target_pairs={{0,64},{64,128},{128,192},{192,0},{1,65},{65,129},{129,193},{193,1... | collective-permute-start | bytes 1228808 | tf_op jit(solution)/shard_map/ppermute | solution.py:43
  52.7 3.3 %collective-permute-start.17 = (bf16[40,640]{1,0:T(8,128)(2,1)S(1)}, bf16[40,640]{1,0:T(8,128)(2,1)S(1)}, u32[]{:S(2)}, u32[]{:S(2)}) collective-permute-start(bf16[40,640]{1,0:T(8,128)(2,1)S(1)} %get-tuple-element.64), channel_id=1, source_target_pairs={{32,0},{64,32},{96,64},{128,96},{160,128},{192,160},{224,192},{33,... | collective-permute-start | bytes 153608 | tf_op jit(solution)/shard_map/ppermute | solution.py:364
  56.0 1.7 %collective-permute-done.17.bottom = bf16[40,640]{1,0:T(8,128)(2,1)S(1)} collective-permute-done((bf16[40,640]{1,0:T(8,128)(2,1)S(1)}, bf16[40,640]{1,0:T(8,128)(2,1)S(1)}, u32[]{:S(2)}, u32[]{:S(2)}) %collective-permute-start.17) | collective-permute-done | bytes 51232 | tf_op jit(solution)/shard_map/ppermute | solution.py:364
  57.8 2.4 %collective-permute-start.26 = (bf16[320,640]{1,0:T(8,128)(2,1)S(1)}, bf16[320,640]{1,0:T(8,128)(2,1)S(1)}, u32[]{:S(2)}, u32[]{:S(2)}) collective-permute-start(bf16[320,640]{1,0:T(8,128)(2,1)S(1)} %get-tuple-element.77), channel_id=1, source_target_pairs={{0,192},{64,0},{128,64},{192,128},{1,193},{65,1},{129,65},{193,129... | collective-permute-start | bytes 1228808 | tf_op jit(solution)/shard_map/ppermute | solution.py:43
  60.2 3.9 %collective-permute-done.12.r2 = bf16[320,640]{1,0:T(8,128)(2,1)S(1)} collective-permute-done((bf16[320,640]{1,0:T(8,128)(2,1)S(1)}, bf16[320,640]{1,0:T(8,128)(2,1)S(1)}, u32[]{:S(2)}, u32[]{:S(2)}) %collective-permute-start.12) | collective-permute-done | bytes 409632 | tf_op jit(solution)/shard_map/ppermute | solution.py:43
  64.1 1.9 %collective-permute-start.15 = (bf16[192,640]{1,0:T(8,128)(2,1)S(1)}, bf16[192,640]{1,0:T(8,128)(2,1)S(1)}, u32[]{:S(2)}, u32[]{:S(2)}) collective-permute-start(bf16[192,640]{1,0:T(8,128)(2,1)S(1)} %get-tuple-element.62.tile), channel_id=1, source_target_pairs={{0,24},{8,0},{16,8},{24,16},{1,25},{9,1},{17,9},{25,17},{2,26},{10... | collective-permute-start | bytes 737288 | tf_op jit(solution)/shard_map/ppermute | solution.py:43
  66.2 0.9 shard_map.114
  67.1 5.4 %collective-permute-done.15.right = bf16[192,640]{1,0:T(8,128)(2,1)S(1)} collective-permute-done((bf16[192,640]{1,0:T(8,128)(2,1)S(1)}, bf16[192,640]{1,0:T(8,128)(2,1)S(1)}, u32[]{:S(2)}, u32[]{:S(2)}) %collective-permute-start.15) | collective-permute-done | bytes 245792 | tf_op jit(solution)/shard_map/ppermute | solution.py:43
  72.5 1.5 %collective-permute-start.20 = (bf16[80,640]{1,0:T(8,128)(2,1)S(1)}, bf16[80,640]{1,0:T(8,128)(2,1)S(1)}, u32[]{:S(2)}, u32[]{:S(2)}) collective-permute-start(bf16[80,640]{1,0:T(8,128)(2,1)S(1)} %get-tuple-element.69), channel_id=1, source_target_pairs={{0,64},{64,128},{128,192},{192,0},{1,65},{65,129},{129,193},{193,1... | collective-permute-start | bytes 307208 | tf_op jit(solution)/shard_map/ppermute | solution.py:43
  74.0 2.7 %collective-permute-done.14.left = bf16[192,640]{1,0:T(8,128)(2,1)S(1)} collective-permute-done((bf16[192,640]{1,0:T(8,128)(2,1)S(1)}, bf16[192,640]{1,0:T(8,128)(2,1)S(1)}, u32[]{:S(2)}, u32[]{:S(2)}) %collective-permute-start.14) | collective-permute-done | bytes 245792 | tf_op jit(solution)/shard_map/ppermute | solution.py:43
  76.7 0.6 shard_map.115
  77.3 1.9 %collective-permute-start.18 = (bf16[64,640]{1,0:T(8,128)(2,1)S(1)}, bf16[64,640]{1,0:T(8,128)(2,1)S(1)}, u32[]{:S(2)}, u32[]{:S(2)}) collective-permute-start(bf16[64,640]{1,0:T(8,128)(2,1)S(1)} %get-tuple-element.65), channel_id=1, source_target_pairs={{0,8},{8,16},{16,24},{24,0},{1,9},{9,17},{17,25},{25,1},{2,10},{10... | collective-permute-start | bytes 245768 | tf_op jit(solution)/shard_map/ppermute | solution.py:43
  79.1 2.0 %collective-permute-start.19 = (bf16[64,640]{1,0:T(8,128)(2,1)S(1)}, bf16[64,640]{1,0:T(8,128)(2,1)S(1)}, u32[]{:S(2)}, u32[]{:S(2)}) collective-permute-start(bf16[64,640]{1,0:T(8,128)(2,1)S(1)} %get-tuple-element.66), channel_id=1, source_target_pairs={{0,24},{8,0},{16,8},{24,16},{1,25},{9,1},{17,9},{25,17},{2,26},{10... | collective-permute-start | bytes 245768 | tf_op jit(solution)/shard_map/ppermute | solution.py:43
  81.2 1.6 %collective-permute-start.21 = (bf16[80,640]{1,0:T(8,128)(2,1)S(1)}, bf16[80,640]{1,0:T(8,128)(2,1)S(1)}, u32[]{:S(2)}, u32[]{:S(2)}) collective-permute-start(bf16[80,640]{1,0:T(8,128)(2,1)S(1)} %get-tuple-element.70), channel_id=1, source_target_pairs={{0,128},{64,192},{128,0},{192,64},{1,129},{65,193},{129,1},{193,65... | collective-permute-start | bytes 307208 | tf_op jit(solution)/shard_map/ppermute | solution.py:43
  82.8 2.1 %collective-permute-start.22 = (bf16[80,640]{1,0:T(8,128)(2,1)S(1)}, bf16[80,640]{1,0:T(8,128)(2,1)S(1)}, u32[]{:S(2)}, u32[]{:S(2)}) collective-permute-start(bf16[80,640]{1,0:T(8,128)(2,1)S(1)} %get-tuple-element.71), channel_id=1, source_target_pairs={{0,192},{64,0},{128,64},{192,128},{1,193},{65,1},{129,65},{193,129... | collective-permute-start | bytes 307208 | tf_op jit(solution)/shard_map/ppermute | solution.py:43
  84.9 1.0 shard_map.118
  86.0 0.9 collective-permute-start.28
  86.8 2.5 %collective-permute-start.29 = (bf16[80,640]{1,0:T(8,128)(2,1)S(1)}, bf16[80,640]{1,0:T(8,128)(2,1)S(1)}, u32[]{:S(2)}, u32[]{:S(2)}) collective-permute-start(bf16[80,640]{1,0:T(8,128)(2,1)S(1)} %get-tuple-element.81), channel_id=1, source_target_pairs={{0,6},{2,0},{4,2},{6,4},{1,7},{3,1},{5,3},{7,5},{8,14},{10,8},{12,... | collective-permute-start | bytes 307208 | tf_op jit(solution)/shard_map/ppermute | solution.py:43
  89.3 4.5 %shard_map.116 = bf16[192,640]{1,0:T(8,128)(2,1)} custom-call(s32[5]{0:T(128)S(1)} %stack.23.place, bf16[192,640]{1,0:T(8,128)(2,1)S(1)} %get-tuple-element.62.tile, bf16[192,640]{1,0:T(8,128)(2,1)S(1)} %collective-permute-done.14.left, bf16[192,640]{1,0:T(8,128)(2,1)S(1)} %collective-permute-done.15.right, bf16[40,640]{1,0:T(8,128)(2,1)S(1)} %collective-permute-done.16.top, ...), custom_call_target="tpu_custom_call" | custom-call | tf_op jit(solution)/shard_map/pallas_call | solution.py:349
  94.1 13.9 %all_to_all.5.parts = bf16[8,20,640]{2,1,0:T(8,128)(2,1)S(1)} all-to-all(bf16[8,20,640]{2,1,0:T(8,128)(2,1)S(1)} %shard_map.119), channel_id=1, replica_groups=mesh['y'=4,'core'=2,'zlo'=4,'x'=4,'zhi'=2] {'zlo','zhi'}, dimensions={0} | all-to-all | bytes 409600 | tf_op jit(solution)/shard_map/all_to_all | solution.py:485
  108.0 0.6 shard_map.120
  (42 shorter events, 1.1 us)
Async XLA Ops:
  0.6 24.1 %copy-start = (bf16[1,12,16,640]{3,2,1,0:T(8,128)(2,1)S(1)}, bf16[1,12,16,640]{3,2,1,0:T(8,128)(2,1)}, u32[]{:S(2)}) copy-start(bf16[1,12,16,640]{3,2,1,0:T(8,128)(2,1)} %param.13) | copy-start | bytes 737284
  0.6 18.5 %collective-permute-start.1 = (bf16[192,640]{1,0:T(8,128)(2,1)}, bf16[192,640]{1,0:T(8,128)(2,1)S(1)}, u32[]{:S(2)}, u32[]{:S(2)}) collective-permute-start(bf16[192,640]{1,0:T(8,128)(2,1)} %bitcast.22), channel_id=1, source_target_pairs={{0,24},{8,0},{16,8},{24,16},{1,25},{9,1},{17,9},{25,17},{2,26},{10... | collective-permute-start | bytes 737288 | tf_op jit(solution)/shard_map/ppermute | solution.py:43
  5.3 14.4 %collective-permute-start = (bf16[192,640]{1,0:T(8,128)(2,1)}, bf16[192,640]{1,0:T(8,128)(2,1)S(1)}, u32[]{:S(2)}, u32[]{:S(2)}) collective-permute-start(bf16[192,640]{1,0:T(8,128)(2,1)} %bitcast.23), channel_id=1, source_target_pairs={{0,8},{8,16},{16,24},{24,0},{1,9},{9,17},{17,25},{25,1},{2,10},{10... | collective-permute-start | bytes 737288 | tf_op jit(solution)/shard_map/ppermute | solution.py:43
  7.2 15.2 %collective-permute-start.8 = (bf16[16,640]{1,0:T(8,128)(2,1)S(1)}, bf16[16,640]{1,0:T(8,128)(2,1)S(1)}, u32[]{:S(2)}, u32[]{:S(2)}) collective-permute-start(bf16[16,640]{1,0:T(8,128)(2,1)S(1)} %pad.4.own_e), channel_id=1, source_target_pairs={{0,16},{8,24},{16,0},{24,8},{1,17},{9,25},{17,1},{25,9},{2,18},{10... | collective-permute-start | bytes 61448 | tf_op jit(solution)/shard_map/ppermute | solution.py:43
  8.8 5.6 %collective-permute-start.2 = (bf16[32,640]{1,0:T(8,128)(2,1)S(1)}, bf16[32,640]{1,0:T(8,128)(2,1)S(1)}, u32[]{:S(2)}, u32[]{:S(2)}) collective-permute-start(bf16[32,640]{1,0:T(8,128)(2,1)S(1)} %bitcast.30), channel_id=1, source_target_pairs={{0,32},{32,64},{64,96},{96,128},{128,160},{160,192},{192,224},{1,3... | collective-permute-start | bytes 122888 | tf_op jit(solution)/shard_map/ppermute | solution.py:363
  10.7 5.3 %collective-permute-start.3 = (bf16[32,640]{1,0:T(8,128)(2,1)S(1)}, bf16[32,640]{1,0:T(8,128)(2,1)S(1)}, u32[]{:S(2)}, u32[]{:S(2)}) collective-permute-start(bf16[32,640]{1,0:T(8,128)(2,1)S(1)} %bitcast.29), channel_id=1, source_target_pairs={{32,0},{64,32},{96,64},{128,96},{160,128},{192,160},{224,192},{33,... | collective-permute-start | bytes 122888 | tf_op jit(solution)/shard_map/ppermute | solution.py:364
  14.4 13.1 %collective-permute-start.9 = (bf16[192,640]{1,0:T(8,128)(2,1)}, bf16[192,640]{1,0:T(8,128)(2,1)S(1)}, u32[]{:S(2)}, u32[]{:S(2)}) collective-permute-start(bf16[192,640]{1,0:T(8,128)(2,1)} %bitcast.18), channel_id=1, source_target_pairs={{0,32},{32,0},{1,33},{33,1},{2,34},{34,2},{3,35},{35,3},{4,36},{36... | collective-permute-start | bytes 737288 | tf_op jit(solution)/shard_map/ppermute | solution.py:43
  14.6 14.7 %copy-start.1 = (bf16[1,12,16,640]{3,2,1,0:T(8,128)(2,1)S(1)}, bf16[1,12,16,640]{3,2,1,0:T(8,128)(2,1)}, u32[]{:S(2)}) copy-start(bf16[1,12,16,640]{3,2,1,0:T(8,128)(2,1)} %param.7) | copy-start | bytes 737284
  16.0 8.5 %collective-permute-start.7 = (bf16[16,640]{1,0:T(8,128)(2,1)S(1)}, bf16[16,640]{1,0:T(8,128)(2,1)S(1)}, u32[]{:S(2)}, u32[]{:S(2)}) collective-permute-start(bf16[16,640]{1,0:T(8,128)(2,1)S(1)} %pad.4.own_e), channel_id=1, source_target_pairs={{0,24},{8,0},{16,8},{24,16},{1,25},{9,1},{17,9},{25,17},{2,26},{10... | collective-permute-start | bytes 61448 | tf_op jit(solution)/shard_map/ppermute | solution.py:43
  19.1 5.6 %collective-permute-start.6 = (bf16[16,640]{1,0:T(8,128)(2,1)S(1)}, bf16[16,640]{1,0:T(8,128)(2,1)S(1)}, u32[]{:S(2)}, u32[]{:S(2)}) collective-permute-start(bf16[16,640]{1,0:T(8,128)(2,1)S(1)} %pad.4.own_e), channel_id=1, source_target_pairs={{0,8},{8,16},{16,24},{24,0},{1,9},{9,17},{17,25},{25,1},{2,10},{10... | collective-permute-start | bytes 61448 | tf_op jit(solution)/shard_map/ppermute | solution.py:43
  20.3 7.2 %collective-permute-start.4 = (bf16[64,640]{1,0:T(8,128)(2,1)S(1)}, bf16[64,640]{1,0:T(8,128)(2,1)S(1)}, u32[]{:S(2)}, u32[]{:S(2)}) collective-permute-start(bf16[64,640]{1,0:T(8,128)(2,1)S(1)} %get-tuple-element.45), channel_id=1, source_target_pairs={{0,8},{8,16},{16,24},{24,0},{1,9},{9,17},{17,25},{25,1},{2,10},{10... | collective-permute-start | bytes 245768 | tf_op jit(solution)/shard_map/ppermute | solution.py:43
  22.4 6.9 %collective-permute-start.5 = (bf16[64,640]{1,0:T(8,128)(2,1)S(1)}, bf16[64,640]{1,0:T(8,128)(2,1)S(1)}, u32[]{:S(2)}, u32[]{:S(2)}) collective-permute-start(bf16[64,640]{1,0:T(8,128)(2,1)S(1)} %get-tuple-element.46), channel_id=1, source_target_pairs={{0,24},{8,0},{16,8},{24,16},{1,25},{9,1},{17,9},{25,17},{2,26},{10... | collective-permute-start | bytes 245768 | tf_op jit(solution)/shard_map/ppermute | solution.py:43
  35.9 2.5 %collective-permute-start.10 = (bf16[192,1920]{1,0:T(8,128)(2,1)S(1)}, bf16[192,1920]{1,0:T(8,128)(2,1)S(1)}, u32[]{:S(2)}, u32[]{:S(2)}) collective-permute-start(bf16[192,1920]{1,0:T(8,128)(2,1)S(1)} %get-tuple-element.54), channel_id=1, source_target_pairs={{0,32},{32,0},{1,33},{33,1},{2,34},{34,2},{3,35},{35,3},{4,36},{36... | collective-permute-start | bytes 2211848 | tf_op jit(solution)/shard_map/ppermute | solution.py:43
  36.3 13.0 %collective-permute-start.23 = (bf16[192,2176]{1,0:T(8,128)(2,1)S(1)}, bf16[192,2176]{1,0:T(8,128)(2,1)S(1)}, u32[]{:S(2)}, u32[]{:S(2)}) collective-permute-start(bf16[192,2176]{1,0:T(8,128)(2,1)S(1)} %get-tuple-element.73), channel_id=1, source_target_pairs={{0,32},{32,0},{1,33},{33,1},{2,34},{34,2},{3,35},{35,3},{4,36},{36... | collective-permute-start | bytes 2506760 | tf_op jit(solution)/shard_map/ppermute | solution.py:43
  41.6 16.2 %collective-permute-start.11 = (bf16[320,640]{1,0:T(8,128)(2,1)S(1)}, bf16[320,640]{1,0:T(8,128)(2,1)S(1)}, u32[]{:S(2)}, u32[]{:S(2)}) collective-permute-start(bf16[320,640]{1,0:T(8,128)(2,1)S(1)} %get-tuple-element.58), channel_id=1, source_target_pairs={{0,2},{2,4},{4,6},{6,0},{1,3},{3,5},{5,7},{7,1},{8,10},{10,12},{12... | collective-permute-start | bytes 1228808 | tf_op jit(solution)/shard_map/ppermute | solution.py:43
  43.1 21.0 %collective-permute-start.12 = (bf16[320,640]{1,0:T(8,128)(2,1)S(1)}, bf16[320,640]{1,0:T(8,128)(2,1)S(1)}, u32[]{:S(2)}, u32[]{:S(2)}) collective-permute-start(bf16[320,640]{1,0:T(8,128)(2,1)S(1)} %get-tuple-element.59), channel_id=1, source_target_pairs={{0,4},{2,6},{4,0},{6,2},{1,5},{3,7},{5,1},{7,3},{8,12},{10,14},{12... | collective-permute-start | bytes 1228808 | tf_op jit(solution)/shard_map/ppermute | solution.py:43
  45.9 20.2 %collective-permute-start.13 = (bf16[320,640]{1,0:T(8,128)(2,1)S(1)}, bf16[320,640]{1,0:T(8,128)(2,1)S(1)}, u32[]{:S(2)}, u32[]{:S(2)}) collective-permute-start(bf16[320,640]{1,0:T(8,128)(2,1)S(1)} %get-tuple-element.60), channel_id=1, source_target_pairs={{0,6},{2,0},{4,2},{6,4},{1,7},{3,1},{5,3},{7,5},{8,14},{10,8},{12,... | collective-permute-start | bytes 1228808 | tf_op jit(solution)/shard_map/ppermute | solution.py:43
  47.3 5.4 %collective-permute-start.16 = (bf16[40,640]{1,0:T(8,128)(2,1)S(1)}, bf16[40,640]{1,0:T(8,128)(2,1)S(1)}, u32[]{:S(2)}, u32[]{:S(2)}) collective-permute-start(bf16[40,640]{1,0:T(8,128)(2,1)S(1)} %get-tuple-element.63), channel_id=1, source_target_pairs={{0,32},{32,64},{64,96},{96,128},{128,160},{160,192},{192,224},{1,3... | collective-permute-start | bytes 153608 | tf_op jit(solution)/shard_map/ppermute | solution.py:363
  51.2 27.9 %collective-permute-start.24 = (bf16[320,640]{1,0:T(8,128)(2,1)S(1)}, bf16[320,640]{1,0:T(8,128)(2,1)S(1)}, u32[]{:S(2)}, u32[]{:S(2)}) collective-permute-start(bf16[320,640]{1,0:T(8,128)(2,1)S(1)} %get-tuple-element.75), channel_id=1, source_target_pairs={{0,64},{64,128},{128,192},{192,0},{1,65},{65,129},{129,193},{193,1... | collective-permute-start | bytes 1228808 | tf_op jit(solution)/shard_map/ppermute | solution.py:43
  52.7 5.1 %collective-permute-start.17 = (bf16[40,640]{1,0:T(8,128)(2,1)S(1)}, bf16[40,640]{1,0:T(8,128)(2,1)S(1)}, u32[]{:S(2)}, u32[]{:S(2)}) collective-permute-start(bf16[40,640]{1,0:T(8,128)(2,1)S(1)} %get-tuple-element.64), channel_id=1, source_target_pairs={{32,0},{64,32},{96,64},{128,96},{160,128},{192,160},{224,192},{33,... | collective-permute-start | bytes 153608 | tf_op jit(solution)/shard_map/ppermute | solution.py:364
  57.8 23.4 %collective-permute-start.25 = (bf16[320,640]{1,0:T(8,128)(2,1)S(1)}, bf16[320,640]{1,0:T(8,128)(2,1)S(1)}, u32[]{:S(2)}, u32[]{:S(2)}) collective-permute-start(bf16[320,640]{1,0:T(8,128)(2,1)S(1)} %get-tuple-element.76), channel_id=1, source_target_pairs={{0,128},{64,192},{128,0},{192,64},{1,129},{65,193},{129,1},{193,65... | collective-permute-start | bytes 1228808 | tf_op jit(solution)/shard_map/ppermute | solution.py:43
  57.8 24.9 %collective-permute-start.26 = (bf16[320,640]{1,0:T(8,128)(2,1)S(1)}, bf16[320,640]{1,0:T(8,128)(2,1)S(1)}, u32[]{:S(2)}, u32[]{:S(2)}) collective-permute-start(bf16[320,640]{1,0:T(8,128)(2,1)S(1)} %get-tuple-element.77), channel_id=1, source_target_pairs={{0,192},{64,0},{128,64},{192,128},{1,193},{65,1},{129,65},{193,129... | collective-permute-start | bytes 1228808 | tf_op jit(solution)/shard_map/ppermute | solution.py:43
  64.1 8.4 %collective-permute-start.15 = (bf16[192,640]{1,0:T(8,128)(2,1)S(1)}, bf16[192,640]{1,0:T(8,128)(2,1)S(1)}, u32[]{:S(2)}, u32[]{:S(2)}) collective-permute-start(bf16[192,640]{1,0:T(8,128)(2,1)S(1)} %get-tuple-element.62.tile), channel_id=1, source_target_pairs={{0,24},{8,0},{16,8},{24,16},{1,25},{9,1},{17,9},{25,17},{2,26},{10... | collective-permute-start | bytes 737288 | tf_op jit(solution)/shard_map/ppermute | solution.py:43
  66.0 10.7 %collective-permute-start.14 = (bf16[192,640]{1,0:T(8,128)(2,1)S(1)}, bf16[192,640]{1,0:T(8,128)(2,1)S(1)}, u32[]{:S(2)}, u32[]{:S(2)}) collective-permute-start(bf16[192,640]{1,0:T(8,128)(2,1)S(1)} %get-tuple-element.62.tile), channel_id=1, source_target_pairs={{0,8},{8,16},{16,24},{24,0},{1,9},{9,17},{17,25},{25,1},{2,10},{10... | collective-permute-start | bytes 737288 | tf_op jit(solution)/shard_map/ppermute | solution.py:43
  72.5 14.3 %collective-permute-start.20 = (bf16[80,640]{1,0:T(8,128)(2,1)S(1)}, bf16[80,640]{1,0:T(8,128)(2,1)S(1)}, u32[]{:S(2)}, u32[]{:S(2)}) collective-permute-start(bf16[80,640]{1,0:T(8,128)(2,1)S(1)} %get-tuple-element.69), channel_id=1, source_target_pairs={{0,64},{64,128},{128,192},{192,0},{1,65},{65,129},{129,193},{193,1... | collective-permute-start | bytes 307208 | tf_op jit(solution)/shard_map/ppermute | solution.py:43
  77.3 8.6 %collective-permute-start.18 = (bf16[64,640]{1,0:T(8,128)(2,1)S(1)}, bf16[64,640]{1,0:T(8,128)(2,1)S(1)}, u32[]{:S(2)}, u32[]{:S(2)}) collective-permute-start(bf16[64,640]{1,0:T(8,128)(2,1)S(1)} %get-tuple-element.65), channel_id=1, source_target_pairs={{0,8},{8,16},{16,24},{24,0},{1,9},{9,17},{17,25},{25,1},{2,10},{10... | collective-permute-start | bytes 245768 | tf_op jit(solution)/shard_map/ppermute | solution.py:43
  79.1 6.8 %collective-permute-start.19 = (bf16[64,640]{1,0:T(8,128)(2,1)S(1)}, bf16[64,640]{1,0:T(8,128)(2,1)S(1)}, u32[]{:S(2)}, u32[]{:S(2)}) collective-permute-start(bf16[64,640]{1,0:T(8,128)(2,1)S(1)} %get-tuple-element.66), channel_id=1, source_target_pairs={{0,24},{8,0},{16,8},{24,16},{1,25},{9,1},{17,9},{25,17},{2,26},{10... | collective-permute-start | bytes 245768 | tf_op jit(solution)/shard_map/ppermute | solution.py:43
  81.2 12.7 %collective-permute-start.21 = (bf16[80,640]{1,0:T(8,128)(2,1)S(1)}, bf16[80,640]{1,0:T(8,128)(2,1)S(1)}, u32[]{:S(2)}, u32[]{:S(2)}) collective-permute-start(bf16[80,640]{1,0:T(8,128)(2,1)S(1)} %get-tuple-element.70), channel_id=1, source_target_pairs={{0,128},{64,192},{128,0},{192,64},{1,129},{65,193},{129,1},{193,65... | collective-permute-start | bytes 307208 | tf_op jit(solution)/shard_map/ppermute | solution.py:43
  82.8 11.1 %collective-permute-start.22 = (bf16[80,640]{1,0:T(8,128)(2,1)S(1)}, bf16[80,640]{1,0:T(8,128)(2,1)S(1)}, u32[]{:S(2)}, u32[]{:S(2)}) collective-permute-start(bf16[80,640]{1,0:T(8,128)(2,1)S(1)} %get-tuple-element.71), channel_id=1, source_target_pairs={{0,192},{64,0},{128,64},{192,128},{1,193},{65,1},{129,65},{193,129... | collective-permute-start | bytes 307208 | tf_op jit(solution)/shard_map/ppermute | solution.py:43
  85.9 8.0 %collective-permute-start.27 = (bf16[80,640]{1,0:T(8,128)(2,1)S(1)}, bf16[80,640]{1,0:T(8,128)(2,1)S(1)}, u32[]{:S(2)}, u32[]{:S(2)}) collective-permute-start(bf16[80,640]{1,0:T(8,128)(2,1)S(1)} %get-tuple-element.79), channel_id=1, source_target_pairs={{0,2},{2,4},{4,6},{6,0},{1,3},{3,5},{5,7},{7,1},{8,10},{10,12},{12... | collective-permute-start | bytes 307208 | tf_op jit(solution)/shard_map/ppermute | solution.py:43
  86.0 7.9 %collective-permute-start.28 = (bf16[80,640]{1,0:T(8,128)(2,1)S(1)}, bf16[80,640]{1,0:T(8,128)(2,1)S(1)}, u32[]{:S(2)}, u32[]{:S(2)}) collective-permute-start(bf16[80,640]{1,0:T(8,128)(2,1)S(1)} %get-tuple-element.80), channel_id=1, source_target_pairs={{0,4},{2,6},{4,0},{6,2},{1,5},{3,7},{5,1},{7,3},{8,12},{10,14},{12... | collective-permute-start | bytes 307208 | tf_op jit(solution)/shard_map/ppermute | solution.py:43
  86.8 7.0 %collective-permute-start.29 = (bf16[80,640]{1,0:T(8,128)(2,1)S(1)}, bf16[80,640]{1,0:T(8,128)(2,1)S(1)}, u32[]{:S(2)}, u32[]{:S(2)}) collective-permute-start(bf16[80,640]{1,0:T(8,128)(2,1)S(1)} %get-tuple-element.81), channel_id=1, source_target_pairs={{0,6},{2,0},{4,2},{6,4},{1,7},{3,1},{5,3},{7,5},{8,14},{10,8},{12,... | collective-permute-start | bytes 307208 | tf_op jit(solution)/shard_map/ppermute | solution.py:43

commit v3 on v1

--- a/solution.py
+++ b/solution.py
@@ -126,9 +126,13 @@
     return dot(band[:, 0 : SPAN * NLON], window, ((1,), (0,)))
 
 
+def hidden_grad_kernel(tangent, weight_out, hidden_grad):
+    hidden_grad[...] = dot(tangent[...], weight_out[...], ((1,), (1,)))
+
+
 def forward_kernel(
     place, tile, left, right, top, bottom, left_side, right_side, far_e, own_e,
-    tangent, conv_hbm, in_hbm, out_hbm,
+    tangent, hidden_grad, conv_hbm, in_hbm, out_hbm,
     out, blend_grad, mine, mine_mlp, theirs, theirs_mlp, to_up, to_down,
     win, band, coef, spread, conv_weight, weight_in, weight_out, sems
 ):
@@ -173,8 +177,7 @@
         blended.astype(f32) + dot(hidden, weight_out[...], ((1,), (0,)))
     ).astype(bf16)
     slope = cdf + preact * jnp.exp(-0.5 * preact * preact) * gauss_norm
-    hidden_grad = dot(tangent[...], weight_out[...], ((1,), (1,)))
-    preact_grad = (hidden_grad * slope).astype(bf16)
+    preact_grad = (hidden_grad[...] * slope).astype(bf16)
     grad = (
         tangent[...].astype(f32) + dot(preact_grad, weight_in[...], ((1,), (1,)))
     ).astype(bf16)
@@ -218,17 +221,13 @@
 
 def mlp_grad_kernel(place, mine, other, tangent, other_tangent, order, o0, o1, o2, o3, acc):
     x = place[3]
-    sides = []
-    for side, cot in ((mine, tangent), (other, other_tangent)):
-        hidden = dot(side[:, EMBED : 2 * EMBED], order[...], ((1,), (0,))).astype(bf16)
-        grad = dot(side[:, 2 * EMBED : 3 * EMBED], order[...], ((1,), (0,))).astype(bf16)
-        sides.append((hidden, grad, side[:, 0:EMBED], cot[...]))
-    acc[0:EMBED, :] = dot(sides[0][1], sides[0][2], ((0,), (0,))) + dot(
-        sides[1][1], sides[1][2], ((0,), (0,))
-    )
-    acc[EMBED : 2 * EMBED, :] = dot(sides[0][0], sides[0][3], ((0,), (0,))) + dot(
-        sides[1][0], sides[1][3], ((0,), (0,))
-    )
+    hidden, grad = slice(EMBED, 2 * EMBED), slice(2 * EMBED, 3 * EMBED)
+    units = jnp.concatenate([mine[:, grad], other[:, grad], mine[:, hidden], other[:, hidden]])
+    units = dot(units, order[...], ((1,), (0,))).astype(bf16)
+    blended = jnp.concatenate([mine[:, 0:EMBED], other[:, 0:EMBED]])
+    cots = jnp.concatenate([tangent[...], other_tangent[...]])
+    acc[0:EMBED, :] = dot(units[0 : 2 * CELLS], blended, ((0,), (0,)))
+    acc[EMBED : 2 * EMBED, :] = dot(units[2 * CELLS :], cots, ((0,), (0,)))
     for s, o in enumerate((o0, o1, o2, o3)):
         at = pl.multiple_of(lax.rem(x + s, 4) * 160, 160)
         o[0:160, :] = acc[pl.ds(at, 160), :].astype(o.dtype)
@@ -237,11 +236,11 @@
 
 def conv_grad_kernel(place, mine, other, o0, o1, o2, o3):
     y = place[4]
+    grads = jnp.concatenate([mine[:, 0:EMBED], other[:, 0:EMBED]])
     for s, o in enumerate((o0, o1, o2, o3)):
         lanes = pl.ds(pl.multiple_of(lax.rem(y + s, 4) * 384 + EMBED, 128), 384)
-        rows = dot(mine[:, lanes], mine[:, 0:EMBED], ((0,), (0,))) + dot(
-            other[:, lanes], other[:, 0:EMBED], ((0,), (0,))
-        )
+        spread = jnp.concatenate([mine[:, lanes], other[:, lanes]])
+        rows = dot(spread, grads, ((0,), (0,)))
         o[...] = rows[0:320, :].astype(o.dtype)
 
 
@@ -409,6 +408,9 @@
     source = uy * 160 + ul * 40 + ux * 10 + ur
     order = (unit[:, None] == source[None, :]).astype(bf16)
 
+    hidden_grad = call(
+        hidden_grad_kernel, struct((CELLS, HIDDEN), f32), [], 8, None, tangent, weight_out
+    )
     far_e, other_tangent, order = lax.optimization_barrier((far_e, other_tangent, order))
     window = pltpu.VMEM(((CYCLES + 2 * HALO) * NLON, EMBED), bf16)
     band = pltpu.VMEM((2, BASIS * LON, 384), bf16)
@@ -431,7 +433,7 @@
             pltpu.SemaphoreType.DMA((3,)),
         ],
         24, place, tile, left, right, top, bottom, left_side, right_side, far_e, own_e,
-        tangent, in_hbm=(conv_weight, weight_in, weight_out),
+        tangent, hidden_grad, in_hbm=(conv_weight, weight_in, weight_out),
     )
     other = shift(theirs, "core", 2, 1)
     other_mlp = shift(theirs_mlp, "core", 2, 1)
@@ -467,8 +469,7 @@
         16, place, blend_grad, g_left, g_right, g_top, g_bottom, g_left_side, g_right_side,
         own_e, left_side, right_side, far_e, in_hbm=(conv_weight,),
     )
-    m0, field_grad = lax.optimization_barrier((m[0], field_grad))
-    packed = call(pack_kernel, struct((8, 20, EMBED), bf16), [], 4, None, m0, *m[1:], *c)
+    packed = call(pack_kernel, struct((8, 20, EMBED), bf16), [], 4, None, *m, *c)
     parts = lax.all_to_all(packed, ("zlo", "zhi"), split_axis=0, concat_axis=0, tiled=True)
     conv_grad, in_grad, out_grad = call(
         final_kernel,

time: 108 us -> 118 us (1.093)
  waiting for transfers between devices: 20.5 us -> 39.5 us
  blocking collectives: 14.3 us -> 0 us
  starting transfers between devices: 46.7 us -> 52 us
    ppermute x24, waiting for transfers between devices: 18.8 us -> 37.7 us  [shift(): lax.ppermute(block, axis, [(i, (i + step) % count) for i in range(count)])]
    all_to_all x1 -> x0, blocking collectives: 14.3 us -> none  [block(): lax.all_to_all(packed, ('zlo', 'zhi'), split_axis=0, concat_axis=0, tiled...]
    all_to_all x0 -> x1, starting transfers between devices: none -> 6.22 us  [block(): lax.all_to_all(packed, ('zlo', 'zhi'), split_axis=0, concat_axis=0, tiled...]
    ppermute x24, starting transfers between devices: 35.8 us -> 34.6 us  [shift(): lax.ppermute(block, axis, [(i, (i + step) % count) for i in range(count)])]
    pallas_call x10 -> x11, Pallas kernels: 20.6 us -> 21.4 us  [call(): pl.pallas_call(kernel, out_shape=outs, in_specs=in_specs, scratch_shapes=...]
  transfers between devices with their start and end apart: 28 -> 29, of which waited for: 8 -> 13; matrix products, arithmetic and copies ran while one was open for 3% -> 3% of each run, Pallas kernels for 12% -> 11%
where the time goes in v3:
time: 118 us; the launch traced here: 117 us
  starting transfers between devices  52 us (44%)
  waiting for transfers between devices  39.5 us (33%)
  Pallas kernels  21.4 us (18%)
  other arithmetic  2.04 us (2%)
    ppermute x24, waiting for transfers between devices, shift(): lax.ppermute(block, axis, [(i, (i + step) % count) for i in range(count)])  37.7 us
    ppermute x24, starting transfers between devices, shift(): lax.ppermute(block, axis, [(i, (i + step) % count) for i in range(count)])  34.6 us
    pallas_call x11, Pallas kernels, call(): pl.pallas_call(kernel, out_shape=outs, in_specs=in_specs, scratch_shapes=...  21.4 us
    ppermute x2, starting transfers between devices, neighbours(): bottom = lax.ppermute(to_down, LAT, backward)  7.28 us
    all_to_all x1, starting transfers between devices, block(): lax.all_to_all(packed, ('zlo', 'zhi'), split_axis=0, concat_axis=0, tiled...  6.22 us
    ppermute x2, starting transfers between devices, neighbours(): top = lax.ppermute(to_up, LAT, forward)  3.83 us
  transfers between devices with their start and end apart: 29, of which 13 were waited for; matrix products, arithmetic and copies ran while one was open for 3% of the time, Pallas kernels for 11%

profile of v3, /device:TPU:8, one launch (start us, length us, event | category | flops | bytes accessed | tf_op | source)
XLA Modules:
  0.0 116.8 jit_solution(5232404226554203626)
XLA Ops:
  0.7 4.7 %collective-permute-start.1 = (bf16[192,640]{1,0:T(8,128)(2,1)}, bf16[192,640]{1,0:T(8,128)(2,1)S(1)}, u32[]{:S(2)}, u32[]{:S(2)}) collective-permute-start(bf16[192,640]{1,0:T(8,128)(2,1)} %bitcast.22), channel_id=1, source_target_pairs={{0,24},{8,0},{16,8},{24,16},{1,25},{9,1},{17,9},{25,17},{2,26},{10... | collective-permute-start | bytes 737288 | tf_op jit(solution)/shard_map/ppermute | solution.py:43
  5.4 0.9 fusion.21
  6.2 1.9 %collective-permute-start.2 = (bf16[32,640]{1,0:T(8,128)(2,1)S(1)}, bf16[32,640]{1,0:T(8,128)(2,1)S(1)}, u32[]{:S(2)}, u32[]{:S(2)}) collective-permute-start(bf16[32,640]{1,0:T(8,128)(2,1)S(1)} %bitcast.30), channel_id=1, source_target_pairs={{0,32},{32,64},{64,96},{96,128},{128,160},{160,192},{192,224},{1,3... | collective-permute-start | bytes 122888 | tf_op jit(solution)/shard_map/ppermute | solution.py:358
  8.1 3.6 %collective-permute-start.3 = (bf16[32,640]{1,0:T(8,128)(2,1)S(1)}, bf16[32,640]{1,0:T(8,128)(2,1)S(1)}, u32[]{:S(2)}, u32[]{:S(2)}) collective-permute-start(bf16[32,640]{1,0:T(8,128)(2,1)S(1)} %bitcast.29), channel_id=1, source_target_pairs={{32,0},{64,32},{96,64},{128,96},{160,128},{192,160},{224,192},{33,... | collective-permute-start | bytes 122888 | tf_op jit(solution)/shard_map/ppermute | solution.py:359
  11.9 0.7 add_select_fusion
  12.6 0.7 convert_bitcast_fusion
  13.9 0.7 collective-permute-start.6
  14.6 2.2 %collective-permute-done.left = bf16[192,640]{1,0:T(8,128)(2,1)S(1)} collective-permute-done((bf16[192,640]{1,0:T(8,128)(2,1)}, bf16[192,640]{1,0:T(8,128)(2,1)S(1)}, u32[]{:S(2)}, u32[]{:S(2)}) %collective-permute-start) | collective-permute-done | bytes 245792 | tf_op jit(solution)/shard_map/ppermute | solution.py:43
  16.8 0.6 shard_map.110
  17.4 2.1 %collective-permute-start.4 = (bf16[80,640]{1,0:T(8,128)(2,1)S(1)}, bf16[80,640]{1,0:T(8,128)(2,1)S(1)}, u32[]{:S(2)}, u32[]{:S(2)}) collective-permute-start(bf16[80,640]{1,0:T(8,128)(2,1)S(1)} %get-tuple-element.39), channel_id=1, source_target_pairs={{0,8},{8,16},{16,24},{24,0},{1,9},{9,17},{17,25},{25,1},{2,10},{10... | collective-permute-start | bytes 307208 | tf_op jit(solution)/shard_map/ppermute | solution.py:43
  19.4 1.8 %collective-permute-start.5 = (bf16[80,640]{1,0:T(8,128)(2,1)S(1)}, bf16[80,640]{1,0:T(8,128)(2,1)S(1)}, u32[]{:S(2)}, u32[]{:S(2)}) collective-permute-start(bf16[80,640]{1,0:T(8,128)(2,1)S(1)} %get-tuple-element.40), channel_id=1, source_target_pairs={{0,24},{8,0},{16,8},{24,16},{1,25},{9,1},{17,9},{25,17},{2,26},{10... | collective-permute-start | bytes 307208 | tf_op jit(solution)/shard_map/ppermute | solution.py:43
  21.5 0.7 shard_map.111.hidden_grad
  22.2 2.1 %collective-permute-done.4.left_side.left_e = bf16[80,640]{1,0:T(8,128)(2,1)S(1)} collective-permute-done((bf16[80,640]{1,0:T(8,128)(2,1)S(1)}, bf16[80,640]{1,0:T(8,128)(2,1)S(1)}, u32[]{:S(2)}, u32[]{:S(2)}) %collective-permute-start.4) | collective-permute-done | bytes 102432 | tf_op jit(solution)/shard_map/ppermute | solution.py:43
  24.4 1.0 collective-permute-done.5.right_side.right_e
  25.4 6.7 %shard_map.112 = (bf16[192,640]{1,0:T(8,128)(2,1)}, bf16[192,640]{1,0:T(8,128)(2,1)S(1)}, bf16[192,2176]{1,0:T(8,128)(2,1)S(1)}, bf16[192,1920]{1,0:T(8,128)(2,1...) custom-call(s32[5]{0:T(128)S(1)} %stack.23.place, ...), custom_call_target="tpu_custom_call" | custom-call | tf_op jit(solution)/shard_map/pallas_call | solution.py:344
  32.7 1.7 %collective-permute-done.14.other = bf16[192,1920]{1,0:T(8,128)(2,1)S(1)} collective-permute-done((bf16[192,1920]{1,0:T(8,128)(2,1)S(1)}, bf16[192,1920]{1,0:T(8,128)(2,1)S(1)}, u32[]{:S(2)}, u32[]{:S(2)}) %collective-permute-start.14) | collective-permute-done | bytes 737312 | tf_op jit(solution)/shard_map/ppermute | solution.py:43
  34.4 3.2 %shard_map.115 = (f32[320,640]{1,0:T(8,128)S(1)}, bf16[320,640]{1,0:T(8,128)(2,1)S(1)}, bf16[320,640]{1,0:T(8,128)(2,1)S(1)}, bf16[320,640]{1,0:T(8,128)(2,1)S(1)}) custom-call(s32[5]{0:T(128)S(1)} %stack.23.place, bf16[192,1920]{1,0:T(8,128)(2,1)S(1)} %get-tuple-element.48.mine, bf16[192,1920]{1,0:T(8,128)(2,1)S(1)} %collective-permute-done.14.other, ...), custom_call_target="tpu_custom_call" | custom-call | tf_op jit(solution)/shard_map/pallas_call | solution.py:344
  37.6 1.6 %collective-permute-start.15 = (bf16[320,640]{1,0:T(8,128)(2,1)S(1)}, bf16[320,640]{1,0:T(8,128)(2,1)S(1)}, u32[]{:S(2)}, u32[]{:S(2)}) collective-permute-start(bf16[320,640]{1,0:T(8,128)(2,1)S(1)} %get-tuple-element.53), channel_id=1, source_target_pairs={{0,2},{2,4},{4,6},{6,0},{1,3},{3,5},{5,7},{7,1},{8,10},{10,12},{12... | collective-permute-start | bytes 1228808 | tf_op jit(solution)/shard_map/ppermute | solution.py:43
  39.2 2.7 %collective-permute-start.16 = (bf16[320,640]{1,0:T(8,128)(2,1)S(1)}, bf16[320,640]{1,0:T(8,128)(2,1)S(1)}, u32[]{:S(2)}, u32[]{:S(2)}) collective-permute-start(bf16[320,640]{1,0:T(8,128)(2,1)S(1)} %get-tuple-element.54), channel_id=1, source_target_pairs={{0,4},{2,6},{4,0},{6,2},{1,5},{3,7},{5,1},{7,3},{8,12},{10,14},{12... | collective-permute-start | bytes 1228808 | tf_op jit(solution)/shard_map/ppermute | solution.py:43
  41.9 1.4 %collective-permute-start.17 = (bf16[320,640]{1,0:T(8,128)(2,1)S(1)}, bf16[320,640]{1,0:T(8,128)(2,1)S(1)}, u32[]{:S(2)}, u32[]{:S(2)}) collective-permute-start(bf16[320,640]{1,0:T(8,128)(2,1)S(1)} %get-tuple-element.55), channel_id=1, source_target_pairs={{0,6},{2,0},{4,2},{6,4},{1,7},{3,1},{5,3},{7,5},{8,14},{10,8},{12,... | collective-permute-start | bytes 1228808 | tf_op jit(solution)/shard_map/ppermute | solution.py:43
  43.4 1.9 %shard_map.117 = (f32[320,640]{1,0:T(8,128)S(1)}, bf16[320,640]{1,0:T(8,128)(2,1)S(1)}, bf16[320,640]{1,0:T(8,128)(2,1)S(1)}, bf16[320,640]{1,0:T(8,128)(2,1)S(1)}) custom-call(s32[5]{0:T(128)S(1)} %stack.23.place, bf16[192,2176]{1,0:T(8,128)(2,1)S(1)} %get-tuple-element.60.mine, bf16[192,2176]{1,0:T(8,128)(2,1)S(1)} %collective-permute-done.21.other), custom_call_target="tpu_custom_call" | custom-call | tf_op jit(solution)/shard_map/pallas_call | solution.py:344
  45.2 1.6 %collective-permute-start.22 = (bf16[320,640]{1,0:T(8,128)(2,1)S(1)}, bf16[320,640]{1,0:T(8,128)(2,1)S(1)}, u32[]{:S(2)}, u32[]{:S(2)}) collective-permute-start(bf16[320,640]{1,0:T(8,128)(2,1)S(1)} %get-tuple-element.63), channel_id=1, source_target_pairs={{0,64},{64,128},{128,192},{192,0},{1,65},{65,129},{129,193},{193,1... | collective-permute-start | bytes 1228808 | tf_op jit(solution)/shard_map/ppermute | solution.py:43
  46.9 0.9 collective-permute-start.23
  47.7 2.7 %collective-permute-done.15.r1 = bf16[320,640]{1,0:T(8,128)(2,1)S(1)} collective-permute-done((bf16[320,640]{1,0:T(8,128)(2,1)S(1)}, bf16[320,640]{1,0:T(8,128)(2,1)S(1)}, u32[]{:S(2)}, u32[]{:S(2)}) %collective-permute-start.15) | collective-permute-done | bytes 409632 | tf_op jit(solution)/shard_map/ppermute | solution.py:43
  50.8 9.4 %collective-permute-done.16.r2 = bf16[320,640]{1,0:T(8,128)(2,1)S(1)} collective-permute-done((bf16[320,640]{1,0:T(8,128)(2,1)S(1)}, bf16[320,640]{1,0:T(8,128)(2,1)S(1)}, u32[]{:S(2)}, u32[]{:S(2)}) %collective-permute-start.16) | collective-permute-done | bytes 409632 | tf_op jit(solution)/shard_map/ppermute | solution.py:43
  60.2 0.9 shard_map.116
  61.1 1.7 %collective-permute-start.18 = (bf16[80,640]{1,0:T(8,128)(2,1)S(1)}, bf16[80,640]{1,0:T(8,128)(2,1)S(1)}, u32[]{:S(2)}, u32[]{:S(2)}) collective-permute-start(bf16[80,640]{1,0:T(8,128)(2,1)S(1)} %get-tuple-element.57), channel_id=1, source_target_pairs={{0,64},{64,128},{128,192},{192,0},{1,65},{65,129},{129,193},{193,1... | collective-permute-start | bytes 307208 | tf_op jit(solution)/shard_map/ppermute | solution.py:43
  62.8 0.9 collective-permute-start.19
  63.6 2.5 %collective-permute-start.20 = (bf16[80,640]{1,0:T(8,128)(2,1)S(1)}, bf16[80,640]{1,0:T(8,128)(2,1)S(1)}, u32[]{:S(2)}, u32[]{:S(2)}) collective-permute-start(bf16[80,640]{1,0:T(8,128)(2,1)S(1)} %get-tuple-element.59), channel_id=1, source_target_pairs={{0,192},{64,0},{128,64},{192,128},{1,193},{65,1},{129,65},{193,129... | collective-permute-start | bytes 307208 | tf_op jit(solution)/shard_map/ppermute | solution.py:43
  66.1 2.6 %collective-permute-done.24.r3 = bf16[320,640]{1,0:T(8,128)(2,1)S(1)} collective-permute-done((bf16[320,640]{1,0:T(8,128)(2,1)S(1)}, bf16[320,640]{1,0:T(8,128)(2,1)S(1)}, u32[]{:S(2)}, u32[]{:S(2)}) %collective-permute-start.24) | collective-permute-done | bytes 409632 | tf_op jit(solution)/shard_map/ppermute | solution.py:43
  68.7 1.0 shard_map.118
  70.2 0.7 collective-permute-start.26
  70.9 2.1 %collective-permute-start.27 = (bf16[80,640]{1,0:T(8,128)(2,1)S(1)}, bf16[80,640]{1,0:T(8,128)(2,1)S(1)}, u32[]{:S(2)}, u32[]{:S(2)}) collective-permute-start(bf16[80,640]{1,0:T(8,128)(2,1)S(1)} %get-tuple-element.69), channel_id=1, source_target_pairs={{0,6},{2,0},{4,2},{6,4},{1,7},{3,1},{5,3},{7,5},{8,14},{10,8},{12,... | collective-permute-start | bytes 307208 | tf_op jit(solution)/shard_map/ppermute | solution.py:43
  73.0 4.9 %collective-permute-done.25.c1 = bf16[80,640]{1,0:T(8,128)(2,1)S(1)} collective-permute-done((bf16[80,640]{1,0:T(8,128)(2,1)S(1)}, bf16[80,640]{1,0:T(8,128)(2,1)S(1)}, u32[]{:S(2)}, u32[]{:S(2)}) %collective-permute-start.25) | collective-permute-done | bytes 102432 | tf_op jit(solution)/shard_map/ppermute | solution.py:43
  77.9 0.6 collective-permute-done.27.c3
  78.5 0.9 shard_map.119
  79.4 6.2 %all-to-all-start = ((bf16[8,20,640]{2,1,0:T(8,128)(2,1)}), bf16[8,20,640]{2,1,0:T(8,128)(2,1)S(1)}, u32[]{:S(2)}, u32[]{:S(2)}) async-start(bf16[8,20,640]{2,1,0:T(8,128)(2,1)} %shard_map.119), calls=%async_computation | async-start | bytes 491520 | tf_op jit(solution)/shard_map/all_to_all | solution.py:473
  85.6 3.8 %collective-permute-start.9 = (bf16[192,640]{1,0:T(8,128)(2,1)S(1)}, bf16[192,640]{1,0:T(8,128)(2,1)S(1)}, u32[]{:S(2)}, u32[]{:S(2)}) collective-permute-start(bf16[192,640]{1,0:T(8,128)(2,1)S(1)} %get-tuple-element.43.tile), channel_id=1, source_target_pairs={{0,24},{8,0},{16,8},{24,16},{1,25},{9,1},{17,9},{25,17},{2,26},{10... | collective-permute-start | bytes 737288 | tf_op jit(solution)/shard_map/ppermute | solution.py:43
  89.5 1.9 %collective-permute-start.10 = (bf16[40,640]{1,0:T(8,128)(2,1)S(1)}, bf16[40,640]{1,0:T(8,128)(2,1)S(1)}, u32[]{:S(2)}, u32[]{:S(2)}) collective-permute-start(bf16[40,640]{1,0:T(8,128)(2,1)S(1)} %get-tuple-element.44), channel_id=1, source_target_pairs={{0,32},{32,64},{64,96},{96,128},{128,160},{160,192},{192,224},{1,3... | collective-permute-start | bytes 153608 | tf_op jit(solution)/shard_map/ppermute | solution.py:358
  91.4 3.6 %collective-permute-start.11 = (bf16[40,640]{1,0:T(8,128)(2,1)S(1)}, bf16[40,640]{1,0:T(8,128)(2,1)S(1)}, u32[]{:S(2)}, u32[]{:S(2)}) collective-permute-start(bf16[40,640]{1,0:T(8,128)(2,1)S(1)} %get-tuple-element.45), channel_id=1, source_target_pairs={{32,0},{64,32},{96,64},{128,96},{160,128},{192,160},{224,192},{33,... | collective-permute-start | bytes 153608 | tf_op jit(solution)/shard_map/ppermute | solution.py:359
  95.0 1.7 %collective-permute-done.11.bottom = bf16[40,640]{1,0:T(8,128)(2,1)S(1)} collective-permute-done((bf16[40,640]{1,0:T(8,128)(2,1)S(1)}, bf16[40,640]{1,0:T(8,128)(2,1)S(1)}, u32[]{:S(2)}, u32[]{:S(2)}) %collective-permute-start.11) | collective-permute-done | bytes 51232 | tf_op jit(solution)/shard_map/ppermute | solution.py:359
  96.8 1.2 %collective-permute-done.9.right = bf16[192,640]{1,0:T(8,128)(2,1)S(1)} collective-permute-done((bf16[192,640]{1,0:T(8,128)(2,1)S(1)}, bf16[192,640]{1,0:T(8,128)(2,1)S(1)}, u32[]{:S(2)}, u32[]{:S(2)}) %collective-permute-start.9) | collective-permute-done | bytes 245792 | tf_op jit(solution)/shard_map/ppermute | solution.py:43
  98.0 6.8 %collective-permute-done.8.left = bf16[192,640]{1,0:T(8,128)(2,1)S(1)} collective-permute-done((bf16[192,640]{1,0:T(8,128)(2,1)S(1)}, bf16[192,640]{1,0:T(8,128)(2,1)S(1)}, u32[]{:S(2)}, u32[]{:S(2)}) %collective-permute-start.8) | collective-permute-done | bytes 245792 | tf_op jit(solution)/shard_map/ppermute | solution.py:43
  104.8 0.6 shard_map.113
  105.5 3.8 %collective-permute-start.13 = (bf16[64,640]{1,0:T(8,128)(2,1)S(1)}, bf16[64,640]{1,0:T(8,128)(2,1)S(1)}, u32[]{:S(2)}, u32[]{:S(2)}) collective-permute-start(bf16[64,640]{1,0:T(8,128)(2,1)S(1)} %get-tuple-element.47), channel_id=1, source_target_pairs={{0,24},{8,0},{16,8},{24,16},{1,25},{9,1},{17,9},{25,17},{2,26},{10... | collective-permute-start | bytes 245768 | tf_op jit(solution)/shard_map/ppermute | solution.py:43
  109.3 2.4 %collective-permute-done.12.left_side = bf16[64,640]{1,0:T(8,128)(2,1)S(1)} collective-permute-done((bf16[64,640]{1,0:T(8,128)(2,1)S(1)}, bf16[64,640]{1,0:T(8,128)(2,1)S(1)}, u32[]{:S(2)}, u32[]{:S(2)}) %collective-permute-start.12) | collective-permute-done | bytes 81952 | tf_op jit(solution)/shard_map/ppermute | solution.py:43
  111.7 4.5 %shard_map.114 = bf16[192,640]{1,0:T(8,128)(2,1)} custom-call(s32[5]{0:T(128)S(1)} %stack.23.place, bf16[192,640]{1,0:T(8,128)(2,1)S(1)} %get-tuple-element.43.tile, bf16[192,640]{1,0:T(8,128)(2,1)S(1)} %collective-permute-done.8.left, bf16[192,640]{1,0:T(8,128)(2,1)S(1)} %collective-permute-done.9.right, bf16[40,640]{1,0:T(8,128)(2,1)S(1)} %collective-permute-done.10.top, ...), custom_call_target="tpu_custom_call" | custom-call | tf_op jit(solution)/shard_map/pallas_call | solution.py:344
  116.2 0.6 shard_map.120
  (41 shorter events, 2.5 us)
Async XLA Ops:
  0.6 20.9 %copy-start.1 = (bf16[1,12,16,640]{3,2,1,0:T(8,128)(2,1)S(1)}, bf16[1,12,16,640]{3,2,1,0:T(8,128)(2,1)}, u32[]{:S(2)}) copy-start(bf16[1,12,16,640]{3,2,1,0:T(8,128)(2,1)} %param.13) | copy-start | bytes 737284
  0.6 20.9 %copy-start = (bf16[1280,640]{1,0:T(8,128)(2,1)S(1)}, bf16[1280,640]{1,0:T(8,128)(2,1)}, u32[]{:S(2)}) copy-start(bf16[1280,640]{1,0:T(8,128)(2,1)} %out_hbm.1) | copy-start | bytes 4915204
  0.7 13.9 %collective-permute-start.1 = (bf16[192,640]{1,0:T(8,128)(2,1)}, bf16[192,640]{1,0:T(8,128)(2,1)S(1)}, u32[]{:S(2)}, u32[]{:S(2)}) collective-permute-start(bf16[192,640]{1,0:T(8,128)(2,1)} %bitcast.22), channel_id=1, source_target_pairs={{0,24},{8,0},{16,8},{24,16},{1,25},{9,1},{17,9},{25,17},{2,26},{10... | collective-permute-start | bytes 737288 | tf_op jit(solution)/shard_map/ppermute | solution.py:43
  5.4 11.4 %collective-permute-start = (bf16[192,640]{1,0:T(8,128)(2,1)}, bf16[192,640]{1,0:T(8,128)(2,1)S(1)}, u32[]{:S(2)}, u32[]{:S(2)}) collective-permute-start(bf16[192,640]{1,0:T(8,128)(2,1)} %bitcast.23), channel_id=1, source_target_pairs={{0,8},{8,16},{16,24},{24,0},{1,9},{9,17},{17,25},{25,1},{2,10},{10... | collective-permute-start | bytes 737288 | tf_op jit(solution)/shard_map/ppermute | solution.py:43
  6.2 7.7 %collective-permute-start.2 = (bf16[32,640]{1,0:T(8,128)(2,1)S(1)}, bf16[32,640]{1,0:T(8,128)(2,1)S(1)}, u32[]{:S(2)}, u32[]{:S(2)}) collective-permute-start(bf16[32,640]{1,0:T(8,128)(2,1)S(1)} %bitcast.30), channel_id=1, source_target_pairs={{0,32},{32,64},{64,96},{96,128},{128,160},{160,192},{192,224},{1,3... | collective-permute-start | bytes 122888 | tf_op jit(solution)/shard_map/ppermute | solution.py:358
  8.1 6.4 %collective-permute-start.3 = (bf16[32,640]{1,0:T(8,128)(2,1)S(1)}, bf16[32,640]{1,0:T(8,128)(2,1)S(1)}, u32[]{:S(2)}, u32[]{:S(2)}) collective-permute-start(bf16[32,640]{1,0:T(8,128)(2,1)S(1)} %bitcast.29), channel_id=1, source_target_pairs={{32,0},{64,32},{96,64},{128,96},{160,128},{192,160},{224,192},{33,... | collective-permute-start | bytes 122888 | tf_op jit(solution)/shard_map/ppermute | solution.py:359
  11.8 10.4 %collective-permute-start.7 = (bf16[192,640]{1,0:T(8,128)(2,1)}, bf16[192,640]{1,0:T(8,128)(2,1)S(1)}, u32[]{:S(2)}, u32[]{:S(2)}) collective-permute-start(bf16[192,640]{1,0:T(8,128)(2,1)} %bitcast.18), channel_id=1, source_target_pairs={{0,32},{32,0},{1,33},{33,1},{2,34},{34,2},{3,35},{35,3},{4,36},{36... | collective-permute-start | bytes 737288 | tf_op jit(solution)/shard_map/ppermute | solution.py:43
  13.9 8.3 %collective-permute-start.6 = (bf16[16,640]{1,0:T(8,128)(2,1)S(1)}, bf16[16,640]{1,0:T(8,128)(2,1)S(1)}, u32[]{:S(2)}, u32[]{:S(2)}) collective-permute-start(bf16[16,640]{1,0:T(8,128)(2,1)S(1)} %pad.4.rest_0_.own_e), channel_id=1, source_target_pairs={{0,16},{8,24},{16,0},{24,8},{1,17},{9,25},{17,1},{25,9},{2,18},{10... | collective-permute-start | bytes 61448 | tf_op jit(solution)/shard_map/ppermute | solution.py:43
  17.4 7.0 %collective-permute-start.4 = (bf16[80,640]{1,0:T(8,128)(2,1)S(1)}, bf16[80,640]{1,0:T(8,128)(2,1)S(1)}, u32[]{:S(2)}, u32[]{:S(2)}) collective-permute-start(bf16[80,640]{1,0:T(8,128)(2,1)S(1)} %get-tuple-element.39), channel_id=1, source_target_pairs={{0,8},{8,16},{16,24},{24,0},{1,9},{9,17},{17,25},{25,1},{2,10},{10... | collective-permute-start | bytes 307208 | tf_op jit(solution)/shard_map/ppermute | solution.py:43
  19.4 5.9 %collective-permute-start.5 = (bf16[80,640]{1,0:T(8,128)(2,1)S(1)}, bf16[80,640]{1,0:T(8,128)(2,1)S(1)}, u32[]{:S(2)}, u32[]{:S(2)}) collective-permute-start(bf16[80,640]{1,0:T(8,128)(2,1)S(1)} %get-tuple-element.40), channel_id=1, source_target_pairs={{0,24},{8,0},{16,8},{24,16},{1,25},{9,1},{17,9},{25,17},{2,26},{10... | collective-permute-start | bytes 307208 | tf_op jit(solution)/shard_map/ppermute | solution.py:43
  21.5 3.9 %copy-start.2 = (bf16[1,12,16,640]{3,2,1,0:T(8,128)(2,1)S(1)}, bf16[1,12,16,640]{3,2,1,0:T(8,128)(2,1)}, u32[]{:S(2)}) copy-start(bf16[1,12,16,640]{3,2,1,0:T(8,128)(2,1)} %param.7) | copy-start | bytes 737284
  32.1 2.3 %collective-permute-start.14 = (bf16[192,1920]{1,0:T(8,128)(2,1)S(1)}, bf16[192,1920]{1,0:T(8,128)(2,1)S(1)}, u32[]{:S(2)}, u32[]{:S(2)}) collective-permute-start(bf16[192,1920]{1,0:T(8,128)(2,1)S(1)} %get-tuple-element.49), channel_id=1, source_target_pairs={{0,32},{32,0},{1,33},{33,1},{2,34},{34,2},{3,35},{35,3},{4,36},{36... | collective-permute-start | bytes 2211848 | tf_op jit(solution)/shard_map/ppermute | solution.py:43
  32.2 11.2 %collective-permute-start.21 = (bf16[192,2176]{1,0:T(8,128)(2,1)S(1)}, bf16[192,2176]{1,0:T(8,128)(2,1)S(1)}, u32[]{:S(2)}, u32[]{:S(2)}) collective-permute-start(bf16[192,2176]{1,0:T(8,128)(2,1)S(1)} %get-tuple-element.61), channel_id=1, source_target_pairs={{0,32},{32,0},{1,33},{33,1},{2,34},{34,2},{3,35},{35,3},{4,36},{36... | collective-permute-start | bytes 2506760 | tf_op jit(solution)/shard_map/ppermute | solution.py:43
  37.6 12.8 %collective-permute-start.15 = (bf16[320,640]{1,0:T(8,128)(2,1)S(1)}, bf16[320,640]{1,0:T(8,128)(2,1)S(1)}, u32[]{:S(2)}, u32[]{:S(2)}) collective-permute-start(bf16[320,640]{1,0:T(8,128)(2,1)S(1)} %get-tuple-element.53), channel_id=1, source_target_pairs={{0,2},{2,4},{4,6},{6,0},{1,3},{3,5},{5,7},{7,1},{8,10},{10,12},{12... | collective-permute-start | bytes 1228808 | tf_op jit(solution)/shard_map/ppermute | solution.py:43
  39.2 21.0 %collective-permute-start.16 = (bf16[320,640]{1,0:T(8,128)(2,1)S(1)}, bf16[320,640]{1,0:T(8,128)(2,1)S(1)}, u32[]{:S(2)}, u32[]{:S(2)}) collective-permute-start(bf16[320,640]{1,0:T(8,128)(2,1)S(1)} %get-tuple-element.54), channel_id=1, source_target_pairs={{0,4},{2,6},{4,0},{6,2},{1,5},{3,7},{5,1},{7,3},{8,12},{10,14},{12... | collective-permute-start | bytes 1228808 | tf_op jit(solution)/shard_map/ppermute | solution.py:43
  41.9 18.3 %collective-permute-start.17 = (bf16[320,640]{1,0:T(8,128)(2,1)S(1)}, bf16[320,640]{1,0:T(8,128)(2,1)S(1)}, u32[]{:S(2)}, u32[]{:S(2)}) collective-permute-start(bf16[320,640]{1,0:T(8,128)(2,1)S(1)} %get-tuple-element.55), channel_id=1, source_target_pairs={{0,6},{2,0},{4,2},{6,4},{1,7},{3,1},{5,3},{7,5},{8,14},{10,8},{12,... | collective-permute-start | bytes 1228808 | tf_op jit(solution)/shard_map/ppermute | solution.py:43
  45.2 18.4 %collective-permute-start.22 = (bf16[320,640]{1,0:T(8,128)(2,1)S(1)}, bf16[320,640]{1,0:T(8,128)(2,1)S(1)}, u32[]{:S(2)}, u32[]{:S(2)}) collective-permute-start(bf16[320,640]{1,0:T(8,128)(2,1)S(1)} %get-tuple-element.63), channel_id=1, source_target_pairs={{0,64},{64,128},{128,192},{192,0},{1,65},{65,129},{129,193},{193,1... | collective-permute-start | bytes 1228808 | tf_op jit(solution)/shard_map/ppermute | solution.py:43
  46.9 19.2 %collective-permute-start.23 = (bf16[320,640]{1,0:T(8,128)(2,1)S(1)}, bf16[320,640]{1,0:T(8,128)(2,1)S(1)}, u32[]{:S(2)}, u32[]{:S(2)}) collective-permute-start(bf16[320,640]{1,0:T(8,128)(2,1)S(1)} %get-tuple-element.64), channel_id=1, source_target_pairs={{0,128},{64,192},{128,0},{192,64},{1,129},{65,193},{129,1},{193,65... | collective-permute-start | bytes 1228808 | tf_op jit(solution)/shard_map/ppermute | solution.py:43
  50.4 18.3 %collective-permute-start.24 = (bf16[320,640]{1,0:T(8,128)(2,1)S(1)}, bf16[320,640]{1,0:T(8,128)(2,1)S(1)}, u32[]{:S(2)}, u32[]{:S(2)}) collective-permute-start(bf16[320,640]{1,0:T(8,128)(2,1)S(1)} %get-tuple-element.65), channel_id=1, source_target_pairs={{0,192},{64,0},{128,64},{192,128},{1,193},{65,1},{129,65},{193,129... | collective-permute-start | bytes 1228808 | tf_op jit(solution)/shard_map/ppermute | solution.py:43
  61.1 9.8 %collective-permute-start.18 = (bf16[80,640]{1,0:T(8,128)(2,1)S(1)}, bf16[80,640]{1,0:T(8,128)(2,1)S(1)}, u32[]{:S(2)}, u32[]{:S(2)}) collective-permute-start(bf16[80,640]{1,0:T(8,128)(2,1)S(1)} %get-tuple-element.57), channel_id=1, source_target_pairs={{0,64},{64,128},{128,192},{192,0},{1,65},{65,129},{129,193},{193,1... | collective-permute-start | bytes 307208 | tf_op jit(solution)/shard_map/ppermute | solution.py:43
  62.8 10.3 %collective-permute-start.19 = (bf16[80,640]{1,0:T(8,128)(2,1)S(1)}, bf16[80,640]{1,0:T(8,128)(2,1)S(1)}, u32[]{:S(2)}, u32[]{:S(2)}) collective-permute-start(bf16[80,640]{1,0:T(8,128)(2,1)S(1)} %get-tuple-element.58), channel_id=1, source_target_pairs={{0,128},{64,192},{128,0},{192,64},{1,129},{65,193},{129,1},{193,65... | collective-permute-start | bytes 307208 | tf_op jit(solution)/shard_map/ppermute | solution.py:43
  63.6 9.4 %collective-permute-start.20 = (bf16[80,640]{1,0:T(8,128)(2,1)S(1)}, bf16[80,640]{1,0:T(8,128)(2,1)S(1)}, u32[]{:S(2)}, u32[]{:S(2)}) collective-permute-start(bf16[80,640]{1,0:T(8,128)(2,1)S(1)} %get-tuple-element.59), channel_id=1, source_target_pairs={{0,192},{64,0},{128,64},{192,128},{1,193},{65,1},{129,65},{193,129... | collective-permute-start | bytes 307208 | tf_op jit(solution)/shard_map/ppermute | solution.py:43
  69.7 8.2 %collective-permute-start.25 = (bf16[80,640]{1,0:T(8,128)(2,1)S(1)}, bf16[80,640]{1,0:T(8,128)(2,1)S(1)}, u32[]{:S(2)}, u32[]{:S(2)}) collective-permute-start(bf16[80,640]{1,0:T(8,128)(2,1)S(1)} %get-tuple-element.67), channel_id=1, source_target_pairs={{0,2},{2,4},{4,6},{6,0},{1,3},{3,5},{5,7},{7,1},{8,10},{10,12},{12... | collective-permute-start | bytes 307208 | tf_op jit(solution)/shard_map/ppermute | solution.py:43
  70.2 7.7 %collective-permute-start.26 = (bf16[80,640]{1,0:T(8,128)(2,1)S(1)}, bf16[80,640]{1,0:T(8,128)(2,1)S(1)}, u32[]{:S(2)}, u32[]{:S(2)}) collective-permute-start(bf16[80,640]{1,0:T(8,128)(2,1)S(1)} %get-tuple-element.68), channel_id=1, source_target_pairs={{0,4},{2,6},{4,0},{6,2},{1,5},{3,7},{5,1},{7,3},{8,12},{10,14},{12... | collective-permute-start | bytes 307208 | tf_op jit(solution)/shard_map/ppermute | solution.py:43
  70.9 7.6 %collective-permute-start.27 = (bf16[80,640]{1,0:T(8,128)(2,1)S(1)}, bf16[80,640]{1,0:T(8,128)(2,1)S(1)}, u32[]{:S(2)}, u32[]{:S(2)}) collective-permute-start(bf16[80,640]{1,0:T(8,128)(2,1)S(1)} %get-tuple-element.69), channel_id=1, source_target_pairs={{0,6},{2,0},{4,2},{6,4},{1,7},{3,1},{5,3},{7,5},{8,14},{10,8},{12,... | collective-permute-start | bytes 307208 | tf_op jit(solution)/shard_map/ppermute | solution.py:43
  79.4 36.8 %all-to-all-start = ((bf16[8,20,640]{2,1,0:T(8,128)(2,1)}), bf16[8,20,640]{2,1,0:T(8,128)(2,1)S(1)}, u32[]{:S(2)}, u32[]{:S(2)}) async-start(bf16[8,20,640]{2,1,0:T(8,128)(2,1)} %shard_map.119), calls=%async_computation | async-start | bytes 491520 | tf_op jit(solution)/shard_map/all_to_all | solution.py:473
  85.6 12.4 %collective-permute-start.9 = (bf16[192,640]{1,0:T(8,128)(2,1)S(1)}, bf16[192,640]{1,0:T(8,128)(2,1)S(1)}, u32[]{:S(2)}, u32[]{:S(2)}) collective-permute-start(bf16[192,640]{1,0:T(8,128)(2,1)S(1)} %get-tuple-element.43.tile), channel_id=1, source_target_pairs={{0,24},{8,0},{16,8},{24,16},{1,25},{9,1},{17,9},{25,17},{2,26},{10... | collective-permute-start | bytes 737288 | tf_op jit(solution)/shard_map/ppermute | solution.py:43
  89.5 15.3 %collective-permute-start.8 = (bf16[192,640]{1,0:T(8,128)(2,1)S(1)}, bf16[192,640]{1,0:T(8,128)(2,1)S(1)}, u32[]{:S(2)}, u32[]{:S(2)}) collective-permute-start(bf16[192,640]{1,0:T(8,128)(2,1)S(1)} %get-tuple-element.43.tile), channel_id=1, source_target_pairs={{0,8},{8,16},{16,24},{24,0},{1,9},{9,17},{17,25},{25,1},{2,10},{10... | collective-permute-start | bytes 737288 | tf_op jit(solution)/shard_map/ppermute | solution.py:43
  89.5 5.6 %collective-permute-start.10 = (bf16[40,640]{1,0:T(8,128)(2,1)S(1)}, bf16[40,640]{1,0:T(8,128)(2,1)S(1)}, u32[]{:S(2)}, u32[]{:S(2)}) collective-permute-start(bf16[40,640]{1,0:T(8,128)(2,1)S(1)} %get-tuple-element.44), channel_id=1, source_target_pairs={{0,32},{32,64},{64,96},{96,128},{128,160},{160,192},{192,224},{1,3... | collective-permute-start | bytes 153608 | tf_op jit(solution)/shard_map/ppermute | solution.py:358
  91.4 5.4 %collective-permute-start.11 = (bf16[40,640]{1,0:T(8,128)(2,1)S(1)}, bf16[40,640]{1,0:T(8,128)(2,1)S(1)}, u32[]{:S(2)}, u32[]{:S(2)}) collective-permute-start(bf16[40,640]{1,0:T(8,128)(2,1)S(1)} %get-tuple-element.45), channel_id=1, source_target_pairs={{32,0},{64,32},{96,64},{128,96},{160,128},{192,160},{224,192},{33,... | collective-permute-start | bytes 153608 | tf_op jit(solution)/shard_map/ppermute | solution.py:359
  105.4 6.3 %collective-permute-start.12 = (bf16[64,640]{1,0:T(8,128)(2,1)S(1)}, bf16[64,640]{1,0:T(8,128)(2,1)S(1)}, u32[]{:S(2)}, u32[]{:S(2)}) collective-permute-start(bf16[64,640]{1,0:T(8,128)(2,1)S(1)} %get-tuple-element.46), channel_id=1, source_target_pairs={{0,8},{8,16},{16,24},{24,0},{1,9},{9,17},{17,25},{25,1},{2,10},{10... | collective-permute-start | bytes 245768 | tf_op jit(solution)/shard_map/ppermute | solution.py:43
  105.5 6.2 %collective-permute-start.13 = (bf16[64,640]{1,0:T(8,128)(2,1)S(1)}, bf16[64,640]{1,0:T(8,128)(2,1)S(1)}, u32[]{:S(2)}, u32[]{:S(2)}) collective-permute-start(bf16[64,640]{1,0:T(8,128)(2,1)S(1)} %get-tuple-element.47), channel_id=1, source_target_pairs={{0,24},{8,0},{16,8},{24,16},{1,25},{9,1},{17,9},{25,17},{2,26},{10... | collective-permute-start | bytes 245768 | tf_op jit(solution)/shard_map/ppermute | solution.py:43

commit v4 on v3

--- a/solution.py
+++ b/solution.py
@@ -223,11 +223,11 @@
     x = place[3]
     hidden, grad = slice(EMBED, 2 * EMBED), slice(2 * EMBED, 3 * EMBED)
     units = jnp.concatenate([mine[:, grad], other[:, grad], mine[:, hidden], other[:, hidden]])
-    units = dot(units, order[...], ((1,), (0,))).astype(bf16)
+    units = dot(order[...], units, ((1,), (1,))).astype(bf16)
     blended = jnp.concatenate([mine[:, 0:EMBED], other[:, 0:EMBED]])
     cots = jnp.concatenate([tangent[...], other_tangent[...]])
-    acc[0:EMBED, :] = dot(units[0 : 2 * CELLS], blended, ((0,), (0,)))
-    acc[EMBED : 2 * EMBED, :] = dot(units[2 * CELLS :], cots, ((0,), (0,)))
+    acc[0:EMBED, :] = dot(units[:, 0 : 2 * CELLS], blended, ((1,), (0,)))
+    acc[EMBED : 2 * EMBED, :] = dot(units[:, 2 * CELLS :], cots, ((1,), (0,)))
     for s, o in enumerate((o0, o1, o2, o3)):
         at = pl.multiple_of(lax.rem(x + s, 4) * 160, 160)
         o[0:160, :] = acc[pl.ds(at, 160), :].astype(o.dtype)
@@ -406,7 +406,7 @@
     unit = jnp.arange(EMBED, dtype=jnp.int32)
     ux, uy, ul, ur = unit // 160, unit // 40 % 4, unit // 10 % 4, unit % 10
     source = uy * 160 + ul * 40 + ux * 10 + ur
-    order = (unit[:, None] == source[None, :]).astype(bf16)
+    order = (source[:, None] == unit[None, :]).astype(bf16)
 
     hidden_grad = call(
         hidden_grad_kernel, struct((CELLS, HIDDEN), f32), [], 8, None, tangent, weight_out

time: 118 us -> 117 us (level)
  no operation moved by 1% of the time
where the time goes in v4:
time: 117 us; the launch traced here: 116 us
  starting transfers between devices  52 us (44%)
  waiting for transfers between devices  39.5 us (34%)
  Pallas kernels  21.1 us (18%)
  other arithmetic  1.99 us (2%)
    ppermute x24, waiting for transfers between devices, shift(): lax.ppermute(block, axis, [(i, (i + step) % count) for i in range(count)])  37.8 us
    ppermute x24, starting transfers between devices, shift(): lax.ppermute(block, axis, [(i, (i + step) % count) for i in range(count)])  34.6 us
    pallas_call x11, Pallas kernels, call(): pl.pallas_call(kernel, out_shape=outs, in_specs=in_specs, scratch_shapes=...  21.1 us
    ppermute x2, starting transfers between devices, neighbours(): bottom = lax.ppermute(to_down, LAT, backward)  7.28 us
    all_to_all x1, starting transfers between devices, block(): lax.all_to_all(packed, ('zlo', 'zhi'), split_axis=0, concat_axis=0, tiled...  6.22 us
    ppermute x2, starting transfers between devices, neighbours(): top = lax.ppermute(to_up, LAT, forward)  3.83 us
  transfers between devices with their start and end apart: 29, of which 13 were waited for; matrix products, arithmetic and copies ran while one was open for 3% of the time, Pallas kernels for 11%

profile of v4, /device:TPU:8, one launch (start us, length us, event | category | flops | bytes accessed | tf_op | source)
XLA Modules:
  0.0 116.5 jit_solution(9247037669535525022)
XLA Ops:
  0.7 4.7 %collective-permute-start.1 = (bf16[192,640]{1,0:T(8,128)(2,1)}, bf16[192,640]{1,0:T(8,128)(2,1)S(1)}, u32[]{:S(2)}, u32[]{:S(2)}) collective-permute-start(bf16[192,640]{1,0:T(8,128)(2,1)} %bitcast.22), channel_id=1, source_target_pairs={{0,24},{8,0},{16,8},{24,16},{1,25},{9,1},{17,9},{25,17},{2,26},{10... | collective-permute-start | bytes 737288 | tf_op jit(solution)/shard_map/ppermute | solution.py:43
  5.4 0.9 fusion.21
  6.2 1.9 %collective-permute-start.2 = (bf16[32,640]{1,0:T(8,128)(2,1)S(1)}, bf16[32,640]{1,0:T(8,128)(2,1)S(1)}, u32[]{:S(2)}, u32[]{:S(2)}) collective-permute-start(bf16[32,640]{1,0:T(8,128)(2,1)S(1)} %bitcast.30), channel_id=1, source_target_pairs={{0,32},{32,64},{64,96},{96,128},{128,160},{160,192},{192,224},{1,3... | collective-permute-start | bytes 122888 | tf_op jit(solution)/shard_map/ppermute | solution.py:358
  8.1 3.6 %collective-permute-start.3 = (bf16[32,640]{1,0:T(8,128)(2,1)S(1)}, bf16[32,640]{1,0:T(8,128)(2,1)S(1)}, u32[]{:S(2)}, u32[]{:S(2)}) collective-permute-start(bf16[32,640]{1,0:T(8,128)(2,1)S(1)} %bitcast.29), channel_id=1, source_target_pairs={{32,0},{64,32},{96,64},{128,96},{160,128},{192,160},{224,192},{33,... | collective-permute-start | bytes 122888 | tf_op jit(solution)/shard_map/ppermute | solution.py:359
  11.9 0.7 add_select_fusion
  12.6 0.7 convert_bitcast_fusion
  13.9 0.7 collective-permute-start.6
  14.6 2.2 %collective-permute-done.left = bf16[192,640]{1,0:T(8,128)(2,1)S(1)} collective-permute-done((bf16[192,640]{1,0:T(8,128)(2,1)}, bf16[192,640]{1,0:T(8,128)(2,1)S(1)}, u32[]{:S(2)}, u32[]{:S(2)}) %collective-permute-start) | collective-permute-done | bytes 245792 | tf_op jit(solution)/shard_map/ppermute | solution.py:43
  16.8 0.6 shard_map.110
  17.4 2.1 %collective-permute-start.4 = (bf16[80,640]{1,0:T(8,128)(2,1)S(1)}, bf16[80,640]{1,0:T(8,128)(2,1)S(1)}, u32[]{:S(2)}, u32[]{:S(2)}) collective-permute-start(bf16[80,640]{1,0:T(8,128)(2,1)S(1)} %get-tuple-element.39), channel_id=1, source_target_pairs={{0,8},{8,16},{16,24},{24,0},{1,9},{9,17},{17,25},{25,1},{2,10},{10... | collective-permute-start | bytes 307208 | tf_op jit(solution)/shard_map/ppermute | solution.py:43
  19.4 1.8 %collective-permute-start.5 = (bf16[80,640]{1,0:T(8,128)(2,1)S(1)}, bf16[80,640]{1,0:T(8,128)(2,1)S(1)}, u32[]{:S(2)}, u32[]{:S(2)}) collective-permute-start(bf16[80,640]{1,0:T(8,128)(2,1)S(1)} %get-tuple-element.40), channel_id=1, source_target_pairs={{0,24},{8,0},{16,8},{24,16},{1,25},{9,1},{17,9},{25,17},{2,26},{10... | collective-permute-start | bytes 307208 | tf_op jit(solution)/shard_map/ppermute | solution.py:43
  21.5 0.7 shard_map.111.hidden_grad
  22.2 2.2 %collective-permute-done.4.left_side.left_e = bf16[80,640]{1,0:T(8,128)(2,1)S(1)} collective-permute-done((bf16[80,640]{1,0:T(8,128)(2,1)S(1)}, bf16[80,640]{1,0:T(8,128)(2,1)S(1)}, u32[]{:S(2)}, u32[]{:S(2)}) %collective-permute-start.4) | collective-permute-done | bytes 102432 | tf_op jit(solution)/shard_map/ppermute | solution.py:43
  24.4 1.0 collective-permute-done.5.right_side.right_e
  25.4 6.7 %shard_map.112 = (bf16[192,640]{1,0:T(8,128)(2,1)}, bf16[192,640]{1,0:T(8,128)(2,1)S(1)}, bf16[192,2176]{1,0:T(8,128)(2,1)S(1)}, bf16[192,1920]{1,0:T(8,128)(2,1...) custom-call(s32[5]{0:T(128)S(1)} %stack.23.place, ...), custom_call_target="tpu_custom_call" | custom-call | tf_op jit(solution)/shard_map/pallas_call | solution.py:344
  32.7 1.7 %collective-permute-done.14.other = bf16[192,1920]{1,0:T(8,128)(2,1)S(1)} collective-permute-done((bf16[192,1920]{1,0:T(8,128)(2,1)S(1)}, bf16[192,1920]{1,0:T(8,128)(2,1)S(1)}, u32[]{:S(2)}, u32[]{:S(2)}) %collective-permute-start.14) | collective-permute-done | bytes 737312 | tf_op jit(solution)/shard_map/ppermute | solution.py:43
  34.4 2.9 %shard_map.115 = (f32[320,640]{1,0:T(8,128)S(1)}, bf16[320,640]{1,0:T(8,128)(2,1)S(1)}, bf16[320,640]{1,0:T(8,128)(2,1)S(1)}, bf16[320,640]{1,0:T(8,128)(2,1)S(1)}) custom-call(s32[5]{0:T(128)S(1)} %stack.23.place, bf16[192,1920]{1,0:T(8,128)(2,1)S(1)} %get-tuple-element.48.mine, bf16[192,1920]{1,0:T(8,128)(2,1)S(1)} %collective-permute-done.14.other, ...), custom_call_target="tpu_custom_call" | custom-call | tf_op jit(solution)/shard_map/pallas_call | solution.py:344
  37.3 1.6 %collective-permute-start.15 = (bf16[320,640]{1,0:T(8,128)(2,1)S(1)}, bf16[320,640]{1,0:T(8,128)(2,1)S(1)}, u32[]{:S(2)}, u32[]{:S(2)}) collective-permute-start(bf16[320,640]{1,0:T(8,128)(2,1)S(1)} %get-tuple-element.53), channel_id=1, source_target_pairs={{0,2},{2,4},{4,6},{6,0},{1,3},{3,5},{5,7},{7,1},{8,10},{10,12},{12... | collective-permute-start | bytes 1228808 | tf_op jit(solution)/shard_map/ppermute | solution.py:43
  38.8 2.7 %collective-permute-start.16 = (bf16[320,640]{1,0:T(8,128)(2,1)S(1)}, bf16[320,640]{1,0:T(8,128)(2,1)S(1)}, u32[]{:S(2)}, u32[]{:S(2)}) collective-permute-start(bf16[320,640]{1,0:T(8,128)(2,1)S(1)} %get-tuple-element.54), channel_id=1, source_target_pairs={{0,4},{2,6},{4,0},{6,2},{1,5},{3,7},{5,1},{7,3},{8,12},{10,14},{12... | collective-permute-start | bytes 1228808 | tf_op jit(solution)/shard_map/ppermute | solution.py:43
  41.6 1.4 %collective-permute-start.17 = (bf16[320,640]{1,0:T(8,128)(2,1)S(1)}, bf16[320,640]{1,0:T(8,128)(2,1)S(1)}, u32[]{:S(2)}, u32[]{:S(2)}) collective-permute-start(bf16[320,640]{1,0:T(8,128)(2,1)S(1)} %get-tuple-element.55), channel_id=1, source_target_pairs={{0,6},{2,0},{4,2},{6,4},{1,7},{3,1},{5,3},{7,5},{8,14},{10,8},{12,... | collective-permute-start | bytes 1228808 | tf_op jit(solution)/shard_map/ppermute | solution.py:43
  43.0 1.9 %shard_map.117 = (f32[320,640]{1,0:T(8,128)S(1)}, bf16[320,640]{1,0:T(8,128)(2,1)S(1)}, bf16[320,640]{1,0:T(8,128)(2,1)S(1)}, bf16[320,640]{1,0:T(8,128)(2,1)S(1)}) custom-call(s32[5]{0:T(128)S(1)} %stack.23.place, bf16[192,2176]{1,0:T(8,128)(2,1)S(1)} %get-tuple-element.60.mine, bf16[192,2176]{1,0:T(8,128)(2,1)S(1)} %collective-permute-done.21.other), custom_call_target="tpu_custom_call" | custom-call | tf_op jit(solution)/shard_map/pallas_call | solution.py:344
  44.9 1.6 %collective-permute-start.22 = (bf16[320,640]{1,0:T(8,128)(2,1)S(1)}, bf16[320,640]{1,0:T(8,128)(2,1)S(1)}, u32[]{:S(2)}, u32[]{:S(2)}) collective-permute-start(bf16[320,640]{1,0:T(8,128)(2,1)S(1)} %get-tuple-element.63), channel_id=1, source_target_pairs={{0,64},{64,128},{128,192},{192,0},{1,65},{65,129},{129,193},{193,1... | collective-permute-start | bytes 1228808 | tf_op jit(solution)/shard_map/ppermute | solution.py:43
  46.5 0.9 collective-permute-start.23
  47.4 2.7 %collective-permute-done.15.r1 = bf16[320,640]{1,0:T(8,128)(2,1)S(1)} collective-permute-done((bf16[320,640]{1,0:T(8,128)(2,1)S(1)}, bf16[320,640]{1,0:T(8,128)(2,1)S(1)}, u32[]{:S(2)}, u32[]{:S(2)}) %collective-permute-start.15) | collective-permute-done | bytes 409632 | tf_op jit(solution)/shard_map/ppermute | solution.py:43
  50.4 9.4 %collective-permute-done.16.r2 = bf16[320,640]{1,0:T(8,128)(2,1)S(1)} collective-permute-done((bf16[320,640]{1,0:T(8,128)(2,1)S(1)}, bf16[320,640]{1,0:T(8,128)(2,1)S(1)}, u32[]{:S(2)}, u32[]{:S(2)}) %collective-permute-start.16) | collective-permute-done | bytes 409632 | tf_op jit(solution)/shard_map/ppermute | solution.py:43
  59.8 0.9 shard_map.116
  60.8 1.7 %collective-permute-start.18 = (bf16[80,640]{1,0:T(8,128)(2,1)S(1)}, bf16[80,640]{1,0:T(8,128)(2,1)S(1)}, u32[]{:S(2)}, u32[]{:S(2)}) collective-permute-start(bf16[80,640]{1,0:T(8,128)(2,1)S(1)} %get-tuple-element.57), channel_id=1, source_target_pairs={{0,64},{64,128},{128,192},{192,0},{1,65},{65,129},{129,193},{193,1... | collective-permute-start | bytes 307208 | tf_op jit(solution)/shard_map/ppermute | solution.py:43
  62.4 0.9 collective-permute-start.19
  63.3 2.5 %collective-permute-start.20 = (bf16[80,640]{1,0:T(8,128)(2,1)S(1)}, bf16[80,640]{1,0:T(8,128)(2,1)S(1)}, u32[]{:S(2)}, u32[]{:S(2)}) collective-permute-start(bf16[80,640]{1,0:T(8,128)(2,1)S(1)} %get-tuple-element.59), channel_id=1, source_target_pairs={{0,192},{64,0},{128,64},{192,128},{1,193},{65,1},{129,65},{193,129... | collective-permute-start | bytes 307208 | tf_op jit(solution)/shard_map/ppermute | solution.py:43
  65.8 2.6 %collective-permute-done.24.r3 = bf16[320,640]{1,0:T(8,128)(2,1)S(1)} collective-permute-done((bf16[320,640]{1,0:T(8,128)(2,1)S(1)}, bf16[320,640]{1,0:T(8,128)(2,1)S(1)}, u32[]{:S(2)}, u32[]{:S(2)}) %collective-permute-start.24) | collective-permute-done | bytes 409632 | tf_op jit(solution)/shard_map/ppermute | solution.py:43
  68.4 1.0 shard_map.118
  69.9 0.7 collective-permute-start.26
  70.6 2.1 %collective-permute-start.27 = (bf16[80,640]{1,0:T(8,128)(2,1)S(1)}, bf16[80,640]{1,0:T(8,128)(2,1)S(1)}, u32[]{:S(2)}, u32[]{:S(2)}) collective-permute-start(bf16[80,640]{1,0:T(8,128)(2,1)S(1)} %get-tuple-element.69), channel_id=1, source_target_pairs={{0,6},{2,0},{4,2},{6,4},{1,7},{3,1},{5,3},{7,5},{8,14},{10,8},{12,... | collective-permute-start | bytes 307208 | tf_op jit(solution)/shard_map/ppermute | solution.py:43
  72.7 4.9 %collective-permute-done.25.c1 = bf16[80,640]{1,0:T(8,128)(2,1)S(1)} collective-permute-done((bf16[80,640]{1,0:T(8,128)(2,1)S(1)}, bf16[80,640]{1,0:T(8,128)(2,1)S(1)}, u32[]{:S(2)}, u32[]{:S(2)}) %collective-permute-start.25) | collective-permute-done | bytes 102432 | tf_op jit(solution)/shard_map/ppermute | solution.py:43
  77.6 0.6 collective-permute-done.27.c3
  78.2 0.9 shard_map.119
  79.1 6.2 %all-to-all-start = ((bf16[8,20,640]{2,1,0:T(8,128)(2,1)}), bf16[8,20,640]{2,1,0:T(8,128)(2,1)S(1)}, u32[]{:S(2)}, u32[]{:S(2)}) async-start(bf16[8,20,640]{2,1,0:T(8,128)(2,1)} %shard_map.119), calls=%async_computation | async-start | bytes 491520 | tf_op jit(solution)/shard_map/all_to_all | solution.py:473
  85.3 3.8 %collective-permute-start.9 = (bf16[192,640]{1,0:T(8,128)(2,1)S(1)}, bf16[192,640]{1,0:T(8,128)(2,1)S(1)}, u32[]{:S(2)}, u32[]{:S(2)}) collective-permute-start(bf16[192,640]{1,0:T(8,128)(2,1)S(1)} %get-tuple-element.43.tile), channel_id=1, source_target_pairs={{0,24},{8,0},{16,8},{24,16},{1,25},{9,1},{17,9},{25,17},{2,26},{10... | collective-permute-start | bytes 737288 | tf_op jit(solution)/shard_map/ppermute | solution.py:43
  89.1 1.9 %collective-permute-start.10 = (bf16[40,640]{1,0:T(8,128)(2,1)S(1)}, bf16[40,640]{1,0:T(8,128)(2,1)S(1)}, u32[]{:S(2)}, u32[]{:S(2)}) collective-permute-start(bf16[40,640]{1,0:T(8,128)(2,1)S(1)} %get-tuple-element.44), channel_id=1, source_target_pairs={{0,32},{32,64},{64,96},{96,128},{128,160},{160,192},{192,224},{1,3... | collective-permute-start | bytes 153608 | tf_op jit(solution)/shard_map/ppermute | solution.py:358
  91.0 3.6 %collective-permute-start.11 = (bf16[40,640]{1,0:T(8,128)(2,1)S(1)}, bf16[40,640]{1,0:T(8,128)(2,1)S(1)}, u32[]{:S(2)}, u32[]{:S(2)}) collective-permute-start(bf16[40,640]{1,0:T(8,128)(2,1)S(1)} %get-tuple-element.45), channel_id=1, source_target_pairs={{32,0},{64,32},{96,64},{128,96},{160,128},{192,160},{224,192},{33,... | collective-permute-start | bytes 153608 | tf_op jit(solution)/shard_map/ppermute | solution.py:359
  94.7 1.7 %collective-permute-done.11.bottom = bf16[40,640]{1,0:T(8,128)(2,1)S(1)} collective-permute-done((bf16[40,640]{1,0:T(8,128)(2,1)S(1)}, bf16[40,640]{1,0:T(8,128)(2,1)S(1)}, u32[]{:S(2)}, u32[]{:S(2)}) %collective-permute-start.11) | collective-permute-done | bytes 51232 | tf_op jit(solution)/shard_map/ppermute | solution.py:359
  96.4 1.2 %collective-permute-done.9.right = bf16[192,640]{1,0:T(8,128)(2,1)S(1)} collective-permute-done((bf16[192,640]{1,0:T(8,128)(2,1)S(1)}, bf16[192,640]{1,0:T(8,128)(2,1)S(1)}, u32[]{:S(2)}, u32[]{:S(2)}) %collective-permute-start.9) | collective-permute-done | bytes 245792 | tf_op jit(solution)/shard_map/ppermute | solution.py:43
  97.7 6.8 %collective-permute-done.8.left = bf16[192,640]{1,0:T(8,128)(2,1)S(1)} collective-permute-done((bf16[192,640]{1,0:T(8,128)(2,1)S(1)}, bf16[192,640]{1,0:T(8,128)(2,1)S(1)}, u32[]{:S(2)}, u32[]{:S(2)}) %collective-permute-start.8) | collective-permute-done | bytes 245792 | tf_op jit(solution)/shard_map/ppermute | solution.py:43
  104.5 0.6 shard_map.113
  105.1 3.8 %collective-permute-start.13 = (bf16[64,640]{1,0:T(8,128)(2,1)S(1)}, bf16[64,640]{1,0:T(8,128)(2,1)S(1)}, u32[]{:S(2)}, u32[]{:S(2)}) collective-permute-start(bf16[64,640]{1,0:T(8,128)(2,1)S(1)} %get-tuple-element.47), channel_id=1, source_target_pairs={{0,24},{8,0},{16,8},{24,16},{1,25},{9,1},{17,9},{25,17},{2,26},{10... | collective-permute-start | bytes 245768 | tf_op jit(solution)/shard_map/ppermute | solution.py:43
  108.9 2.4 %collective-permute-done.12.left_side = bf16[64,640]{1,0:T(8,128)(2,1)S(1)} collective-permute-done((bf16[64,640]{1,0:T(8,128)(2,1)S(1)}, bf16[64,640]{1,0:T(8,128)(2,1)S(1)}, u32[]{:S(2)}, u32[]{:S(2)}) %collective-permute-start.12) | collective-permute-done | bytes 81952 | tf_op jit(solution)/shard_map/ppermute | solution.py:43
  111.4 4.5 %shard_map.114 = bf16[192,640]{1,0:T(8,128)(2,1)} custom-call(s32[5]{0:T(128)S(1)} %stack.23.place, bf16[192,640]{1,0:T(8,128)(2,1)S(1)} %get-tuple-element.43.tile, bf16[192,640]{1,0:T(8,128)(2,1)S(1)} %collective-permute-done.8.left, bf16[192,640]{1,0:T(8,128)(2,1)S(1)} %collective-permute-done.9.right, bf16[40,640]{1,0:T(8,128)(2,1)S(1)} %collective-permute-done.10.top, ...), custom_call_target="tpu_custom_call" | custom-call | tf_op jit(solution)/shard_map/pallas_call | solution.py:344
  115.8 0.6 shard_map.120
  (41 shorter events, 2.4 us)
Async XLA Ops:
  0.6 20.8 %copy-start.1 = (bf16[1,12,16,640]{3,2,1,0:T(8,128)(2,1)S(1)}, bf16[1,12,16,640]{3,2,1,0:T(8,128)(2,1)}, u32[]{:S(2)}) copy-start(bf16[1,12,16,640]{3,2,1,0:T(8,128)(2,1)} %param.13) | copy-start | bytes 737284
  0.6 20.8 %copy-start = (bf16[1280,640]{1,0:T(8,128)(2,1)S(1)}, bf16[1280,640]{1,0:T(8,128)(2,1)}, u32[]{:S(2)}) copy-start(bf16[1280,640]{1,0:T(8,128)(2,1)} %out_hbm.1) | copy-start | bytes 4915204
  0.7 13.9 %collective-permute-start.1 = (bf16[192,640]{1,0:T(8,128)(2,1)}, bf16[192,640]{1,0:T(8,128)(2,1)S(1)}, u32[]{:S(2)}, u32[]{:S(2)}) collective-permute-start(bf16[192,640]{1,0:T(8,128)(2,1)} %bitcast.22), channel_id=1, source_target_pairs={{0,24},{8,0},{16,8},{24,16},{1,25},{9,1},{17,9},{25,17},{2,26},{10... | collective-permute-start | bytes 737288 | tf_op jit(solution)/shard_map/ppermute | solution.py:43
  5.4 11.4 %collective-permute-start = (bf16[192,640]{1,0:T(8,128)(2,1)}, bf16[192,640]{1,0:T(8,128)(2,1)S(1)}, u32[]{:S(2)}, u32[]{:S(2)}) collective-permute-start(bf16[192,640]{1,0:T(8,128)(2,1)} %bitcast.23), channel_id=1, source_target_pairs={{0,8},{8,16},{16,24},{24,0},{1,9},{9,17},{17,25},{25,1},{2,10},{10... | collective-permute-start | bytes 737288 | tf_op jit(solution)/shard_map/ppermute | solution.py:43
  6.2 7.7 %collective-permute-start.2 = (bf16[32,640]{1,0:T(8,128)(2,1)S(1)}, bf16[32,640]{1,0:T(8,128)(2,1)S(1)}, u32[]{:S(2)}, u32[]{:S(2)}) collective-permute-start(bf16[32,640]{1,0:T(8,128)(2,1)S(1)} %bitcast.30), channel_id=1, source_target_pairs={{0,32},{32,64},{64,96},{96,128},{128,160},{160,192},{192,224},{1,3... | collective-permute-start | bytes 122888 | tf_op jit(solution)/shard_map/ppermute | solution.py:358
  8.1 6.4 %collective-permute-start.3 = (bf16[32,640]{1,0:T(8,128)(2,1)S(1)}, bf16[32,640]{1,0:T(8,128)(2,1)S(1)}, u32[]{:S(2)}, u32[]{:S(2)}) collective-permute-start(bf16[32,640]{1,0:T(8,128)(2,1)S(1)} %bitcast.29), channel_id=1, source_target_pairs={{32,0},{64,32},{96,64},{128,96},{160,128},{192,160},{224,192},{33,... | collective-permute-start | bytes 122888 | tf_op jit(solution)/shard_map/ppermute | solution.py:359
  11.8 10.4 %collective-permute-start.7 = (bf16[192,640]{1,0:T(8,128)(2,1)}, bf16[192,640]{1,0:T(8,128)(2,1)S(1)}, u32[]{:S(2)}, u32[]{:S(2)}) collective-permute-start(bf16[192,640]{1,0:T(8,128)(2,1)} %bitcast.18), channel_id=1, source_target_pairs={{0,32},{32,0},{1,33},{33,1},{2,34},{34,2},{3,35},{35,3},{4,36},{36... | collective-permute-start | bytes 737288 | tf_op jit(solution)/shard_map/ppermute | solution.py:43
  13.9 8.3 %collective-permute-start.6 = (bf16[16,640]{1,0:T(8,128)(2,1)S(1)}, bf16[16,640]{1,0:T(8,128)(2,1)S(1)}, u32[]{:S(2)}, u32[]{:S(2)}) collective-permute-start(bf16[16,640]{1,0:T(8,128)(2,1)S(1)} %pad.4.rest_0_.own_e), channel_id=1, source_target_pairs={{0,16},{8,24},{16,0},{24,8},{1,17},{9,25},{17,1},{25,9},{2,18},{10... | collective-permute-start | bytes 61448 | tf_op jit(solution)/shard_map/ppermute | solution.py:43
  17.4 7.0 %collective-permute-start.4 = (bf16[80,640]{1,0:T(8,128)(2,1)S(1)}, bf16[80,640]{1,0:T(8,128)(2,1)S(1)}, u32[]{:S(2)}, u32[]{:S(2)}) collective-permute-start(bf16[80,640]{1,0:T(8,128)(2,1)S(1)} %get-tuple-element.39), channel_id=1, source_target_pairs={{0,8},{8,16},{16,24},{24,0},{1,9},{9,17},{17,25},{25,1},{2,10},{10... | collective-permute-start | bytes 307208 | tf_op jit(solution)/shard_map/ppermute | solution.py:43
  19.4 5.9 %collective-permute-start.5 = (bf16[80,640]{1,0:T(8,128)(2,1)S(1)}, bf16[80,640]{1,0:T(8,128)(2,1)S(1)}, u32[]{:S(2)}, u32[]{:S(2)}) collective-permute-start(bf16[80,640]{1,0:T(8,128)(2,1)S(1)} %get-tuple-element.40), channel_id=1, source_target_pairs={{0,24},{8,0},{16,8},{24,16},{1,25},{9,1},{17,9},{25,17},{2,26},{10... | collective-permute-start | bytes 307208 | tf_op jit(solution)/shard_map/ppermute | solution.py:43
  21.5 3.9 %copy-start.2 = (bf16[1,12,16,640]{3,2,1,0:T(8,128)(2,1)S(1)}, bf16[1,12,16,640]{3,2,1,0:T(8,128)(2,1)}, u32[]{:S(2)}) copy-start(bf16[1,12,16,640]{3,2,1,0:T(8,128)(2,1)} %param.7) | copy-start | bytes 737284
  32.1 2.3 %collective-permute-start.14 = (bf16[192,1920]{1,0:T(8,128)(2,1)S(1)}, bf16[192,1920]{1,0:T(8,128)(2,1)S(1)}, u32[]{:S(2)}, u32[]{:S(2)}) collective-permute-start(bf16[192,1920]{1,0:T(8,128)(2,1)S(1)} %get-tuple-element.49), channel_id=1, source_target_pairs={{0,32},{32,0},{1,33},{33,1},{2,34},{34,2},{3,35},{35,3},{4,36},{36... | collective-permute-start | bytes 2211848 | tf_op jit(solution)/shard_map/ppermute | solution.py:43
  32.2 10.8 %collective-permute-start.21 = (bf16[192,2176]{1,0:T(8,128)(2,1)S(1)}, bf16[192,2176]{1,0:T(8,128)(2,1)S(1)}, u32[]{:S(2)}, u32[]{:S(2)}) collective-permute-start(bf16[192,2176]{1,0:T(8,128)(2,1)S(1)} %get-tuple-element.61), channel_id=1, source_target_pairs={{0,32},{32,0},{1,33},{33,1},{2,34},{34,2},{3,35},{35,3},{4,36},{36... | collective-permute-start | bytes 2506760 | tf_op jit(solution)/shard_map/ppermute | solution.py:43
  37.3 12.8 %collective-permute-start.15 = (bf16[320,640]{1,0:T(8,128)(2,1)S(1)}, bf16[320,640]{1,0:T(8,128)(2,1)S(1)}, u32[]{:S(2)}, u32[]{:S(2)}) collective-permute-start(bf16[320,640]{1,0:T(8,128)(2,1)S(1)} %get-tuple-element.53), channel_id=1, source_target_pairs={{0,2},{2,4},{4,6},{6,0},{1,3},{3,5},{5,7},{7,1},{8,10},{10,12},{12... | collective-permute-start | bytes 1228808 | tf_op jit(solution)/shard_map/ppermute | solution.py:43
  38.8 21.0 %collective-permute-start.16 = (bf16[320,640]{1,0:T(8,128)(2,1)S(1)}, bf16[320,640]{1,0:T(8,128)(2,1)S(1)}, u32[]{:S(2)}, u32[]{:S(2)}) collective-permute-start(bf16[320,640]{1,0:T(8,128)(2,1)S(1)} %get-tuple-element.54), channel_id=1, source_target_pairs={{0,4},{2,6},{4,0},{6,2},{1,5},{3,7},{5,1},{7,3},{8,12},{10,14},{12... | collective-permute-start | bytes 1228808 | tf_op jit(solution)/shard_map/ppermute | solution.py:43
  41.6 18.3 %collective-permute-start.17 = (bf16[320,640]{1,0:T(8,128)(2,1)S(1)}, bf16[320,640]{1,0:T(8,128)(2,1)S(1)}, u32[]{:S(2)}, u32[]{:S(2)}) collective-permute-start(bf16[320,640]{1,0:T(8,128)(2,1)S(1)} %get-tuple-element.55), channel_id=1, source_target_pairs={{0,6},{2,0},{4,2},{6,4},{1,7},{3,1},{5,3},{7,5},{8,14},{10,8},{12,... | collective-permute-start | bytes 1228808 | tf_op jit(solution)/shard_map/ppermute | solution.py:43
  44.9 18.4 %collective-permute-start.22 = (bf16[320,640]{1,0:T(8,128)(2,1)S(1)}, bf16[320,640]{1,0:T(8,128)(2,1)S(1)}, u32[]{:S(2)}, u32[]{:S(2)}) collective-permute-start(bf16[320,640]{1,0:T(8,128)(2,1)S(1)} %get-tuple-element.63), channel_id=1, source_target_pairs={{0,64},{64,128},{128,192},{192,0},{1,65},{65,129},{129,193},{193,1... | collective-permute-start | bytes 1228808 | tf_op jit(solution)/shard_map/ppermute | solution.py:43
  46.5 19.2 %collective-permute-start.23 = (bf16[320,640]{1,0:T(8,128)(2,1)S(1)}, bf16[320,640]{1,0:T(8,128)(2,1)S(1)}, u32[]{:S(2)}, u32[]{:S(2)}) collective-permute-start(bf16[320,640]{1,0:T(8,128)(2,1)S(1)} %get-tuple-element.64), channel_id=1, source_target_pairs={{0,128},{64,192},{128,0},{192,64},{1,129},{65,193},{129,1},{193,65... | collective-permute-start | bytes 1228808 | tf_op jit(solution)/shard_map/ppermute | solution.py:43
  50.1 18.3 %collective-permute-start.24 = (bf16[320,640]{1,0:T(8,128)(2,1)S(1)}, bf16[320,640]{1,0:T(8,128)(2,1)S(1)}, u32[]{:S(2)}, u32[]{:S(2)}) collective-permute-start(bf16[320,640]{1,0:T(8,128)(2,1)S(1)} %get-tuple-element.65), channel_id=1, source_target_pairs={{0,192},{64,0},{128,64},{192,128},{1,193},{65,1},{129,65},{193,129... | collective-permute-start | bytes 1228808 | tf_op jit(solution)/shard_map/ppermute | solution.py:43
  60.8 9.8 %collective-permute-start.18 = (bf16[80,640]{1,0:T(8,128)(2,1)S(1)}, bf16[80,640]{1,0:T(8,128)(2,1)S(1)}, u32[]{:S(2)}, u32[]{:S(2)}) collective-permute-start(bf16[80,640]{1,0:T(8,128)(2,1)S(1)} %get-tuple-element.57), channel_id=1, source_target_pairs={{0,64},{64,128},{128,192},{192,0},{1,65},{65,129},{129,193},{193,1... | collective-permute-start | bytes 307208 | tf_op jit(solution)/shard_map/ppermute | solution.py:43
  62.4 10.3 %collective-permute-start.19 = (bf16[80,640]{1,0:T(8,128)(2,1)S(1)}, bf16[80,640]{1,0:T(8,128)(2,1)S(1)}, u32[]{:S(2)}, u32[]{:S(2)}) collective-permute-start(bf16[80,640]{1,0:T(8,128)(2,1)S(1)} %get-tuple-element.58), channel_id=1, source_target_pairs={{0,128},{64,192},{128,0},{192,64},{1,129},{65,193},{129,1},{193,65... | collective-permute-start | bytes 307208 | tf_op jit(solution)/shard_map/ppermute | solution.py:43
  63.3 9.4 %collective-permute-start.20 = (bf16[80,640]{1,0:T(8,128)(2,1)S(1)}, bf16[80,640]{1,0:T(8,128)(2,1)S(1)}, u32[]{:S(2)}, u32[]{:S(2)}) collective-permute-start(bf16[80,640]{1,0:T(8,128)(2,1)S(1)} %get-tuple-element.59), channel_id=1, source_target_pairs={{0,192},{64,0},{128,64},{192,128},{1,193},{65,1},{129,65},{193,129... | collective-permute-start | bytes 307208 | tf_op jit(solution)/shard_map/ppermute | solution.py:43
  69.4 8.2 %collective-permute-start.25 = (bf16[80,640]{1,0:T(8,128)(2,1)S(1)}, bf16[80,640]{1,0:T(8,128)(2,1)S(1)}, u32[]{:S(2)}, u32[]{:S(2)}) collective-permute-start(bf16[80,640]{1,0:T(8,128)(2,1)S(1)} %get-tuple-element.67), channel_id=1, source_target_pairs={{0,2},{2,4},{4,6},{6,0},{1,3},{3,5},{5,7},{7,1},{8,10},{10,12},{12... | collective-permute-start | bytes 307208 | tf_op jit(solution)/shard_map/ppermute | solution.py:43
  69.9 7.7 %collective-permute-start.26 = (bf16[80,640]{1,0:T(8,128)(2,1)S(1)}, bf16[80,640]{1,0:T(8,128)(2,1)S(1)}, u32[]{:S(2)}, u32[]{:S(2)}) collective-permute-start(bf16[80,640]{1,0:T(8,128)(2,1)S(1)} %get-tuple-element.68), channel_id=1, source_target_pairs={{0,4},{2,6},{4,0},{6,2},{1,5},{3,7},{5,1},{7,3},{8,12},{10,14},{12... | collective-permute-start | bytes 307208 | tf_op jit(solution)/shard_map/ppermute | solution.py:43
  70.6 7.6 %collective-permute-start.27 = (bf16[80,640]{1,0:T(8,128)(2,1)S(1)}, bf16[80,640]{1,0:T(8,128)(2,1)S(1)}, u32[]{:S(2)}, u32[]{:S(2)}) collective-permute-start(bf16[80,640]{1,0:T(8,128)(2,1)S(1)} %get-tuple-element.69), channel_id=1, source_target_pairs={{0,6},{2,0},{4,2},{6,4},{1,7},{3,1},{5,3},{7,5},{8,14},{10,8},{12,... | collective-permute-start | bytes 307208 | tf_op jit(solution)/shard_map/ppermute | solution.py:43
  79.1 36.8 %all-to-all-start = ((bf16[8,20,640]{2,1,0:T(8,128)(2,1)}), bf16[8,20,640]{2,1,0:T(8,128)(2,1)S(1)}, u32[]{:S(2)}, u32[]{:S(2)}) async-start(bf16[8,20,640]{2,1,0:T(8,128)(2,1)} %shard_map.119), calls=%async_computation | async-start | bytes 491520 | tf_op jit(solution)/shard_map/all_to_all | solution.py:473
  85.3 12.4 %collective-permute-start.9 = (bf16[192,640]{1,0:T(8,128)(2,1)S(1)}, bf16[192,640]{1,0:T(8,128)(2,1)S(1)}, u32[]{:S(2)}, u32[]{:S(2)}) collective-permute-start(bf16[192,640]{1,0:T(8,128)(2,1)S(1)} %get-tuple-element.43.tile), channel_id=1, source_target_pairs={{0,24},{8,0},{16,8},{24,16},{1,25},{9,1},{17,9},{25,17},{2,26},{10... | collective-permute-start | bytes 737288 | tf_op jit(solution)/shard_map/ppermute | solution.py:43
  89.1 15.3 %collective-permute-start.8 = (bf16[192,640]{1,0:T(8,128)(2,1)S(1)}, bf16[192,640]{1,0:T(8,128)(2,1)S(1)}, u32[]{:S(2)}, u32[]{:S(2)}) collective-permute-start(bf16[192,640]{1,0:T(8,128)(2,1)S(1)} %get-tuple-element.43.tile), channel_id=1, source_target_pairs={{0,8},{8,16},{16,24},{24,0},{1,9},{9,17},{17,25},{25,1},{2,10},{10... | collective-permute-start | bytes 737288 | tf_op jit(solution)/shard_map/ppermute | solution.py:43
  89.1 5.6 %collective-permute-start.10 = (bf16[40,640]{1,0:T(8,128)(2,1)S(1)}, bf16[40,640]{1,0:T(8,128)(2,1)S(1)}, u32[]{:S(2)}, u32[]{:S(2)}) collective-permute-start(bf16[40,640]{1,0:T(8,128)(2,1)S(1)} %get-tuple-element.44), channel_id=1, source_target_pairs={{0,32},{32,64},{64,96},{96,128},{128,160},{160,192},{192,224},{1,3... | collective-permute-start | bytes 153608 | tf_op jit(solution)/shard_map/ppermute | solution.py:358
  91.0 5.4 %collective-permute-start.11 = (bf16[40,640]{1,0:T(8,128)(2,1)S(1)}, bf16[40,640]{1,0:T(8,128)(2,1)S(1)}, u32[]{:S(2)}, u32[]{:S(2)}) collective-permute-start(bf16[40,640]{1,0:T(8,128)(2,1)S(1)} %get-tuple-element.45), channel_id=1, source_target_pairs={{32,0},{64,32},{96,64},{128,96},{160,128},{192,160},{224,192},{33,... | collective-permute-start | bytes 153608 | tf_op jit(solution)/shard_map/ppermute | solution.py:359
  105.0 6.3 %collective-permute-start.12 = (bf16[64,640]{1,0:T(8,128)(2,1)S(1)}, bf16[64,640]{1,0:T(8,128)(2,1)S(1)}, u32[]{:S(2)}, u32[]{:S(2)}) collective-permute-start(bf16[64,640]{1,0:T(8,128)(2,1)S(1)} %get-tuple-element.46), channel_id=1, source_target_pairs={{0,8},{8,16},{16,24},{24,0},{1,9},{9,17},{17,25},{25,1},{2,10},{10... | collective-permute-start | bytes 245768 | tf_op jit(solution)/shard_map/ppermute | solution.py:43
  105.1 6.2 %collective-permute-start.13 = (bf16[64,640]{1,0:T(8,128)(2,1)S(1)}, bf16[64,640]{1,0:T(8,128)(2,1)S(1)}, u32[]{:S(2)}, u32[]{:S(2)}) collective-permute-start(bf16[64,640]{1,0:T(8,128)(2,1)S(1)} %get-tuple-element.47), channel_id=1, source_target_pairs={{0,24},{8,0},{16,8},{24,16},{1,25},{9,1},{17,9},{25,17},{2,26},{10... | collective-permute-start | bytes 245768 | tf_op jit(solution)/shard_map/ppermute | solution.py:43

commit v5 on v4

--- a/solution.py
+++ b/solution.py
@@ -269,9 +269,10 @@
     mlp = m0[...] + m1[...].astype(f32) + m2[...].astype(f32) + m3[...].astype(f32)
     conv = c0[...] + c1[...].astype(f32) + c2[...].astype(f32) + c3[...].astype(f32)
     for to in range(8):
-        o[to, 0:10, :] = conv[to * 10 : to * 10 + 10, :].astype(bf16)
-        o[to, 10:15, :] = mlp[to * 5 : to * 5 + 5, :].astype(bf16)
-        o[to, 15:20, :] = mlp[40 + to * 5 : 45 + to * 5, :].astype(bf16)
+        rows = to % 4 * 2 + to // 4
+        o[to, 0:10, :] = conv[rows * 10 : rows * 10 + 10, :].astype(bf16)
+        o[to, 10:15, :] = mlp[rows * 5 : rows * 5 + 5, :].astype(bf16)
+        o[to, 15:20, :] = mlp[40 + rows * 5 : 45 + rows * 5, :].astype(bf16)
 
 
 def final_kernel(parts, conv, w_in, w_out):
@@ -470,7 +471,7 @@
         own_e, left_side, right_side, far_e, in_hbm=(conv_weight,),
     )
     packed = call(pack_kernel, struct((8, 20, EMBED), bf16), [], 4, None, *m, *c)
-    parts = lax.all_to_all(packed, ("zlo", "zhi"), split_axis=0, concat_axis=0, tiled=True)
+    parts = lax.all_to_all(packed, ("zhi", "zlo"), split_axis=0, concat_axis=0, tiled=True)
     conv_grad, in_grad, out_grad = call(
         final_kernel,
         (struct((10, EMBED), f32), struct((5, EMBED), f32), struct((5, EMBED), f32)),

time: 117 us -> 117 us (level)
  no operation moved by 1% of the time
where the time goes in v5:
time: 117 us; the launch traced here: 116 us
  starting transfers between devices  52 us (44%)
  waiting for transfers between devices  39.5 us (34%)
  Pallas kernels  21.1 us (18%)
  other arithmetic  1.99 us (2%)
    ppermute x24, waiting for transfers between devices, shift(): lax.ppermute(block, axis, [(i, (i + step) % count) for i in range(count)])  37.8 us
    ppermute x24, starting transfers between devices, shift(): lax.ppermute(block, axis, [(i, (i + step) % count) for i in range(count)])  34.6 us
    pallas_call x11, Pallas kernels, call(): pl.pallas_call(kernel, out_shape=outs, in_specs=in_specs, scratch_shapes=...  21.1 us
    ppermute x2, starting transfers between devices, neighbours(): bottom = lax.ppermute(to_down, LAT, backward)  7.28 us
    all_to_all x1, starting transfers between devices, block(): lax.all_to_all(packed, ('zhi', 'zlo'), split_axis=0, concat_axis=0, tiled...  6.22 us
    ppermute x2, starting transfers between devices, neighbours(): top = lax.ppermute(to_up, LAT, forward)  3.83 us
  transfers between devices with their start and end apart: 29, of which 13 were waited for; matrix products, arithmetic and copies ran while one was open for 3% of the time, Pallas kernels for 11%

profile of v5, /device:TPU:8, one launch (start us, length us, event | category | flops | bytes accessed | tf_op | source)
XLA Modules:
  0.0 116.5 jit_solution(11342356203707734271)
XLA Ops:
  0.7 4.7 %collective-permute-start.1 = (bf16[192,640]{1,0:T(8,128)(2,1)}, bf16[192,640]{1,0:T(8,128)(2,1)S(1)}, u32[]{:S(2)}, u32[]{:S(2)}) collective-permute-start(bf16[192,640]{1,0:T(8,128)(2,1)} %bitcast.22), channel_id=1, source_target_pairs={{0,24},{8,0},{16,8},{24,16},{1,25},{9,1},{17,9},{25,17},{2,26},{10... | collective-permute-start | bytes 737288 | tf_op jit(solution)/shard_map/ppermute | solution.py:43
  5.4 0.9 fusion.21
  6.2 1.9 %collective-permute-start.2 = (bf16[32,640]{1,0:T(8,128)(2,1)S(1)}, bf16[32,640]{1,0:T(8,128)(2,1)S(1)}, u32[]{:S(2)}, u32[]{:S(2)}) collective-permute-start(bf16[32,640]{1,0:T(8,128)(2,1)S(1)} %bitcast.30), channel_id=1, source_target_pairs={{0,32},{32,64},{64,96},{96,128},{128,160},{160,192},{192,224},{1,3... | collective-permute-start | bytes 122888 | tf_op jit(solution)/shard_map/ppermute | solution.py:359
  8.1 3.6 %collective-permute-start.3 = (bf16[32,640]{1,0:T(8,128)(2,1)S(1)}, bf16[32,640]{1,0:T(8,128)(2,1)S(1)}, u32[]{:S(2)}, u32[]{:S(2)}) collective-permute-start(bf16[32,640]{1,0:T(8,128)(2,1)S(1)} %bitcast.29), channel_id=1, source_target_pairs={{32,0},{64,32},{96,64},{128,96},{160,128},{192,160},{224,192},{33,... | collective-permute-start | bytes 122888 | tf_op jit(solution)/shard_map/ppermute | solution.py:360
  11.9 0.7 add_select_fusion
  12.6 0.7 convert_bitcast_fusion
  13.9 0.7 collective-permute-start.6
  14.6 2.2 %collective-permute-done.left = bf16[192,640]{1,0:T(8,128)(2,1)S(1)} collective-permute-done((bf16[192,640]{1,0:T(8,128)(2,1)}, bf16[192,640]{1,0:T(8,128)(2,1)S(1)}, u32[]{:S(2)}, u32[]{:S(2)}) %collective-permute-start) | collective-permute-done | bytes 245792 | tf_op jit(solution)/shard_map/ppermute | solution.py:43
  16.8 0.6 shard_map.110
  17.4 2.1 %collective-permute-start.4 = (bf16[80,640]{1,0:T(8,128)(2,1)S(1)}, bf16[80,640]{1,0:T(8,128)(2,1)S(1)}, u32[]{:S(2)}, u32[]{:S(2)}) collective-permute-start(bf16[80,640]{1,0:T(8,128)(2,1)S(1)} %get-tuple-element.39), channel_id=1, source_target_pairs={{0,8},{8,16},{16,24},{24,0},{1,9},{9,17},{17,25},{25,1},{2,10},{10... | collective-permute-start | bytes 307208 | tf_op jit(solution)/shard_map/ppermute | solution.py:43
  19.4 1.8 %collective-permute-start.5 = (bf16[80,640]{1,0:T(8,128)(2,1)S(1)}, bf16[80,640]{1,0:T(8,128)(2,1)S(1)}, u32[]{:S(2)}, u32[]{:S(2)}) collective-permute-start(bf16[80,640]{1,0:T(8,128)(2,1)S(1)} %get-tuple-element.40), channel_id=1, source_target_pairs={{0,24},{8,0},{16,8},{24,16},{1,25},{9,1},{17,9},{25,17},{2,26},{10... | collective-permute-start | bytes 307208 | tf_op jit(solution)/shard_map/ppermute | solution.py:43
  21.5 0.7 shard_map.111.hidden_grad
  22.2 2.2 %collective-permute-done.4.left_side.left_e = bf16[80,640]{1,0:T(8,128)(2,1)S(1)} collective-permute-done((bf16[80,640]{1,0:T(8,128)(2,1)S(1)}, bf16[80,640]{1,0:T(8,128)(2,1)S(1)}, u32[]{:S(2)}, u32[]{:S(2)}) %collective-permute-start.4) | collective-permute-done | bytes 102432 | tf_op jit(solution)/shard_map/ppermute | solution.py:43
  24.4 1.0 collective-permute-done.5.right_side.right_e
  25.4 6.7 %shard_map.112 = (bf16[192,640]{1,0:T(8,128)(2,1)}, bf16[192,640]{1,0:T(8,128)(2,1)S(1)}, bf16[192,2176]{1,0:T(8,128)(2,1)S(1)}, bf16[192,1920]{1,0:T(8,128)(2,1...) custom-call(s32[5]{0:T(128)S(1)} %stack.23.place, ...), custom_call_target="tpu_custom_call" | custom-call | tf_op jit(solution)/shard_map/pallas_call | solution.py:345
  32.7 1.7 %collective-permute-done.14.other = bf16[192,1920]{1,0:T(8,128)(2,1)S(1)} collective-permute-done((bf16[192,1920]{1,0:T(8,128)(2,1)S(1)}, bf16[192,1920]{1,0:T(8,128)(2,1)S(1)}, u32[]{:S(2)}, u32[]{:S(2)}) %collective-permute-start.14) | collective-permute-done | bytes 737312 | tf_op jit(solution)/shard_map/ppermute | solution.py:43
  34.4 2.9 %shard_map.115 = (f32[320,640]{1,0:T(8,128)S(1)}, bf16[320,640]{1,0:T(8,128)(2,1)S(1)}, bf16[320,640]{1,0:T(8,128)(2,1)S(1)}, bf16[320,640]{1,0:T(8,128)(2,1)S(1)}) custom-call(s32[5]{0:T(128)S(1)} %stack.23.place, bf16[192,1920]{1,0:T(8,128)(2,1)S(1)} %get-tuple-element.48.mine, bf16[192,1920]{1,0:T(8,128)(2,1)S(1)} %collective-permute-done.14.other, ...), custom_call_target="tpu_custom_call" | custom-call | tf_op jit(solution)/shard_map/pallas_call | solution.py:345
  37.3 1.6 %collective-permute-start.15 = (bf16[320,640]{1,0:T(8,128)(2,1)S(1)}, bf16[320,640]{1,0:T(8,128)(2,1)S(1)}, u32[]{:S(2)}, u32[]{:S(2)}) collective-permute-start(bf16[320,640]{1,0:T(8,128)(2,1)S(1)} %get-tuple-element.53), channel_id=1, source_target_pairs={{0,2},{2,4},{4,6},{6,0},{1,3},{3,5},{5,7},{7,1},{8,10},{10,12},{12... | collective-permute-start | bytes 1228808 | tf_op jit(solution)/shard_map/ppermute | solution.py:43
  38.8 2.7 %collective-permute-start.16 = (bf16[320,640]{1,0:T(8,128)(2,1)S(1)}, bf16[320,640]{1,0:T(8,128)(2,1)S(1)}, u32[]{:S(2)}, u32[]{:S(2)}) collective-permute-start(bf16[320,640]{1,0:T(8,128)(2,1)S(1)} %get-tuple-element.54), channel_id=1, source_target_pairs={{0,4},{2,6},{4,0},{6,2},{1,5},{3,7},{5,1},{7,3},{8,12},{10,14},{12... | collective-permute-start | bytes 1228808 | tf_op jit(solution)/shard_map/ppermute | solution.py:43
  41.6 1.4 %collective-permute-start.17 = (bf16[320,640]{1,0:T(8,128)(2,1)S(1)}, bf16[320,640]{1,0:T(8,128)(2,1)S(1)}, u32[]{:S(2)}, u32[]{:S(2)}) collective-permute-start(bf16[320,640]{1,0:T(8,128)(2,1)S(1)} %get-tuple-element.55), channel_id=1, source_target_pairs={{0,6},{2,0},{4,2},{6,4},{1,7},{3,1},{5,3},{7,5},{8,14},{10,8},{12,... | collective-permute-start | bytes 1228808 | tf_op jit(solution)/shard_map/ppermute | solution.py:43
  43.0 1.9 %shard_map.117 = (f32[320,640]{1,0:T(8,128)S(1)}, bf16[320,640]{1,0:T(8,128)(2,1)S(1)}, bf16[320,640]{1,0:T(8,128)(2,1)S(1)}, bf16[320,640]{1,0:T(8,128)(2,1)S(1)}) custom-call(s32[5]{0:T(128)S(1)} %stack.23.place, bf16[192,2176]{1,0:T(8,128)(2,1)S(1)} %get-tuple-element.60.mine, bf16[192,2176]{1,0:T(8,128)(2,1)S(1)} %collective-permute-done.21.other), custom_call_target="tpu_custom_call" | custom-call | tf_op jit(solution)/shard_map/pallas_call | solution.py:345
  44.9 1.6 %collective-permute-start.22 = (bf16[320,640]{1,0:T(8,128)(2,1)S(1)}, bf16[320,640]{1,0:T(8,128)(2,1)S(1)}, u32[]{:S(2)}, u32[]{:S(2)}) collective-permute-start(bf16[320,640]{1,0:T(8,128)(2,1)S(1)} %get-tuple-element.63), channel_id=1, source_target_pairs={{0,64},{64,128},{128,192},{192,0},{1,65},{65,129},{129,193},{193,1... | collective-permute-start | bytes 1228808 | tf_op jit(solution)/shard_map/ppermute | solution.py:43
  46.5 0.9 collective-permute-start.23
  47.4 2.7 %collective-permute-done.15.r1 = bf16[320,640]{1,0:T(8,128)(2,1)S(1)} collective-permute-done((bf16[320,640]{1,0:T(8,128)(2,1)S(1)}, bf16[320,640]{1,0:T(8,128)(2,1)S(1)}, u32[]{:S(2)}, u32[]{:S(2)}) %collective-permute-start.15) | collective-permute-done | bytes 409632 | tf_op jit(solution)/shard_map/ppermute | solution.py:43
  50.4 9.4 %collective-permute-done.16.r2 = bf16[320,640]{1,0:T(8,128)(2,1)S(1)} collective-permute-done((bf16[320,640]{1,0:T(8,128)(2,1)S(1)}, bf16[320,640]{1,0:T(8,128)(2,1)S(1)}, u32[]{:S(2)}, u32[]{:S(2)}) %collective-permute-start.16) | collective-permute-done | bytes 409632 | tf_op jit(solution)/shard_map/ppermute | solution.py:43
  59.8 0.9 shard_map.116
  60.8 1.7 %collective-permute-start.18 = (bf16[80,640]{1,0:T(8,128)(2,1)S(1)}, bf16[80,640]{1,0:T(8,128)(2,1)S(1)}, u32[]{:S(2)}, u32[]{:S(2)}) collective-permute-start(bf16[80,640]{1,0:T(8,128)(2,1)S(1)} %get-tuple-element.57), channel_id=1, source_target_pairs={{0,64},{64,128},{128,192},{192,0},{1,65},{65,129},{129,193},{193,1... | collective-permute-start | bytes 307208 | tf_op jit(solution)/shard_map/ppermute | solution.py:43
  62.4 0.9 collective-permute-start.19
  63.3 2.5 %collective-permute-start.20 = (bf16[80,640]{1,0:T(8,128)(2,1)S(1)}, bf16[80,640]{1,0:T(8,128)(2,1)S(1)}, u32[]{:S(2)}, u32[]{:S(2)}) collective-permute-start(bf16[80,640]{1,0:T(8,128)(2,1)S(1)} %get-tuple-element.59), channel_id=1, source_target_pairs={{0,192},{64,0},{128,64},{192,128},{1,193},{65,1},{129,65},{193,129... | collective-permute-start | bytes 307208 | tf_op jit(solution)/shard_map/ppermute | solution.py:43
  65.8 2.6 %collective-permute-done.24.r3 = bf16[320,640]{1,0:T(8,128)(2,1)S(1)} collective-permute-done((bf16[320,640]{1,0:T(8,128)(2,1)S(1)}, bf16[320,640]{1,0:T(8,128)(2,1)S(1)}, u32[]{:S(2)}, u32[]{:S(2)}) %collective-permute-start.24) | collective-permute-done | bytes 409632 | tf_op jit(solution)/shard_map/ppermute | solution.py:43
  68.4 1.0 shard_map.118
  69.9 0.7 collective-permute-start.26
  70.6 2.1 %collective-permute-start.27 = (bf16[80,640]{1,0:T(8,128)(2,1)S(1)}, bf16[80,640]{1,0:T(8,128)(2,1)S(1)}, u32[]{:S(2)}, u32[]{:S(2)}) collective-permute-start(bf16[80,640]{1,0:T(8,128)(2,1)S(1)} %get-tuple-element.69), channel_id=1, source_target_pairs={{0,6},{2,0},{4,2},{6,4},{1,7},{3,1},{5,3},{7,5},{8,14},{10,8},{12,... | collective-permute-start | bytes 307208 | tf_op jit(solution)/shard_map/ppermute | solution.py:43
  72.7 4.9 %collective-permute-done.25.c1 = bf16[80,640]{1,0:T(8,128)(2,1)S(1)} collective-permute-done((bf16[80,640]{1,0:T(8,128)(2,1)S(1)}, bf16[80,640]{1,0:T(8,128)(2,1)S(1)}, u32[]{:S(2)}, u32[]{:S(2)}) %collective-permute-start.25) | collective-permute-done | bytes 102432 | tf_op jit(solution)/shard_map/ppermute | solution.py:43
  77.6 0.6 collective-permute-done.27.c3
  78.2 0.9 shard_map.119
  79.1 6.2 %all-to-all-start = ((bf16[8,20,640]{2,1,0:T(8,128)(2,1)}), bf16[8,20,640]{2,1,0:T(8,128)(2,1)S(1)}, u32[]{:S(2)}, u32[]{:S(2)}) async-start(bf16[8,20,640]{2,1,0:T(8,128)(2,1)} %shard_map.119), calls=%async_computation | async-start | bytes 491520 | tf_op jit(solution)/shard_map/all_to_all | solution.py:474
  85.3 3.8 %collective-permute-start.9 = (bf16[192,640]{1,0:T(8,128)(2,1)S(1)}, bf16[192,640]{1,0:T(8,128)(2,1)S(1)}, u32[]{:S(2)}, u32[]{:S(2)}) collective-permute-start(bf16[192,640]{1,0:T(8,128)(2,1)S(1)} %get-tuple-element.43.tile), channel_id=1, source_target_pairs={{0,24},{8,0},{16,8},{24,16},{1,25},{9,1},{17,9},{25,17},{2,26},{10... | collective-permute-start | bytes 737288 | tf_op jit(solution)/shard_map/ppermute | solution.py:43
  89.1 1.9 %collective-permute-start.10 = (bf16[40,640]{1,0:T(8,128)(2,1)S(1)}, bf16[40,640]{1,0:T(8,128)(2,1)S(1)}, u32[]{:S(2)}, u32[]{:S(2)}) collective-permute-start(bf16[40,640]{1,0:T(8,128)(2,1)S(1)} %get-tuple-element.44), channel_id=1, source_target_pairs={{0,32},{32,64},{64,96},{96,128},{128,160},{160,192},{192,224},{1,3... | collective-permute-start | bytes 153608 | tf_op jit(solution)/shard_map/ppermute | solution.py:359
  91.0 3.6 %collective-permute-start.11 = (bf16[40,640]{1,0:T(8,128)(2,1)S(1)}, bf16[40,640]{1,0:T(8,128)(2,1)S(1)}, u32[]{:S(2)}, u32[]{:S(2)}) collective-permute-start(bf16[40,640]{1,0:T(8,128)(2,1)S(1)} %get-tuple-element.45), channel_id=1, source_target_pairs={{32,0},{64,32},{96,64},{128,96},{160,128},{192,160},{224,192},{33,... | collective-permute-start | bytes 153608 | tf_op jit(solution)/shard_map/ppermute | solution.py:360
  94.7 1.7 %collective-permute-done.11.bottom = bf16[40,640]{1,0:T(8,128)(2,1)S(1)} collective-permute-done((bf16[40,640]{1,0:T(8,128)(2,1)S(1)}, bf16[40,640]{1,0:T(8,128)(2,1)S(1)}, u32[]{:S(2)}, u32[]{:S(2)}) %collective-permute-start.11) | collective-permute-done | bytes 51232 | tf_op jit(solution)/shard_map/ppermute | solution.py:360
  96.4 1.3 %collective-permute-done.9.right = bf16[192,640]{1,0:T(8,128)(2,1)S(1)} collective-permute-done((bf16[192,640]{1,0:T(8,128)(2,1)S(1)}, bf16[192,640]{1,0:T(8,128)(2,1)S(1)}, u32[]{:S(2)}, u32[]{:S(2)}) %collective-permute-start.9) | collective-permute-done | bytes 245792 | tf_op jit(solution)/shard_map/ppermute | solution.py:43
  97.7 6.8 %collective-permute-done.8.left = bf16[192,640]{1,0:T(8,128)(2,1)S(1)} collective-permute-done((bf16[192,640]{1,0:T(8,128)(2,1)S(1)}, bf16[192,640]{1,0:T(8,128)(2,1)S(1)}, u32[]{:S(2)}, u32[]{:S(2)}) %collective-permute-start.8) | collective-permute-done | bytes 245792 | tf_op jit(solution)/shard_map/ppermute | solution.py:43
  104.5 0.6 shard_map.113
  105.1 3.8 %collective-permute-start.13 = (bf16[64,640]{1,0:T(8,128)(2,1)S(1)}, bf16[64,640]{1,0:T(8,128)(2,1)S(1)}, u32[]{:S(2)}, u32[]{:S(2)}) collective-permute-start(bf16[64,640]{1,0:T(8,128)(2,1)S(1)} %get-tuple-element.47), channel_id=1, source_target_pairs={{0,24},{8,0},{16,8},{24,16},{1,25},{9,1},{17,9},{25,17},{2,26},{10... | collective-permute-start | bytes 245768 | tf_op jit(solution)/shard_map/ppermute | solution.py:43
  108.9 2.4 %collective-permute-done.12.left_side = bf16[64,640]{1,0:T(8,128)(2,1)S(1)} collective-permute-done((bf16[64,640]{1,0:T(8,128)(2,1)S(1)}, bf16[64,640]{1,0:T(8,128)(2,1)S(1)}, u32[]{:S(2)}, u32[]{:S(2)}) %collective-permute-start.12) | collective-permute-done | bytes 81952 | tf_op jit(solution)/shard_map/ppermute | solution.py:43
  111.3 4.5 %shard_map.114 = bf16[192,640]{1,0:T(8,128)(2,1)} custom-call(s32[5]{0:T(128)S(1)} %stack.23.place, bf16[192,640]{1,0:T(8,128)(2,1)S(1)} %get-tuple-element.43.tile, bf16[192,640]{1,0:T(8,128)(2,1)S(1)} %collective-permute-done.8.left, bf16[192,640]{1,0:T(8,128)(2,1)S(1)} %collective-permute-done.9.right, bf16[40,640]{1,0:T(8,128)(2,1)S(1)} %collective-permute-done.10.top, ...), custom_call_target="tpu_custom_call" | custom-call | tf_op jit(solution)/shard_map/pallas_call | solution.py:345
  115.8 0.6 shard_map.120
  (41 shorter events, 2.4 us)
Async XLA Ops:
  0.6 20.8 %copy-start.1 = (bf16[1,12,16,640]{3,2,1,0:T(8,128)(2,1)S(1)}, bf16[1,12,16,640]{3,2,1,0:T(8,128)(2,1)}, u32[]{:S(2)}) copy-start(bf16[1,12,16,640]{3,2,1,0:T(8,128)(2,1)} %param.13) | copy-start | bytes 737284
  0.6 20.8 %copy-start = (bf16[1280,640]{1,0:T(8,128)(2,1)S(1)}, bf16[1280,640]{1,0:T(8,128)(2,1)}, u32[]{:S(2)}) copy-start(bf16[1280,640]{1,0:T(8,128)(2,1)} %out_hbm.1) | copy-start | bytes 4915204
  0.7 13.9 %collective-permute-start.1 = (bf16[192,640]{1,0:T(8,128)(2,1)}, bf16[192,640]{1,0:T(8,128)(2,1)S(1)}, u32[]{:S(2)}, u32[]{:S(2)}) collective-permute-start(bf16[192,640]{1,0:T(8,128)(2,1)} %bitcast.22), channel_id=1, source_target_pairs={{0,24},{8,0},{16,8},{24,16},{1,25},{9,1},{17,9},{25,17},{2,26},{10... | collective-permute-start | bytes 737288 | tf_op jit(solution)/shard_map/ppermute | solution.py:43
  5.4 11.4 %collective-permute-start = (bf16[192,640]{1,0:T(8,128)(2,1)}, bf16[192,640]{1,0:T(8,128)(2,1)S(1)}, u32[]{:S(2)}, u32[]{:S(2)}) collective-permute-start(bf16[192,640]{1,0:T(8,128)(2,1)} %bitcast.23), channel_id=1, source_target_pairs={{0,8},{8,16},{16,24},{24,0},{1,9},{9,17},{17,25},{25,1},{2,10},{10... | collective-permute-start | bytes 737288 | tf_op jit(solution)/shard_map/ppermute | solution.py:43
  6.2 7.7 %collective-permute-start.2 = (bf16[32,640]{1,0:T(8,128)(2,1)S(1)}, bf16[32,640]{1,0:T(8,128)(2,1)S(1)}, u32[]{:S(2)}, u32[]{:S(2)}) collective-permute-start(bf16[32,640]{1,0:T(8,128)(2,1)S(1)} %bitcast.30), channel_id=1, source_target_pairs={{0,32},{32,64},{64,96},{96,128},{128,160},{160,192},{192,224},{1,3... | collective-permute-start | bytes 122888 | tf_op jit(solution)/shard_map/ppermute | solution.py:359
  8.1 6.4 %collective-permute-start.3 = (bf16[32,640]{1,0:T(8,128)(2,1)S(1)}, bf16[32,640]{1,0:T(8,128)(2,1)S(1)}, u32[]{:S(2)}, u32[]{:S(2)}) collective-permute-start(bf16[32,640]{1,0:T(8,128)(2,1)S(1)} %bitcast.29), channel_id=1, source_target_pairs={{32,0},{64,32},{96,64},{128,96},{160,128},{192,160},{224,192},{33,... | collective-permute-start | bytes 122888 | tf_op jit(solution)/shard_map/ppermute | solution.py:360
  11.8 10.4 %collective-permute-start.7 = (bf16[192,640]{1,0:T(8,128)(2,1)}, bf16[192,640]{1,0:T(8,128)(2,1)S(1)}, u32[]{:S(2)}, u32[]{:S(2)}) collective-permute-start(bf16[192,640]{1,0:T(8,128)(2,1)} %bitcast.18), channel_id=1, source_target_pairs={{0,32},{32,0},{1,33},{33,1},{2,34},{34,2},{3,35},{35,3},{4,36},{36... | collective-permute-start | bytes 737288 | tf_op jit(solution)/shard_map/ppermute | solution.py:43
  13.9 8.3 %collective-permute-start.6 = (bf16[16,640]{1,0:T(8,128)(2,1)S(1)}, bf16[16,640]{1,0:T(8,128)(2,1)S(1)}, u32[]{:S(2)}, u32[]{:S(2)}) collective-permute-start(bf16[16,640]{1,0:T(8,128)(2,1)S(1)} %pad.4.rest_0_.own_e), channel_id=1, source_target_pairs={{0,16},{8,24},{16,0},{24,8},{1,17},{9,25},{17,1},{25,9},{2,18},{10... | collective-permute-start | bytes 61448 | tf_op jit(solution)/shard_map/ppermute | solution.py:43
  17.4 7.0 %collective-permute-start.4 = (bf16[80,640]{1,0:T(8,128)(2,1)S(1)}, bf16[80,640]{1,0:T(8,128)(2,1)S(1)}, u32[]{:S(2)}, u32[]{:S(2)}) collective-permute-start(bf16[80,640]{1,0:T(8,128)(2,1)S(1)} %get-tuple-element.39), channel_id=1, source_target_pairs={{0,8},{8,16},{16,24},{24,0},{1,9},{9,17},{17,25},{25,1},{2,10},{10... | collective-permute-start | bytes 307208 | tf_op jit(solution)/shard_map/ppermute | solution.py:43
  19.4 5.9 %collective-permute-start.5 = (bf16[80,640]{1,0:T(8,128)(2,1)S(1)}, bf16[80,640]{1,0:T(8,128)(2,1)S(1)}, u32[]{:S(2)}, u32[]{:S(2)}) collective-permute-start(bf16[80,640]{1,0:T(8,128)(2,1)S(1)} %get-tuple-element.40), channel_id=1, source_target_pairs={{0,24},{8,0},{16,8},{24,16},{1,25},{9,1},{17,9},{25,17},{2,26},{10... | collective-permute-start | bytes 307208 | tf_op jit(solution)/shard_map/ppermute | solution.py:43
  21.5 3.9 %copy-start.2 = (bf16[1,12,16,640]{3,2,1,0:T(8,128)(2,1)S(1)}, bf16[1,12,16,640]{3,2,1,0:T(8,128)(2,1)}, u32[]{:S(2)}) copy-start(bf16[1,12,16,640]{3,2,1,0:T(8,128)(2,1)} %param.7) | copy-start | bytes 737284
  32.1 2.3 %collective-permute-start.14 = (bf16[192,1920]{1,0:T(8,128)(2,1)S(1)}, bf16[192,1920]{1,0:T(8,128)(2,1)S(1)}, u32[]{:S(2)}, u32[]{:S(2)}) collective-permute-start(bf16[192,1920]{1,0:T(8,128)(2,1)S(1)} %get-tuple-element.49), channel_id=1, source_target_pairs={{0,32},{32,0},{1,33},{33,1},{2,34},{34,2},{3,35},{35,3},{4,36},{36... | collective-permute-start | bytes 2211848 | tf_op jit(solution)/shard_map/ppermute | solution.py:43
  32.2 10.8 %collective-permute-start.21 = (bf16[192,2176]{1,0:T(8,128)(2,1)S(1)}, bf16[192,2176]{1,0:T(8,128)(2,1)S(1)}, u32[]{:S(2)}, u32[]{:S(2)}) collective-permute-start(bf16[192,2176]{1,0:T(8,128)(2,1)S(1)} %get-tuple-element.61), channel_id=1, source_target_pairs={{0,32},{32,0},{1,33},{33,1},{2,34},{34,2},{3,35},{35,3},{4,36},{36... | collective-permute-start | bytes 2506760 | tf_op jit(solution)/shard_map/ppermute | solution.py:43
  37.3 12.8 %collective-permute-start.15 = (bf16[320,640]{1,0:T(8,128)(2,1)S(1)}, bf16[320,640]{1,0:T(8,128)(2,1)S(1)}, u32[]{:S(2)}, u32[]{:S(2)}) collective-permute-start(bf16[320,640]{1,0:T(8,128)(2,1)S(1)} %get-tuple-element.53), channel_id=1, source_target_pairs={{0,2},{2,4},{4,6},{6,0},{1,3},{3,5},{5,7},{7,1},{8,10},{10,12},{12... | collective-permute-start | bytes 1228808 | tf_op jit(solution)/shard_map/ppermute | solution.py:43
  38.8 21.0 %collective-permute-start.16 = (bf16[320,640]{1,0:T(8,128)(2,1)S(1)}, bf16[320,640]{1,0:T(8,128)(2,1)S(1)}, u32[]{:S(2)}, u32[]{:S(2)}) collective-permute-start(bf16[320,640]{1,0:T(8,128)(2,1)S(1)} %get-tuple-element.54), channel_id=1, source_target_pairs={{0,4},{2,6},{4,0},{6,2},{1,5},{3,7},{5,1},{7,3},{8,12},{10,14},{12... | collective-permute-start | bytes 1228808 | tf_op jit(solution)/shard_map/ppermute | solution.py:43
  41.6 18.3 %collective-permute-start.17 = (bf16[320,640]{1,0:T(8,128)(2,1)S(1)}, bf16[320,640]{1,0:T(8,128)(2,1)S(1)}, u32[]{:S(2)}, u32[]{:S(2)}) collective-permute-start(bf16[320,640]{1,0:T(8,128)(2,1)S(1)} %get-tuple-element.55), channel_id=1, source_target_pairs={{0,6},{2,0},{4,2},{6,4},{1,7},{3,1},{5,3},{7,5},{8,14},{10,8},{12,... | collective-permute-start | bytes 1228808 | tf_op jit(solution)/shard_map/ppermute | solution.py:43
  44.9 18.4 %collective-permute-start.22 = (bf16[320,640]{1,0:T(8,128)(2,1)S(1)}, bf16[320,640]{1,0:T(8,128)(2,1)S(1)}, u32[]{:S(2)}, u32[]{:S(2)}) collective-permute-start(bf16[320,640]{1,0:T(8,128)(2,1)S(1)} %get-tuple-element.63), channel_id=1, source_target_pairs={{0,64},{64,128},{128,192},{192,0},{1,65},{65,129},{129,193},{193,1... | collective-permute-start | bytes 1228808 | tf_op jit(solution)/shard_map/ppermute | solution.py:43
  46.5 19.2 %collective-permute-start.23 = (bf16[320,640]{1,0:T(8,128)(2,1)S(1)}, bf16[320,640]{1,0:T(8,128)(2,1)S(1)}, u32[]{:S(2)}, u32[]{:S(2)}) collective-permute-start(bf16[320,640]{1,0:T(8,128)(2,1)S(1)} %get-tuple-element.64), channel_id=1, source_target_pairs={{0,128},{64,192},{128,0},{192,64},{1,129},{65,193},{129,1},{193,65... | collective-permute-start | bytes 1228808 | tf_op jit(solution)/shard_map/ppermute | solution.py:43
  50.1 18.3 %collective-permute-start.24 = (bf16[320,640]{1,0:T(8,128)(2,1)S(1)}, bf16[320,640]{1,0:T(8,128)(2,1)S(1)}, u32[]{:S(2)}, u32[]{:S(2)}) collective-permute-start(bf16[320,640]{1,0:T(8,128)(2,1)S(1)} %get-tuple-element.65), channel_id=1, source_target_pairs={{0,192},{64,0},{128,64},{192,128},{1,193},{65,1},{129,65},{193,129... | collective-permute-start | bytes 1228808 | tf_op jit(solution)/shard_map/ppermute | solution.py:43
  60.8 9.8 %collective-permute-start.18 = (bf16[80,640]{1,0:T(8,128)(2,1)S(1)}, bf16[80,640]{1,0:T(8,128)(2,1)S(1)}, u32[]{:S(2)}, u32[]{:S(2)}) collective-permute-start(bf16[80,640]{1,0:T(8,128)(2,1)S(1)} %get-tuple-element.57), channel_id=1, source_target_pairs={{0,64},{64,128},{128,192},{192,0},{1,65},{65,129},{129,193},{193,1... | collective-permute-start | bytes 307208 | tf_op jit(solution)/shard_map/ppermute | solution.py:43
  62.4 10.3 %collective-permute-start.19 = (bf16[80,640]{1,0:T(8,128)(2,1)S(1)}, bf16[80,640]{1,0:T(8,128)(2,1)S(1)}, u32[]{:S(2)}, u32[]{:S(2)}) collective-permute-start(bf16[80,640]{1,0:T(8,128)(2,1)S(1)} %get-tuple-element.58), channel_id=1, source_target_pairs={{0,128},{64,192},{128,0},{192,64},{1,129},{65,193},{129,1},{193,65... | collective-permute-start | bytes 307208 | tf_op jit(solution)/shard_map/ppermute | solution.py:43
  63.3 9.4 %collective-permute-start.20 = (bf16[80,640]{1,0:T(8,128)(2,1)S(1)}, bf16[80,640]{1,0:T(8,128)(2,1)S(1)}, u32[]{:S(2)}, u32[]{:S(2)}) collective-permute-start(bf16[80,640]{1,0:T(8,128)(2,1)S(1)} %get-tuple-element.59), channel_id=1, source_target_pairs={{0,192},{64,0},{128,64},{192,128},{1,193},{65,1},{129,65},{193,129... | collective-permute-start | bytes 307208 | tf_op jit(solution)/shard_map/ppermute | solution.py:43
  69.4 8.2 %collective-permute-start.25 = (bf16[80,640]{1,0:T(8,128)(2,1)S(1)}, bf16[80,640]{1,0:T(8,128)(2,1)S(1)}, u32[]{:S(2)}, u32[]{:S(2)}) collective-permute-start(bf16[80,640]{1,0:T(8,128)(2,1)S(1)} %get-tuple-element.67), channel_id=1, source_target_pairs={{0,2},{2,4},{4,6},{6,0},{1,3},{3,5},{5,7},{7,1},{8,10},{10,12},{12... | collective-permute-start | bytes 307208 | tf_op jit(solution)/shard_map/ppermute | solution.py:43
  69.9 7.7 %collective-permute-start.26 = (bf16[80,640]{1,0:T(8,128)(2,1)S(1)}, bf16[80,640]{1,0:T(8,128)(2,1)S(1)}, u32[]{:S(2)}, u32[]{:S(2)}) collective-permute-start(bf16[80,640]{1,0:T(8,128)(2,1)S(1)} %get-tuple-element.68), channel_id=1, source_target_pairs={{0,4},{2,6},{4,0},{6,2},{1,5},{3,7},{5,1},{7,3},{8,12},{10,14},{12... | collective-permute-start | bytes 307208 | tf_op jit(solution)/shard_map/ppermute | solution.py:43
  70.6 7.6 %collective-permute-start.27 = (bf16[80,640]{1,0:T(8,128)(2,1)S(1)}, bf16[80,640]{1,0:T(8,128)(2,1)S(1)}, u32[]{:S(2)}, u32[]{:S(2)}) collective-permute-start(bf16[80,640]{1,0:T(8,128)(2,1)S(1)} %get-tuple-element.69), channel_id=1, source_target_pairs={{0,6},{2,0},{4,2},{6,4},{1,7},{3,1},{5,3},{7,5},{8,14},{10,8},{12,... | collective-permute-start | bytes 307208 | tf_op jit(solution)/shard_map/ppermute | solution.py:43
  79.1 36.7 %all-to-all-start = ((bf16[8,20,640]{2,1,0:T(8,128)(2,1)}), bf16[8,20,640]{2,1,0:T(8,128)(2,1)S(1)}, u32[]{:S(2)}, u32[]{:S(2)}) async-start(bf16[8,20,640]{2,1,0:T(8,128)(2,1)} %shard_map.119), calls=%async_computation | async-start | bytes 491520 | tf_op jit(solution)/shard_map/all_to_all | solution.py:474
  85.3 12.4 %collective-permute-start.9 = (bf16[192,640]{1,0:T(8,128)(2,1)S(1)}, bf16[192,640]{1,0:T(8,128)(2,1)S(1)}, u32[]{:S(2)}, u32[]{:S(2)}) collective-permute-start(bf16[192,640]{1,0:T(8,128)(2,1)S(1)} %get-tuple-element.43.tile), channel_id=1, source_target_pairs={{0,24},{8,0},{16,8},{24,16},{1,25},{9,1},{17,9},{25,17},{2,26},{10... | collective-permute-start | bytes 737288 | tf_op jit(solution)/shard_map/ppermute | solution.py:43
  89.1 15.3 %collective-permute-start.8 = (bf16[192,640]{1,0:T(8,128)(2,1)S(1)}, bf16[192,640]{1,0:T(8,128)(2,1)S(1)}, u32[]{:S(2)}, u32[]{:S(2)}) collective-permute-start(bf16[192,640]{1,0:T(8,128)(2,1)S(1)} %get-tuple-element.43.tile), channel_id=1, source_target_pairs={{0,8},{8,16},{16,24},{24,0},{1,9},{9,17},{17,25},{25,1},{2,10},{10... | collective-permute-start | bytes 737288 | tf_op jit(solution)/shard_map/ppermute | solution.py:43
  89.1 5.6 %collective-permute-start.10 = (bf16[40,640]{1,0:T(8,128)(2,1)S(1)}, bf16[40,640]{1,0:T(8,128)(2,1)S(1)}, u32[]{:S(2)}, u32[]{:S(2)}) collective-permute-start(bf16[40,640]{1,0:T(8,128)(2,1)S(1)} %get-tuple-element.44), channel_id=1, source_target_pairs={{0,32},{32,64},{64,96},{96,128},{128,160},{160,192},{192,224},{1,3... | collective-permute-start | bytes 153608 | tf_op jit(solution)/shard_map/ppermute | solution.py:359
  91.0 5.4 %collective-permute-start.11 = (bf16[40,640]{1,0:T(8,128)(2,1)S(1)}, bf16[40,640]{1,0:T(8,128)(2,1)S(1)}, u32[]{:S(2)}, u32[]{:S(2)}) collective-permute-start(bf16[40,640]{1,0:T(8,128)(2,1)S(1)} %get-tuple-element.45), channel_id=1, source_target_pairs={{32,0},{64,32},{96,64},{128,96},{160,128},{192,160},{224,192},{33,... | collective-permute-start | bytes 153608 | tf_op jit(solution)/shard_map/ppermute | solution.py:360
  105.0 6.3 %collective-permute-start.12 = (bf16[64,640]{1,0:T(8,128)(2,1)S(1)}, bf16[64,640]{1,0:T(8,128)(2,1)S(1)}, u32[]{:S(2)}, u32[]{:S(2)}) collective-permute-start(bf16[64,640]{1,0:T(8,128)(2,1)S(1)} %get-tuple-element.46), channel_id=1, source_target_pairs={{0,8},{8,16},{16,24},{24,0},{1,9},{9,17},{17,25},{25,1},{2,10},{10... | collective-permute-start | bytes 245768 | tf_op jit(solution)/shard_map/ppermute | solution.py:43
  105.1 6.2 %collective-permute-start.13 = (bf16[64,640]{1,0:T(8,128)(2,1)S(1)}, bf16[64,640]{1,0:T(8,128)(2,1)S(1)}, u32[]{:S(2)}, u32[]{:S(2)}) collective-permute-start(bf16[64,640]{1,0:T(8,128)(2,1)S(1)} %get-tuple-element.47), channel_id=1, source_target_pairs={{0,24},{8,0},{16,8},{24,16},{1,25},{9,1},{17,9},{25,17},{2,26},{10... | collective-permute-start | bytes 245768 | tf_op jit(solution)/shard_map/ppermute | solution.py:43

commit v6 on v5

--- a/solution.py
+++ b/solution.py
@@ -31,6 +31,7 @@
 
 
 LAT = ("y", "core")
+LINE = ("zl1", "zl0")
 bf16 = jnp.bfloat16
 f32 = jnp.float32
 
@@ -269,7 +270,7 @@
     mlp = m0[...] + m1[...].astype(f32) + m2[...].astype(f32) + m3[...].astype(f32)
     conv = c0[...] + c1[...].astype(f32) + c2[...].astype(f32) + c3[...].astype(f32)
     for to in range(8):
-        rows = to % 4 * 2 + to // 4
+        rows = to // 2 % 2 * 4 + to // 4 * 2 + to % 2
         o[to, 0:10, :] = conv[rows * 10 : rows * 10 + 10, :].astype(bf16)
         o[to, 10:15, :] = mlp[rows * 5 : rows * 5 + 5, :].astype(bf16)
         o[to, 15:20, :] = mlp[40 + rows * 5 : 45 + rows * 5, :].astype(bf16)
@@ -354,8 +355,8 @@
 def neighbours(tile, to_up, to_down):
     forward = [(i, i + 1) for i in range(7)]
     backward = [(i + 1, i) for i in range(7)]
-    left = shift(tile, "zlo", 4, 1)
-    right = shift(tile, "zlo", 4, 3)
+    left = shift(tile, LINE, 4, 1)
+    right = shift(tile, LINE, 4, 3)
     top = lax.ppermute(to_up, LAT, forward)
     bottom = lax.ppermute(to_down, LAT, backward)
     return left, right, top, bottom
@@ -367,8 +368,8 @@
         side_kernel, (struct((rows, EMBED), bf16),) * 2, [], 4, place,
         left, right, top, bottom, *extra,
     )
-    left_side = shift(to_right, "zlo", 4, 1)
-    right_side = shift(to_left, "zlo", 4, 3)
+    left_side = shift(to_right, LINE, 4, 1)
+    right_side = shift(to_left, LINE, 4, 3)
     return left_side, right_side
 
 
@@ -391,7 +392,7 @@
 def block(fields, filter_basis, lon_offsets, conv_weight, weight_in, weight_out, cotangent):
     y = lax.axis_index("y")
     core = lax.axis_index("core")
-    lon = lax.axis_index("zlo")
+    lon = lax.axis_index(LINE)
     x = lax.axis_index("x")
     lat = 2 * y + core
     place = jnp.stack([lat, lon, core, x, y]).astype(jnp.int32)
@@ -400,7 +401,7 @@
 
     left, right, top, bottom = neighbours(tile, tile[CELLS - RIM :], tile[:RIM])
     own_e = coefficients(filter_basis, lon_offsets)
-    far_e = shift(own_e, "zlo", 4, 2)
+    far_e = shift(own_e, LINE, 4, 2)
     left_side, right_side = relay(place, left, right, top, bottom, own_e)
     other_tangent = shift(tangent, "core", 2, 1)
 
@@ -471,7 +472,7 @@
         own_e, left_side, right_side, far_e, in_hbm=(conv_weight,),
     )
     packed = call(pack_kernel, struct((8, 20, EMBED), bf16), [], 4, None, *m, *c)
-    parts = lax.all_to_all(packed, ("zhi", "zlo"), split_axis=0, concat_axis=0, tiled=True)
+    parts = lax.all_to_all(packed, ("zl0", "zl1", "zhi"), split_axis=0, concat_axis=0, tiled=True)
     conv_grad, in_grad, out_grad = call(
         final_kernel,
         (struct((10, EMBED), f32), struct((5, EMBED), f32), struct((5, EMBED), f32)),
@@ -487,16 +488,16 @@
 
 
 def solution(mesh):
-    fine = Mesh(mesh.devices.reshape(4, 2, 4, 4, 2), ("y", "core", "zlo", "x", "zhi"))
-    tile_spec = P(("x", "zhi"), LAT, "zlo", None)
-    everyone = ("y", "core", "zlo", "x", "zhi")
+    everyone = LAT + LINE + ("x", "zhi")
+    fine = Mesh(mesh.devices.reshape(4, 2, 2, 2, 4, 2), everyone)
+    tile_spec = P(("x", "zhi"), LAT, LINE, None)
     return jax.shard_map(
         block,
         mesh=fine,
         in_specs=(
             tile_spec,
-            P(LAT + ("zlo",), None, None, None),
-            P(LAT + ("zlo",), None, None),
+            P(LAT + LINE, None, None, None),
+            P(LAT + LINE, None, None),
             P(),
             P(),
             P(),

time: 117 us -> 117 us (level)
  no operation moved by 1% of the time
where the time goes in v6:
time: 117 us; the launch traced here: 116 us
  starting transfers between devices  52 us (44%)
  waiting for transfers between devices  39.5 us (34%)
  Pallas kernels  21.1 us (18%)
  other arithmetic  1.99 us (2%)
    ppermute x24, waiting for transfers between devices, shift(): lax.ppermute(block, axis, [(i, (i + step) % count) for i in range(count)])  37.8 us
    ppermute x24, starting transfers between devices, shift(): lax.ppermute(block, axis, [(i, (i + step) % count) for i in range(count)])  34.6 us
    pallas_call x11, Pallas kernels, call(): pl.pallas_call(kernel, out_shape=outs, in_specs=in_specs, scratch_shapes=...  21.1 us
    ppermute x2, starting transfers between devices, neighbours(): bottom = lax.ppermute(to_down, LAT, backward)  7.28 us
    all_to_all x1, starting transfers between devices, block(): lax.all_to_all(packed, ('zl0', 'zl1', 'zhi'), split_axis=0, concat_axis=0...  6.22 us
    ppermute x2, starting transfers between devices, neighbours(): top = lax.ppermute(to_up, LAT, forward)  3.83 us
  transfers between devices with their start and end apart: 29, of which 13 were waited for; matrix products, arithmetic and copies ran while one was open for 3% of the time, Pallas kernels for 11%

profile of v6, /device:TPU:8, one launch (start us, length us, event | category | flops | bytes accessed | tf_op | source)
XLA Modules:
  0.0 116.5 jit_solution(4632624974906138946)
XLA Ops:
  0.7 4.7 %collective-permute-start.1 = (bf16[192,640]{1,0:T(8,128)(2,1)}, bf16[192,640]{1,0:T(8,128)(2,1)S(1)}, u32[]{:S(2)}, u32[]{:S(2)}) collective-permute-start(bf16[192,640]{1,0:T(8,128)(2,1)} %bitcast.22), channel_id=1, source_target_pairs={{0,24},{8,0},{16,8},{24,16},{1,25},{9,1},{17,9},{25,17},{2,26},{10... | collective-permute-start | bytes 737288 | tf_op jit(solution)/shard_map/ppermute | solution.py:44
  5.4 0.9 fusion.21
  6.2 1.9 %collective-permute-start.2 = (bf16[32,640]{1,0:T(8,128)(2,1)S(1)}, bf16[32,640]{1,0:T(8,128)(2,1)S(1)}, u32[]{:S(2)}, u32[]{:S(2)}) collective-permute-start(bf16[32,640]{1,0:T(8,128)(2,1)S(1)} %bitcast.30), channel_id=1, source_target_pairs={{0,32},{32,64},{64,96},{96,128},{128,160},{160,192},{192,224},{1,3... | collective-permute-start | bytes 122888 | tf_op jit(solution)/shard_map/ppermute | solution.py:360
  8.1 3.6 %collective-permute-start.3 = (bf16[32,640]{1,0:T(8,128)(2,1)S(1)}, bf16[32,640]{1,0:T(8,128)(2,1)S(1)}, u32[]{:S(2)}, u32[]{:S(2)}) collective-permute-start(bf16[32,640]{1,0:T(8,128)(2,1)S(1)} %bitcast.29), channel_id=1, source_target_pairs={{32,0},{64,32},{96,64},{128,96},{160,128},{192,160},{224,192},{33,... | collective-permute-start | bytes 122888 | tf_op jit(solution)/shard_map/ppermute | solution.py:361
  11.9 0.7 add_select_fusion
  12.6 0.7 convert_bitcast_fusion
  13.9 0.7 collective-permute-start.6
  14.6 2.2 %collective-permute-done.left = bf16[192,640]{1,0:T(8,128)(2,1)S(1)} collective-permute-done((bf16[192,640]{1,0:T(8,128)(2,1)}, bf16[192,640]{1,0:T(8,128)(2,1)S(1)}, u32[]{:S(2)}, u32[]{:S(2)}) %collective-permute-start) | collective-permute-done | bytes 245792 | tf_op jit(solution)/shard_map/ppermute | solution.py:44
  16.8 0.6 shard_map.110
  17.4 2.1 %collective-permute-start.4 = (bf16[80,640]{1,0:T(8,128)(2,1)S(1)}, bf16[80,640]{1,0:T(8,128)(2,1)S(1)}, u32[]{:S(2)}, u32[]{:S(2)}) collective-permute-start(bf16[80,640]{1,0:T(8,128)(2,1)S(1)} %get-tuple-element.39), channel_id=1, source_target_pairs={{0,8},{8,16},{16,24},{24,0},{1,9},{9,17},{17,25},{25,1},{2,10},{10... | collective-permute-start | bytes 307208 | tf_op jit(solution)/shard_map/ppermute | solution.py:44
  19.4 1.8 %collective-permute-start.5 = (bf16[80,640]{1,0:T(8,128)(2,1)S(1)}, bf16[80,640]{1,0:T(8,128)(2,1)S(1)}, u32[]{:S(2)}, u32[]{:S(2)}) collective-permute-start(bf16[80,640]{1,0:T(8,128)(2,1)S(1)} %get-tuple-element.40), channel_id=1, source_target_pairs={{0,24},{8,0},{16,8},{24,16},{1,25},{9,1},{17,9},{25,17},{2,26},{10... | collective-permute-start | bytes 307208 | tf_op jit(solution)/shard_map/ppermute | solution.py:44
  21.5 0.7 shard_map.111.hidden_grad
  22.2 2.2 %collective-permute-done.4.left_side.left_e = bf16[80,640]{1,0:T(8,128)(2,1)S(1)} collective-permute-done((bf16[80,640]{1,0:T(8,128)(2,1)S(1)}, bf16[80,640]{1,0:T(8,128)(2,1)S(1)}, u32[]{:S(2)}, u32[]{:S(2)}) %collective-permute-start.4) | collective-permute-done | bytes 102432 | tf_op jit(solution)/shard_map/ppermute | solution.py:44
  24.4 1.0 collective-permute-done.5.right_side.right_e
  25.4 6.7 %shard_map.112 = (bf16[192,640]{1,0:T(8,128)(2,1)}, bf16[192,640]{1,0:T(8,128)(2,1)S(1)}, bf16[192,2176]{1,0:T(8,128)(2,1)S(1)}, bf16[192,1920]{1,0:T(8,128)(2,1...) custom-call(s32[5]{0:T(128)S(1)} %stack.23.place, ...), custom_call_target="tpu_custom_call" | custom-call | tf_op jit(solution)/shard_map/pallas_call | solution.py:346
  32.7 1.7 %collective-permute-done.14.other = bf16[192,1920]{1,0:T(8,128)(2,1)S(1)} collective-permute-done((bf16[192,1920]{1,0:T(8,128)(2,1)S(1)}, bf16[192,1920]{1,0:T(8,128)(2,1)S(1)}, u32[]{:S(2)}, u32[]{:S(2)}) %collective-permute-start.14) | collective-permute-done | bytes 737312 | tf_op jit(solution)/shard_map/ppermute | solution.py:44
  34.4 2.9 %shard_map.115 = (f32[320,640]{1,0:T(8,128)S(1)}, bf16[320,640]{1,0:T(8,128)(2,1)S(1)}, bf16[320,640]{1,0:T(8,128)(2,1)S(1)}, bf16[320,640]{1,0:T(8,128)(2,1)S(1)}) custom-call(s32[5]{0:T(128)S(1)} %stack.23.place, bf16[192,1920]{1,0:T(8,128)(2,1)S(1)} %get-tuple-element.48.mine, bf16[192,1920]{1,0:T(8,128)(2,1)S(1)} %collective-permute-done.14.other, ...), custom_call_target="tpu_custom_call" | custom-call | tf_op jit(solution)/shard_map/pallas_call | solution.py:346
  37.3 1.6 %collective-permute-start.15 = (bf16[320,640]{1,0:T(8,128)(2,1)S(1)}, bf16[320,640]{1,0:T(8,128)(2,1)S(1)}, u32[]{:S(2)}, u32[]{:S(2)}) collective-permute-start(bf16[320,640]{1,0:T(8,128)(2,1)S(1)} %get-tuple-element.53), channel_id=1, source_target_pairs={{0,2},{2,4},{4,6},{6,0},{1,3},{3,5},{5,7},{7,1},{8,10},{10,12},{12... | collective-permute-start | bytes 1228808 | tf_op jit(solution)/shard_map/ppermute | solution.py:44
  38.8 2.7 %collective-permute-start.16 = (bf16[320,640]{1,0:T(8,128)(2,1)S(1)}, bf16[320,640]{1,0:T(8,128)(2,1)S(1)}, u32[]{:S(2)}, u32[]{:S(2)}) collective-permute-start(bf16[320,640]{1,0:T(8,128)(2,1)S(1)} %get-tuple-element.54), channel_id=1, source_target_pairs={{0,4},{2,6},{4,0},{6,2},{1,5},{3,7},{5,1},{7,3},{8,12},{10,14},{12... | collective-permute-start | bytes 1228808 | tf_op jit(solution)/shard_map/ppermute | solution.py:44
  41.6 1.4 %collective-permute-start.17 = (bf16[320,640]{1,0:T(8,128)(2,1)S(1)}, bf16[320,640]{1,0:T(8,128)(2,1)S(1)}, u32[]{:S(2)}, u32[]{:S(2)}) collective-permute-start(bf16[320,640]{1,0:T(8,128)(2,1)S(1)} %get-tuple-element.55), channel_id=1, source_target_pairs={{0,6},{2,0},{4,2},{6,4},{1,7},{3,1},{5,3},{7,5},{8,14},{10,8},{12,... | collective-permute-start | bytes 1228808 | tf_op jit(solution)/shard_map/ppermute | solution.py:44
  43.0 1.9 %shard_map.117 = (f32[320,640]{1,0:T(8,128)S(1)}, bf16[320,640]{1,0:T(8,128)(2,1)S(1)}, bf16[320,640]{1,0:T(8,128)(2,1)S(1)}, bf16[320,640]{1,0:T(8,128)(2,1)S(1)}) custom-call(s32[5]{0:T(128)S(1)} %stack.23.place, bf16[192,2176]{1,0:T(8,128)(2,1)S(1)} %get-tuple-element.60.mine, bf16[192,2176]{1,0:T(8,128)(2,1)S(1)} %collective-permute-done.21.other), custom_call_target="tpu_custom_call" | custom-call | tf_op jit(solution)/shard_map/pallas_call | solution.py:346
  44.9 1.6 %collective-permute-start.22 = (bf16[320,640]{1,0:T(8,128)(2,1)S(1)}, bf16[320,640]{1,0:T(8,128)(2,1)S(1)}, u32[]{:S(2)}, u32[]{:S(2)}) collective-permute-start(bf16[320,640]{1,0:T(8,128)(2,1)S(1)} %get-tuple-element.63), channel_id=1, source_target_pairs={{0,64},{64,128},{128,192},{192,0},{1,65},{65,129},{129,193},{193,1... | collective-permute-start | bytes 1228808 | tf_op jit(solution)/shard_map/ppermute | solution.py:44
  46.5 0.9 collective-permute-start.23
  47.4 2.7 %collective-permute-done.15.r1 = bf16[320,640]{1,0:T(8,128)(2,1)S(1)} collective-permute-done((bf16[320,640]{1,0:T(8,128)(2,1)S(1)}, bf16[320,640]{1,0:T(8,128)(2,1)S(1)}, u32[]{:S(2)}, u32[]{:S(2)}) %collective-permute-start.15) | collective-permute-done | bytes 409632 | tf_op jit(solution)/shard_map/ppermute | solution.py:44
  50.4 9.4 %collective-permute-done.16.r2 = bf16[320,640]{1,0:T(8,128)(2,1)S(1)} collective-permute-done((bf16[320,640]{1,0:T(8,128)(2,1)S(1)}, bf16[320,640]{1,0:T(8,128)(2,1)S(1)}, u32[]{:S(2)}, u32[]{:S(2)}) %collective-permute-start.16) | collective-permute-done | bytes 409632 | tf_op jit(solution)/shard_map/ppermute | solution.py:44
  59.8 0.9 shard_map.116
  60.8 1.7 %collective-permute-start.18 = (bf16[80,640]{1,0:T(8,128)(2,1)S(1)}, bf16[80,640]{1,0:T(8,128)(2,1)S(1)}, u32[]{:S(2)}, u32[]{:S(2)}) collective-permute-start(bf16[80,640]{1,0:T(8,128)(2,1)S(1)} %get-tuple-element.57), channel_id=1, source_target_pairs={{0,64},{64,128},{128,192},{192,0},{1,65},{65,129},{129,193},{193,1... | collective-permute-start | bytes 307208 | tf_op jit(solution)/shard_map/ppermute | solution.py:44
  62.4 0.9 collective-permute-start.19
  63.3 2.5 %collective-permute-start.20 = (bf16[80,640]{1,0:T(8,128)(2,1)S(1)}, bf16[80,640]{1,0:T(8,128)(2,1)S(1)}, u32[]{:S(2)}, u32[]{:S(2)}) collective-permute-start(bf16[80,640]{1,0:T(8,128)(2,1)S(1)} %get-tuple-element.59), channel_id=1, source_target_pairs={{0,192},{64,0},{128,64},{192,128},{1,193},{65,1},{129,65},{193,129... | collective-permute-start | bytes 307208 | tf_op jit(solution)/shard_map/ppermute | solution.py:44
  65.8 2.6 %collective-permute-done.24.r3 = bf16[320,640]{1,0:T(8,128)(2,1)S(1)} collective-permute-done((bf16[320,640]{1,0:T(8,128)(2,1)S(1)}, bf16[320,640]{1,0:T(8,128)(2,1)S(1)}, u32[]{:S(2)}, u32[]{:S(2)}) %collective-permute-start.24) | collective-permute-done | bytes 409632 | tf_op jit(solution)/shard_map/ppermute | solution.py:44
  68.4 1.0 shard_map.118
  69.9 0.7 collective-permute-start.26
  70.6 2.1 %collective-permute-start.27 = (bf16[80,640]{1,0:T(8,128)(2,1)S(1)}, bf16[80,640]{1,0:T(8,128)(2,1)S(1)}, u32[]{:S(2)}, u32[]{:S(2)}) collective-permute-start(bf16[80,640]{1,0:T(8,128)(2,1)S(1)} %get-tuple-element.69), channel_id=1, source_target_pairs={{0,6},{2,0},{4,2},{6,4},{1,7},{3,1},{5,3},{7,5},{8,14},{10,8},{12,... | collective-permute-start | bytes 307208 | tf_op jit(solution)/shard_map/ppermute | solution.py:44
  72.7 4.9 %collective-permute-done.25.c1 = bf16[80,640]{1,0:T(8,128)(2,1)S(1)} collective-permute-done((bf16[80,640]{1,0:T(8,128)(2,1)S(1)}, bf16[80,640]{1,0:T(8,128)(2,1)S(1)}, u32[]{:S(2)}, u32[]{:S(2)}) %collective-permute-start.25) | collective-permute-done | bytes 102432 | tf_op jit(solution)/shard_map/ppermute | solution.py:44
  77.6 0.6 collective-permute-done.27.c3
  78.2 0.9 shard_map.119
  79.1 6.2 %all-to-all-start = ((bf16[8,20,640]{2,1,0:T(8,128)(2,1)}), bf16[8,20,640]{2,1,0:T(8,128)(2,1)S(1)}, u32[]{:S(2)}, u32[]{:S(2)}) async-start(bf16[8,20,640]{2,1,0:T(8,128)(2,1)} %shard_map.119), calls=%async_computation | async-start | bytes 491520 | tf_op jit(solution)/shard_map/all_to_all | solution.py:475
  85.3 3.8 %collective-permute-start.9 = (bf16[192,640]{1,0:T(8,128)(2,1)S(1)}, bf16[192,640]{1,0:T(8,128)(2,1)S(1)}, u32[]{:S(2)}, u32[]{:S(2)}) collective-permute-start(bf16[192,640]{1,0:T(8,128)(2,1)S(1)} %get-tuple-element.43.tile), channel_id=1, source_target_pairs={{0,24},{8,0},{16,8},{24,16},{1,25},{9,1},{17,9},{25,17},{2,26},{10... | collective-permute-start | bytes 737288 | tf_op jit(solution)/shard_map/ppermute | solution.py:44
  89.1 1.9 %collective-permute-start.10 = (bf16[40,640]{1,0:T(8,128)(2,1)S(1)}, bf16[40,640]{1,0:T(8,128)(2,1)S(1)}, u32[]{:S(2)}, u32[]{:S(2)}) collective-permute-start(bf16[40,640]{1,0:T(8,128)(2,1)S(1)} %get-tuple-element.44), channel_id=1, source_target_pairs={{0,32},{32,64},{64,96},{96,128},{128,160},{160,192},{192,224},{1,3... | collective-permute-start | bytes 153608 | tf_op jit(solution)/shard_map/ppermute | solution.py:360
  91.0 3.6 %collective-permute-start.11 = (bf16[40,640]{1,0:T(8,128)(2,1)S(1)}, bf16[40,640]{1,0:T(8,128)(2,1)S(1)}, u32[]{:S(2)}, u32[]{:S(2)}) collective-permute-start(bf16[40,640]{1,0:T(8,128)(2,1)S(1)} %get-tuple-element.45), channel_id=1, source_target_pairs={{32,0},{64,32},{96,64},{128,96},{160,128},{192,160},{224,192},{33,... | collective-permute-start | bytes 153608 | tf_op jit(solution)/shard_map/ppermute | solution.py:361
  94.7 1.7 %collective-permute-done.11.bottom = bf16[40,640]{1,0:T(8,128)(2,1)S(1)} collective-permute-done((bf16[40,640]{1,0:T(8,128)(2,1)S(1)}, bf16[40,640]{1,0:T(8,128)(2,1)S(1)}, u32[]{:S(2)}, u32[]{:S(2)}) %collective-permute-start.11) | collective-permute-done | bytes 51232 | tf_op jit(solution)/shard_map/ppermute | solution.py:361
  96.4 1.2 %collective-permute-done.9.right = bf16[192,640]{1,0:T(8,128)(2,1)S(1)} collective-permute-done((bf16[192,640]{1,0:T(8,128)(2,1)S(1)}, bf16[192,640]{1,0:T(8,128)(2,1)S(1)}, u32[]{:S(2)}, u32[]{:S(2)}) %collective-permute-start.9) | collective-permute-done | bytes 245792 | tf_op jit(solution)/shard_map/ppermute | solution.py:44
  97.7 6.8 %collective-permute-done.8.left = bf16[192,640]{1,0:T(8,128)(2,1)S(1)} collective-permute-done((bf16[192,640]{1,0:T(8,128)(2,1)S(1)}, bf16[192,640]{1,0:T(8,128)(2,1)S(1)}, u32[]{:S(2)}, u32[]{:S(2)}) %collective-permute-start.8) | collective-permute-done | bytes 245792 | tf_op jit(solution)/shard_map/ppermute | solution.py:44
  104.5 0.6 shard_map.113
  105.1 3.8 %collective-permute-start.13 = (bf16[64,640]{1,0:T(8,128)(2,1)S(1)}, bf16[64,640]{1,0:T(8,128)(2,1)S(1)}, u32[]{:S(2)}, u32[]{:S(2)}) collective-permute-start(bf16[64,640]{1,0:T(8,128)(2,1)S(1)} %get-tuple-element.47), channel_id=1, source_target_pairs={{0,24},{8,0},{16,8},{24,16},{1,25},{9,1},{17,9},{25,17},{2,26},{10... | collective-permute-start | bytes 245768 | tf_op jit(solution)/shard_map/ppermute | solution.py:44
  108.9 2.4 %collective-permute-done.12.left_side = bf16[64,640]{1,0:T(8,128)(2,1)S(1)} collective-permute-done((bf16[64,640]{1,0:T(8,128)(2,1)S(1)}, bf16[64,640]{1,0:T(8,128)(2,1)S(1)}, u32[]{:S(2)}, u32[]{:S(2)}) %collective-permute-start.12) | collective-permute-done | bytes 81952 | tf_op jit(solution)/shard_map/ppermute | solution.py:44
  111.4 4.5 %shard_map.114 = bf16[192,640]{1,0:T(8,128)(2,1)} custom-call(s32[5]{0:T(128)S(1)} %stack.23.place, bf16[192,640]{1,0:T(8,128)(2,1)S(1)} %get-tuple-element.43.tile, bf16[192,640]{1,0:T(8,128)(2,1)S(1)} %collective-permute-done.8.left, bf16[192,640]{1,0:T(8,128)(2,1)S(1)} %collective-permute-done.9.right, bf16[40,640]{1,0:T(8,128)(2,1)S(1)} %collective-permute-done.10.top, ...), custom_call_target="tpu_custom_call" | custom-call | tf_op jit(solution)/shard_map/pallas_call | solution.py:346
  115.8 0.6 shard_map.120
  (41 shorter events, 2.4 us)
Async XLA Ops:
  0.6 20.8 %copy-start.1 = (bf16[1,12,16,640]{3,2,1,0:T(8,128)(2,1)S(1)}, bf16[1,12,16,640]{3,2,1,0:T(8,128)(2,1)}, u32[]{:S(2)}) copy-start(bf16[1,12,16,640]{3,2,1,0:T(8,128)(2,1)} %param.13) | copy-start | bytes 737284
  0.6 20.8 %copy-start = (bf16[1280,640]{1,0:T(8,128)(2,1)S(1)}, bf16[1280,640]{1,0:T(8,128)(2,1)}, u32[]{:S(2)}) copy-start(bf16[1280,640]{1,0:T(8,128)(2,1)} %out_hbm.1) | copy-start | bytes 4915204
  0.7 13.9 %collective-permute-start.1 = (bf16[192,640]{1,0:T(8,128)(2,1)}, bf16[192,640]{1,0:T(8,128)(2,1)S(1)}, u32[]{:S(2)}, u32[]{:S(2)}) collective-permute-start(bf16[192,640]{1,0:T(8,128)(2,1)} %bitcast.22), channel_id=1, source_target_pairs={{0,24},{8,0},{16,8},{24,16},{1,25},{9,1},{17,9},{25,17},{2,26},{10... | collective-permute-start | bytes 737288 | tf_op jit(solution)/shard_map/ppermute | solution.py:44
  5.4 11.4 %collective-permute-start = (bf16[192,640]{1,0:T(8,128)(2,1)}, bf16[192,640]{1,0:T(8,128)(2,1)S(1)}, u32[]{:S(2)}, u32[]{:S(2)}) collective-permute-start(bf16[192,640]{1,0:T(8,128)(2,1)} %bitcast.23), channel_id=1, source_target_pairs={{0,8},{8,16},{16,24},{24,0},{1,9},{9,17},{17,25},{25,1},{2,10},{10... | collective-permute-start | bytes 737288 | tf_op jit(solution)/shard_map/ppermute | solution.py:44
  6.2 7.7 %collective-permute-start.2 = (bf16[32,640]{1,0:T(8,128)(2,1)S(1)}, bf16[32,640]{1,0:T(8,128)(2,1)S(1)}, u32[]{:S(2)}, u32[]{:S(2)}) collective-permute-start(bf16[32,640]{1,0:T(8,128)(2,1)S(1)} %bitcast.30), channel_id=1, source_target_pairs={{0,32},{32,64},{64,96},{96,128},{128,160},{160,192},{192,224},{1,3... | collective-permute-start | bytes 122888 | tf_op jit(solution)/shard_map/ppermute | solution.py:360
  8.1 6.4 %collective-permute-start.3 = (bf16[32,640]{1,0:T(8,128)(2,1)S(1)}, bf16[32,640]{1,0:T(8,128)(2,1)S(1)}, u32[]{:S(2)}, u32[]{:S(2)}) collective-permute-start(bf16[32,640]{1,0:T(8,128)(2,1)S(1)} %bitcast.29), channel_id=1, source_target_pairs={{32,0},{64,32},{96,64},{128,96},{160,128},{192,160},{224,192},{33,... | collective-permute-start | bytes 122888 | tf_op jit(solution)/shard_map/ppermute | solution.py:361
  11.8 10.4 %collective-permute-start.7 = (bf16[192,640]{1,0:T(8,128)(2,1)}, bf16[192,640]{1,0:T(8,128)(2,1)S(1)}, u32[]{:S(2)}, u32[]{:S(2)}) collective-permute-start(bf16[192,640]{1,0:T(8,128)(2,1)} %bitcast.18), channel_id=1, source_target_pairs={{0,32},{32,0},{1,33},{33,1},{2,34},{34,2},{3,35},{35,3},{4,36},{36... | collective-permute-start | bytes 737288 | tf_op jit(solution)/shard_map/ppermute | solution.py:44
  13.9 8.3 %collective-permute-start.6 = (bf16[16,640]{1,0:T(8,128)(2,1)S(1)}, bf16[16,640]{1,0:T(8,128)(2,1)S(1)}, u32[]{:S(2)}, u32[]{:S(2)}) collective-permute-start(bf16[16,640]{1,0:T(8,128)(2,1)S(1)} %pad.4.rest_0_.own_e), channel_id=1, source_target_pairs={{0,16},{8,24},{16,0},{24,8},{1,17},{9,25},{17,1},{25,9},{2,18},{10... | collective-permute-start | bytes 61448 | tf_op jit(solution)/shard_map/ppermute | solution.py:44
  17.4 7.0 %collective-permute-start.4 = (bf16[80,640]{1,0:T(8,128)(2,1)S(1)}, bf16[80,640]{1,0:T(8,128)(2,1)S(1)}, u32[]{:S(2)}, u32[]{:S(2)}) collective-permute-start(bf16[80,640]{1,0:T(8,128)(2,1)S(1)} %get-tuple-element.39), channel_id=1, source_target_pairs={{0,8},{8,16},{16,24},{24,0},{1,9},{9,17},{17,25},{25,1},{2,10},{10... | collective-permute-start | bytes 307208 | tf_op jit(solution)/shard_map/ppermute | solution.py:44
  19.4 5.9 %collective-permute-start.5 = (bf16[80,640]{1,0:T(8,128)(2,1)S(1)}, bf16[80,640]{1,0:T(8,128)(2,1)S(1)}, u32[]{:S(2)}, u32[]{:S(2)}) collective-permute-start(bf16[80,640]{1,0:T(8,128)(2,1)S(1)} %get-tuple-element.40), channel_id=1, source_target_pairs={{0,24},{8,0},{16,8},{24,16},{1,25},{9,1},{17,9},{25,17},{2,26},{10... | collective-permute-start | bytes 307208 | tf_op jit(solution)/shard_map/ppermute | solution.py:44
  21.5 3.9 %copy-start.2 = (bf16[1,12,16,640]{3,2,1,0:T(8,128)(2,1)S(1)}, bf16[1,12,16,640]{3,2,1,0:T(8,128)(2,1)}, u32[]{:S(2)}) copy-start(bf16[1,12,16,640]{3,2,1,0:T(8,128)(2,1)} %param.7) | copy-start | bytes 737284
  32.1 2.3 %collective-permute-start.14 = (bf16[192,1920]{1,0:T(8,128)(2,1)S(1)}, bf16[192,1920]{1,0:T(8,128)(2,1)S(1)}, u32[]{:S(2)}, u32[]{:S(2)}) collective-permute-start(bf16[192,1920]{1,0:T(8,128)(2,1)S(1)} %get-tuple-element.49), channel_id=1, source_target_pairs={{0,32},{32,0},{1,33},{33,1},{2,34},{34,2},{3,35},{35,3},{4,36},{36... | collective-permute-start | bytes 2211848 | tf_op jit(solution)/shard_map/ppermute | solution.py:44
  32.2 10.8 %collective-permute-start.21 = (bf16[192,2176]{1,0:T(8,128)(2,1)S(1)}, bf16[192,2176]{1,0:T(8,128)(2,1)S(1)}, u32[]{:S(2)}, u32[]{:S(2)}) collective-permute-start(bf16[192,2176]{1,0:T(8,128)(2,1)S(1)} %get-tuple-element.61), channel_id=1, source_target_pairs={{0,32},{32,0},{1,33},{33,1},{2,34},{34,2},{3,35},{35,3},{4,36},{36... | collective-permute-start | bytes 2506760 | tf_op jit(solution)/shard_map/ppermute | solution.py:44
  37.3 12.8 %collective-permute-start.15 = (bf16[320,640]{1,0:T(8,128)(2,1)S(1)}, bf16[320,640]{1,0:T(8,128)(2,1)S(1)}, u32[]{:S(2)}, u32[]{:S(2)}) collective-permute-start(bf16[320,640]{1,0:T(8,128)(2,1)S(1)} %get-tuple-element.53), channel_id=1, source_target_pairs={{0,2},{2,4},{4,6},{6,0},{1,3},{3,5},{5,7},{7,1},{8,10},{10,12},{12... | collective-permute-start | bytes 1228808 | tf_op jit(solution)/shard_map/ppermute | solution.py:44
  38.8 21.0 %collective-permute-start.16 = (bf16[320,640]{1,0:T(8,128)(2,1)S(1)}, bf16[320,640]{1,0:T(8,128)(2,1)S(1)}, u32[]{:S(2)}, u32[]{:S(2)}) collective-permute-start(bf16[320,640]{1,0:T(8,128)(2,1)S(1)} %get-tuple-element.54), channel_id=1, source_target_pairs={{0,4},{2,6},{4,0},{6,2},{1,5},{3,7},{5,1},{7,3},{8,12},{10,14},{12... | collective-permute-start | bytes 1228808 | tf_op jit(solution)/shard_map/ppermute | solution.py:44
  41.6 18.3 %collective-permute-start.17 = (bf16[320,640]{1,0:T(8,128)(2,1)S(1)}, bf16[320,640]{1,0:T(8,128)(2,1)S(1)}, u32[]{:S(2)}, u32[]{:S(2)}) collective-permute-start(bf16[320,640]{1,0:T(8,128)(2,1)S(1)} %get-tuple-element.55), channel_id=1, source_target_pairs={{0,6},{2,0},{4,2},{6,4},{1,7},{3,1},{5,3},{7,5},{8,14},{10,8},{12,... | collective-permute-start | bytes 1228808 | tf_op jit(solution)/shard_map/ppermute | solution.py:44
  44.9 18.4 %collective-permute-start.22 = (bf16[320,640]{1,0:T(8,128)(2,1)S(1)}, bf16[320,640]{1,0:T(8,128)(2,1)S(1)}, u32[]{:S(2)}, u32[]{:S(2)}) collective-permute-start(bf16[320,640]{1,0:T(8,128)(2,1)S(1)} %get-tuple-element.63), channel_id=1, source_target_pairs={{0,64},{64,128},{128,192},{192,0},{1,65},{65,129},{129,193},{193,1... | collective-permute-start | bytes 1228808 | tf_op jit(solution)/shard_map/ppermute | solution.py:44
  46.5 19.2 %collective-permute-start.23 = (bf16[320,640]{1,0:T(8,128)(2,1)S(1)}, bf16[320,640]{1,0:T(8,128)(2,1)S(1)}, u32[]{:S(2)}, u32[]{:S(2)}) collective-permute-start(bf16[320,640]{1,0:T(8,128)(2,1)S(1)} %get-tuple-element.64), channel_id=1, source_target_pairs={{0,128},{64,192},{128,0},{192,64},{1,129},{65,193},{129,1},{193,65... | collective-permute-start | bytes 1228808 | tf_op jit(solution)/shard_map/ppermute | solution.py:44
  50.1 18.3 %collective-permute-start.24 = (bf16[320,640]{1,0:T(8,128)(2,1)S(1)}, bf16[320,640]{1,0:T(8,128)(2,1)S(1)}, u32[]{:S(2)}, u32[]{:S(2)}) collective-permute-start(bf16[320,640]{1,0:T(8,128)(2,1)S(1)} %get-tuple-element.65), channel_id=1, source_target_pairs={{0,192},{64,0},{128,64},{192,128},{1,193},{65,1},{129,65},{193,129... | collective-permute-start | bytes 1228808 | tf_op jit(solution)/shard_map/ppermute | solution.py:44
  60.8 9.8 %collective-permute-start.18 = (bf16[80,640]{1,0:T(8,128)(2,1)S(1)}, bf16[80,640]{1,0:T(8,128)(2,1)S(1)}, u32[]{:S(2)}, u32[]{:S(2)}) collective-permute-start(bf16[80,640]{1,0:T(8,128)(2,1)S(1)} %get-tuple-element.57), channel_id=1, source_target_pairs={{0,64},{64,128},{128,192},{192,0},{1,65},{65,129},{129,193},{193,1... | collective-permute-start | bytes 307208 | tf_op jit(solution)/shard_map/ppermute | solution.py:44
  62.4 10.3 %collective-permute-start.19 = (bf16[80,640]{1,0:T(8,128)(2,1)S(1)}, bf16[80,640]{1,0:T(8,128)(2,1)S(1)}, u32[]{:S(2)}, u32[]{:S(2)}) collective-permute-start(bf16[80,640]{1,0:T(8,128)(2,1)S(1)} %get-tuple-element.58), channel_id=1, source_target_pairs={{0,128},{64,192},{128,0},{192,64},{1,129},{65,193},{129,1},{193,65... | collective-permute-start | bytes 307208 | tf_op jit(solution)/shard_map/ppermute | solution.py:44
  63.3 9.4 %collective-permute-start.20 = (bf16[80,640]{1,0:T(8,128)(2,1)S(1)}, bf16[80,640]{1,0:T(8,128)(2,1)S(1)}, u32[]{:S(2)}, u32[]{:S(2)}) collective-permute-start(bf16[80,640]{1,0:T(8,128)(2,1)S(1)} %get-tuple-element.59), channel_id=1, source_target_pairs={{0,192},{64,0},{128,64},{192,128},{1,193},{65,1},{129,65},{193,129... | collective-permute-start | bytes 307208 | tf_op jit(solution)/shard_map/ppermute | solution.py:44
  69.4 8.2 %collective-permute-start.25 = (bf16[80,640]{1,0:T(8,128)(2,1)S(1)}, bf16[80,640]{1,0:T(8,128)(2,1)S(1)}, u32[]{:S(2)}, u32[]{:S(2)}) collective-permute-start(bf16[80,640]{1,0:T(8,128)(2,1)S(1)} %get-tuple-element.67), channel_id=1, source_target_pairs={{0,2},{2,4},{4,6},{6,0},{1,3},{3,5},{5,7},{7,1},{8,10},{10,12},{12... | collective-permute-start | bytes 307208 | tf_op jit(solution)/shard_map/ppermute | solution.py:44
  69.9 7.7 %collective-permute-start.26 = (bf16[80,640]{1,0:T(8,128)(2,1)S(1)}, bf16[80,640]{1,0:T(8,128)(2,1)S(1)}, u32[]{:S(2)}, u32[]{:S(2)}) collective-permute-start(bf16[80,640]{1,0:T(8,128)(2,1)S(1)} %get-tuple-element.68), channel_id=1, source_target_pairs={{0,4},{2,6},{4,0},{6,2},{1,5},{3,7},{5,1},{7,3},{8,12},{10,14},{12... | collective-permute-start | bytes 307208 | tf_op jit(solution)/shard_map/ppermute | solution.py:44
  70.6 7.6 %collective-permute-start.27 = (bf16[80,640]{1,0:T(8,128)(2,1)S(1)}, bf16[80,640]{1,0:T(8,128)(2,1)S(1)}, u32[]{:S(2)}, u32[]{:S(2)}) collective-permute-start(bf16[80,640]{1,0:T(8,128)(2,1)S(1)} %get-tuple-element.69), channel_id=1, source_target_pairs={{0,6},{2,0},{4,2},{6,4},{1,7},{3,1},{5,3},{7,5},{8,14},{10,8},{12,... | collective-permute-start | bytes 307208 | tf_op jit(solution)/shard_map/ppermute | solution.py:44
  79.1 36.8 %all-to-all-start = ((bf16[8,20,640]{2,1,0:T(8,128)(2,1)}), bf16[8,20,640]{2,1,0:T(8,128)(2,1)S(1)}, u32[]{:S(2)}, u32[]{:S(2)}) async-start(bf16[8,20,640]{2,1,0:T(8,128)(2,1)} %shard_map.119), calls=%async_computation | async-start | bytes 491520 | tf_op jit(solution)/shard_map/all_to_all | solution.py:475
  85.3 12.4 %collective-permute-start.9 = (bf16[192,640]{1,0:T(8,128)(2,1)S(1)}, bf16[192,640]{1,0:T(8,128)(2,1)S(1)}, u32[]{:S(2)}, u32[]{:S(2)}) collective-permute-start(bf16[192,640]{1,0:T(8,128)(2,1)S(1)} %get-tuple-element.43.tile), channel_id=1, source_target_pairs={{0,24},{8,0},{16,8},{24,16},{1,25},{9,1},{17,9},{25,17},{2,26},{10... | collective-permute-start | bytes 737288 | tf_op jit(solution)/shard_map/ppermute | solution.py:44
  89.1 15.3 %collective-permute-start.8 = (bf16[192,640]{1,0:T(8,128)(2,1)S(1)}, bf16[192,640]{1,0:T(8,128)(2,1)S(1)}, u32[]{:S(2)}, u32[]{:S(2)}) collective-permute-start(bf16[192,640]{1,0:T(8,128)(2,1)S(1)} %get-tuple-element.43.tile), channel_id=1, source_target_pairs={{0,8},{8,16},{16,24},{24,0},{1,9},{9,17},{17,25},{25,1},{2,10},{10... | collective-permute-start | bytes 737288 | tf_op jit(solution)/shard_map/ppermute | solution.py:44
  89.1 5.6 %collective-permute-start.10 = (bf16[40,640]{1,0:T(8,128)(2,1)S(1)}, bf16[40,640]{1,0:T(8,128)(2,1)S(1)}, u32[]{:S(2)}, u32[]{:S(2)}) collective-permute-start(bf16[40,640]{1,0:T(8,128)(2,1)S(1)} %get-tuple-element.44), channel_id=1, source_target_pairs={{0,32},{32,64},{64,96},{96,128},{128,160},{160,192},{192,224},{1,3... | collective-permute-start | bytes 153608 | tf_op jit(solution)/shard_map/ppermute | solution.py:360
  91.0 5.4 %collective-permute-start.11 = (bf16[40,640]{1,0:T(8,128)(2,1)S(1)}, bf16[40,640]{1,0:T(8,128)(2,1)S(1)}, u32[]{:S(2)}, u32[]{:S(2)}) collective-permute-start(bf16[40,640]{1,0:T(8,128)(2,1)S(1)} %get-tuple-element.45), channel_id=1, source_target_pairs={{32,0},{64,32},{96,64},{128,96},{160,128},{192,160},{224,192},{33,... | collective-permute-start | bytes 153608 | tf_op jit(solution)/shard_map/ppermute | solution.py:361
  105.0 6.3 %collective-permute-start.12 = (bf16[64,640]{1,0:T(8,128)(2,1)S(1)}, bf16[64,640]{1,0:T(8,128)(2,1)S(1)}, u32[]{:S(2)}, u32[]{:S(2)}) collective-permute-start(bf16[64,640]{1,0:T(8,128)(2,1)S(1)} %get-tuple-element.46), channel_id=1, source_target_pairs={{0,8},{8,16},{16,24},{24,0},{1,9},{9,17},{17,25},{25,1},{2,10},{10... | collective-permute-start | bytes 245768 | tf_op jit(solution)/shard_map/ppermute | solution.py:44
  105.1 6.2 %collective-permute-start.13 = (bf16[64,640]{1,0:T(8,128)(2,1)S(1)}, bf16[64,640]{1,0:T(8,128)(2,1)S(1)}, u32[]{:S(2)}, u32[]{:S(2)}) collective-permute-start(bf16[64,640]{1,0:T(8,128)(2,1)S(1)} %get-tuple-element.47), channel_id=1, source_target_pairs={{0,24},{8,0},{16,8},{24,16},{1,25},{9,1},{17,9},{25,17},{2,26},{10... | collective-permute-start | bytes 245768 | tf_op jit(solution)/shard_map/ppermute | solution.py:44

commit v7 on v6

--- a/solution.py
+++ b/solution.py
@@ -133,9 +133,9 @@
 
 def forward_kernel(
     place, tile, left, right, top, bottom, left_side, right_side, far_e, own_e,
-    tangent, hidden_grad, conv_hbm, in_hbm, out_hbm,
-    out, blend_grad, mine, mine_mlp, theirs, theirs_mlp, to_up, to_down,
-    win, band, coef, spread, conv_weight, weight_in, weight_out, sems
+    tangent, hidden_grad, conv_hbm, in_hbm,
+    hidden_all, blend_grad, mine, mine_mlp, theirs, theirs_mlp, to_up, to_down,
+    win, band, coef, spread, conv_weight, weight_in, sems
 ):
     lat = place[0]
     lon = place[1]
@@ -143,7 +143,7 @@
     loads = [
         pltpu.make_async_copy(source, target, sems.at[i])
         for i, (source, target) in enumerate(
-            ((conv_hbm, conv_weight), (in_hbm, weight_in), (out_hbm, weight_out))
+            ((conv_hbm, conv_weight), (in_hbm, weight_in))
         )
     ]
     for load in loads:
@@ -173,10 +173,7 @@
     preact = dot(blended, weight_in[...], ((1,), (0,)))
     cdf = 0.5 * (1.0 + lax.erf(preact * half_root))
     hidden = (preact * cdf).astype(bf16)
-    loads[2].wait()
-    out[...] = (
-        blended.astype(f32) + dot(hidden, weight_out[...], ((1,), (0,)))
-    ).astype(bf16)
+    hidden_all[...] = hidden
     slope = cdf + preact * jnp.exp(-0.5 * preact * preact) * gauss_norm
     preact_grad = (hidden_grad[...] * slope).astype(bf16)
     grad = (
@@ -218,6 +215,12 @@
     to_up[RIM : RIM + 8, :] = jnp.concatenate(edges[8:], axis=0).astype(bf16)
     to_down[0:RIM, :] = grad[:RIM, :]
     to_down[RIM : RIM + 8, :] = jnp.concatenate(edges[:8], axis=0).astype(bf16)
+
+
+def block_out_kernel(hidden, mine_mlp, weight_out, out):
+    out[...] = (
+        mine_mlp[:, 0:EMBED].astype(f32) + dot(hidden[...], weight_out[...], ((1,), (0,)))
+    ).astype(bf16)
 
 
 def mlp_grad_kernel(place, mine, other, tangent, other_tangent, order, o0, o1, o2, o3, acc):
@@ -418,9 +421,9 @@
     band = pltpu.VMEM((2, BASIS * LON, 384), bf16)
     edge = struct((RIM + 8, EMBED), bf16)
     parts = (struct((CELLS, CONV_PART), bf16), struct((CELLS, MLP_PART), bf16))
-    block_out, blend_grad, mine, mine_mlp, theirs, theirs_mlp, to_up, to_down = call(
+    hidden, blend_grad, mine, mine_mlp, theirs, theirs_mlp, to_up, to_down = call(
         forward_kernel,
-        (struct((CELLS, EMBED), bf16), struct((CELLS, EMBED), bf16))
+        (struct((CELLS, HIDDEN), bf16), struct((CELLS, EMBED), bf16))
         + parts
         + parts
         + (edge, edge),
@@ -431,11 +434,14 @@
             pltpu.VMEM((CELLS, WIDE), bf16),
             pltpu.VMEM((WIDE, EMBED), bf16),
             pltpu.VMEM((EMBED, HIDDEN), bf16),
-            pltpu.VMEM((HIDDEN, EMBED), bf16),
-            pltpu.SemaphoreType.DMA((3,)),
+            pltpu.SemaphoreType.DMA((2,)),
         ],
         24, place, tile, left, right, top, bottom, left_side, right_side, far_e, own_e,
-        tangent, hidden_grad, in_hbm=(conv_weight, weight_in, weight_out),
+        tangent, hidden_grad, in_hbm=(conv_weight, weight_in),
+    )
+    block_out = call(
+        block_out_kernel, struct((CELLS, EMBED), bf16), [], 8, None,
+        hidden, mine_mlp, weight_out,
     )
     other = shift(theirs, "core", 2, 1)
     other_mlp = shift(theirs_mlp, "core", 2, 1)

time: 117 us -> 116 us (level)
  waiting for transfers between devices: 39.5 us -> 37.5 us
    ppermute x24, waiting for transfers between devices: 37.8 us -> 35.8 us  [shift(): lax.ppermute(block, axis, [(i, (i + step) % count) for i in range(count)])]
    pallas_call x11 -> x12, Pallas kernels: 21.1 us -> 21 us  [call(): pl.pallas_call(kernel, out_shape=outs, in_specs=in_specs, scratch_shapes=...]
  transfers between devices with their start and end apart: 29 -> 29, of which waited for: 13 -> 13; matrix products, arithmetic and copies ran while one was open for 3% -> 3% of each run, Pallas kernels for 11% -> 12%
where the time goes in v7:
time: 116 us; the launch traced here: 115 us
  starting transfers between devices  52 us (45%)
  waiting for transfers between devices  37.5 us (32%)
  Pallas kernels  21 us (18%)
  other arithmetic  1.99 us (2%)
  local copies, waits for them, and re-layouts  1.71 us (1%)
    ppermute x24, waiting for transfers between devices, shift(): lax.ppermute(block, axis, [(i, (i + step) % count) for i in range(count)])  35.8 us
    ppermute x24, starting transfers between devices, shift(): lax.ppermute(block, axis, [(i, (i + step) % count) for i in range(count)])  34.7 us
    pallas_call x12, Pallas kernels, call(): pl.pallas_call(kernel, out_shape=outs, in_specs=in_specs, scratch_shapes=...  21 us
    ppermute x2, starting transfers between devices, neighbours(): bottom = lax.ppermute(to_down, LAT, backward)  7.28 us
    all_to_all x1, starting transfers between devices, block(): lax.all_to_all(packed, ('zl0', 'zl1', 'zhi'), split_axis=0, concat_axis=0...  6.22 us
    ppermute x2, starting transfers between devices, neighbours(): top = lax.ppermute(to_up, LAT, forward)  3.83 us
  transfers between devices with their start and end apart: 29, of which 13 were waited for; matrix products, arithmetic and copies ran while one was open for 3% of the time, Pallas kernels for 12%

profile of v7, /device:TPU:8, one launch (start us, length us, event | category | flops | bytes accessed | tf_op | source)
XLA Modules:
  0.0 115.2 jit_solution(8325494013003743571)
XLA Ops:
  0.7 4.7 %collective-permute-start.1 = (bf16[192,640]{1,0:T(8,128)(2,1)}, bf16[192,640]{1,0:T(8,128)(2,1)S(1)}, u32[]{:S(2)}, u32[]{:S(2)}) collective-permute-start(bf16[192,640]{1,0:T(8,128)(2,1)} %bitcast.22), channel_id=1, source_target_pairs={{0,24},{8,0},{16,8},{24,16},{1,25},{9,1},{17,9},{25,17},{2,26},{10... | collective-permute-start | bytes 737288 | tf_op jit(solution)/shard_map/ppermute | solution.py:44
  5.4 0.9 fusion.21
  6.2 1.9 %collective-permute-start.2 = (bf16[32,640]{1,0:T(8,128)(2,1)S(1)}, bf16[32,640]{1,0:T(8,128)(2,1)S(1)}, u32[]{:S(2)}, u32[]{:S(2)}) collective-permute-start(bf16[32,640]{1,0:T(8,128)(2,1)S(1)} %bitcast.31), channel_id=1, source_target_pairs={{0,32},{32,64},{64,96},{96,128},{128,160},{160,192},{192,224},{1,3... | collective-permute-start | bytes 122888 | tf_op jit(solution)/shard_map/ppermute | solution.py:363
  8.1 3.6 %collective-permute-start.3 = (bf16[32,640]{1,0:T(8,128)(2,1)S(1)}, bf16[32,640]{1,0:T(8,128)(2,1)S(1)}, u32[]{:S(2)}, u32[]{:S(2)}) collective-permute-start(bf16[32,640]{1,0:T(8,128)(2,1)S(1)} %bitcast.30), channel_id=1, source_target_pairs={{32,0},{64,32},{96,64},{128,96},{160,128},{192,160},{224,192},{33,... | collective-permute-start | bytes 122888 | tf_op jit(solution)/shard_map/ppermute | solution.py:364
  11.9 0.7 add_select_fusion
  12.6 0.7 convert_bitcast_fusion
  13.9 0.7 collective-permute-start.6
  14.6 2.2 %collective-permute-done.left = bf16[192,640]{1,0:T(8,128)(2,1)S(1)} collective-permute-done((bf16[192,640]{1,0:T(8,128)(2,1)}, bf16[192,640]{1,0:T(8,128)(2,1)S(1)}, u32[]{:S(2)}, u32[]{:S(2)}) %collective-permute-start) | collective-permute-done | bytes 245792 | tf_op jit(solution)/shard_map/ppermute | solution.py:44
  17.4 2.1 %collective-permute-start.4 = (bf16[80,640]{1,0:T(8,128)(2,1)S(1)}, bf16[80,640]{1,0:T(8,128)(2,1)S(1)}, u32[]{:S(2)}, u32[]{:S(2)}) collective-permute-start(bf16[80,640]{1,0:T(8,128)(2,1)S(1)} %get-tuple-element.39), channel_id=1, source_target_pairs={{0,8},{8,16},{16,24},{24,0},{1,9},{9,17},{17,25},{25,1},{2,10},{10... | collective-permute-start | bytes 307208 | tf_op jit(solution)/shard_map/ppermute | solution.py:44
  19.4 1.8 %collective-permute-start.5 = (bf16[80,640]{1,0:T(8,128)(2,1)S(1)}, bf16[80,640]{1,0:T(8,128)(2,1)S(1)}, u32[]{:S(2)}, u32[]{:S(2)}) collective-permute-start(bf16[80,640]{1,0:T(8,128)(2,1)S(1)} %get-tuple-element.40), channel_id=1, source_target_pairs={{0,24},{8,0},{16,8},{24,16},{1,25},{9,1},{17,9},{25,17},{2,26},{10... | collective-permute-start | bytes 307208 | tf_op jit(solution)/shard_map/ppermute | solution.py:44
  21.5 0.7 shard_map.111.hidden_grad
  22.2 0.7 copy-done.7
  22.9 1.5 %collective-permute-done.4.left_side.left_e = bf16[80,640]{1,0:T(8,128)(2,1)S(1)} collective-permute-done((bf16[80,640]{1,0:T(8,128)(2,1)S(1)}, bf16[80,640]{1,0:T(8,128)(2,1)S(1)}, u32[]{:S(2)}, u32[]{:S(2)}) %collective-permute-start.4) | collective-permute-done | bytes 102432 | tf_op jit(solution)/shard_map/ppermute | solution.py:44
  24.4 1.0 collective-permute-done.5.right_side.right_e
  25.4 5.4 %shard_map.112 = (bf16[192,1280]{1,0:T(8,128)(2,1)S(1)}, bf16[192,640]{1,0:T(8,128)(2,1)S(1)}, bf16[192,2176]{1,0:T(8,128)(2,1)S(1)}, bf16[192,1920]{1,0:T(8,128...) custom-call(s32[5]{0:T(128)S(1)} %stack.23.place, ...), custom_call_target="tpu_custom_call" | custom-call | tf_op jit(solution)/shard_map/pallas_call | solution.py:349
  31.4 1.7 %collective-permute-done.14.other = bf16[192,1920]{1,0:T(8,128)(2,1)S(1)} collective-permute-done((bf16[192,1920]{1,0:T(8,128)(2,1)S(1)}, bf16[192,1920]{1,0:T(8,128)(2,1)S(1)}, u32[]{:S(2)}, u32[]{:S(2)}) %collective-permute-start.14) | collective-permute-done | bytes 737312 | tf_op jit(solution)/shard_map/ppermute | solution.py:44
  33.1 2.9 %shard_map.116 = (f32[320,640]{1,0:T(8,128)S(1)}, bf16[320,640]{1,0:T(8,128)(2,1)S(1)}, bf16[320,640]{1,0:T(8,128)(2,1)S(1)}, bf16[320,640]{1,0:T(8,128)(2,1)S(1)}) custom-call(s32[5]{0:T(128)S(1)} %stack.23.place, bf16[192,1920]{1,0:T(8,128)(2,1)S(1)} %get-tuple-element.43.mine_mlp.mine, bf16[192,1920]{1,0:T(8,128)(2,1)S(1)} %collective-permute-done.14.other, ...), custom_call_target="tpu_custom_call" | custom-call | tf_op jit(solution)/shard_map/pallas_call | solution.py:349
  36.0 1.6 %collective-permute-start.15 = (bf16[320,640]{1,0:T(8,128)(2,1)S(1)}, bf16[320,640]{1,0:T(8,128)(2,1)S(1)}, u32[]{:S(2)}, u32[]{:S(2)}) collective-permute-start(bf16[320,640]{1,0:T(8,128)(2,1)S(1)} %get-tuple-element.53), channel_id=1, source_target_pairs={{0,2},{2,4},{4,6},{6,0},{1,3},{3,5},{5,7},{7,1},{8,10},{10,12},{12... | collective-permute-start | bytes 1228808 | tf_op jit(solution)/shard_map/ppermute | solution.py:44
  37.5 2.7 %collective-permute-start.16 = (bf16[320,640]{1,0:T(8,128)(2,1)S(1)}, bf16[320,640]{1,0:T(8,128)(2,1)S(1)}, u32[]{:S(2)}, u32[]{:S(2)}) collective-permute-start(bf16[320,640]{1,0:T(8,128)(2,1)S(1)} %get-tuple-element.54), channel_id=1, source_target_pairs={{0,4},{2,6},{4,0},{6,2},{1,5},{3,7},{5,1},{7,3},{8,12},{10,14},{12... | collective-permute-start | bytes 1228808 | tf_op jit(solution)/shard_map/ppermute | solution.py:44
  40.3 1.4 %collective-permute-start.17 = (bf16[320,640]{1,0:T(8,128)(2,1)S(1)}, bf16[320,640]{1,0:T(8,128)(2,1)S(1)}, u32[]{:S(2)}, u32[]{:S(2)}) collective-permute-start(bf16[320,640]{1,0:T(8,128)(2,1)S(1)} %get-tuple-element.55), channel_id=1, source_target_pairs={{0,6},{2,0},{4,2},{6,4},{1,7},{3,1},{5,3},{7,5},{8,14},{10,8},{12,... | collective-permute-start | bytes 1228808 | tf_op jit(solution)/shard_map/ppermute | solution.py:44
  41.7 1.9 %shard_map.118 = (f32[320,640]{1,0:T(8,128)S(1)}, bf16[320,640]{1,0:T(8,128)(2,1)S(1)}, bf16[320,640]{1,0:T(8,128)(2,1)S(1)}, bf16[320,640]{1,0:T(8,128)(2,1)S(1)}) custom-call(s32[5]{0:T(128)S(1)} %stack.23.place, bf16[192,2176]{1,0:T(8,128)(2,1)S(1)} %get-tuple-element.60.mine, bf16[192,2176]{1,0:T(8,128)(2,1)S(1)} %collective-permute-done.21.other), custom_call_target="tpu_custom_call" | custom-call | tf_op jit(solution)/shard_map/pallas_call | solution.py:349
  43.6 1.7 %collective-permute-start.22 = (bf16[320,640]{1,0:T(8,128)(2,1)S(1)}, bf16[320,640]{1,0:T(8,128)(2,1)S(1)}, u32[]{:S(2)}, u32[]{:S(2)}) collective-permute-start(bf16[320,640]{1,0:T(8,128)(2,1)S(1)} %get-tuple-element.63), channel_id=1, source_target_pairs={{0,64},{64,128},{128,192},{192,0},{1,65},{65,129},{129,193},{193,1... | collective-permute-start | bytes 1228808 | tf_op jit(solution)/shard_map/ppermute | solution.py:44
  45.3 0.9 collective-permute-start.23
  46.1 2.6 %collective-permute-done.15.r1 = bf16[320,640]{1,0:T(8,128)(2,1)S(1)} collective-permute-done((bf16[320,640]{1,0:T(8,128)(2,1)S(1)}, bf16[320,640]{1,0:T(8,128)(2,1)S(1)}, u32[]{:S(2)}, u32[]{:S(2)}) %collective-permute-start.15) | collective-permute-done | bytes 409632 | tf_op jit(solution)/shard_map/ppermute | solution.py:44
  49.1 9.4 %collective-permute-done.16.r2 = bf16[320,640]{1,0:T(8,128)(2,1)S(1)} collective-permute-done((bf16[320,640]{1,0:T(8,128)(2,1)S(1)}, bf16[320,640]{1,0:T(8,128)(2,1)S(1)}, u32[]{:S(2)}, u32[]{:S(2)}) %collective-permute-start.16) | collective-permute-done | bytes 409632 | tf_op jit(solution)/shard_map/ppermute | solution.py:44
  58.5 0.9 shard_map.117
  59.4 1.7 %collective-permute-start.18 = (bf16[80,640]{1,0:T(8,128)(2,1)S(1)}, bf16[80,640]{1,0:T(8,128)(2,1)S(1)}, u32[]{:S(2)}, u32[]{:S(2)}) collective-permute-start(bf16[80,640]{1,0:T(8,128)(2,1)S(1)} %get-tuple-element.57), channel_id=1, source_target_pairs={{0,64},{64,128},{128,192},{192,0},{1,65},{65,129},{129,193},{193,1... | collective-permute-start | bytes 307208 | tf_op jit(solution)/shard_map/ppermute | solution.py:44
  61.1 0.9 collective-permute-start.19
  62.0 2.5 %collective-permute-start.20 = (bf16[80,640]{1,0:T(8,128)(2,1)S(1)}, bf16[80,640]{1,0:T(8,128)(2,1)S(1)}, u32[]{:S(2)}, u32[]{:S(2)}) collective-permute-start(bf16[80,640]{1,0:T(8,128)(2,1)S(1)} %get-tuple-element.59), channel_id=1, source_target_pairs={{0,192},{64,0},{128,64},{192,128},{1,193},{65,1},{129,65},{193,129... | collective-permute-start | bytes 307208 | tf_op jit(solution)/shard_map/ppermute | solution.py:44
  64.5 2.7 %collective-permute-done.24.r3 = bf16[320,640]{1,0:T(8,128)(2,1)S(1)} collective-permute-done((bf16[320,640]{1,0:T(8,128)(2,1)S(1)}, bf16[320,640]{1,0:T(8,128)(2,1)S(1)}, u32[]{:S(2)}, u32[]{:S(2)}) %collective-permute-start.24) | collective-permute-done | bytes 409632 | tf_op jit(solution)/shard_map/ppermute | solution.py:44
  67.1 1.0 shard_map.119
  68.7 0.6 collective-permute-start.26
  69.3 2.2 %collective-permute-start.27 = (bf16[80,640]{1,0:T(8,128)(2,1)S(1)}, bf16[80,640]{1,0:T(8,128)(2,1)S(1)}, u32[]{:S(2)}, u32[]{:S(2)}) collective-permute-start(bf16[80,640]{1,0:T(8,128)(2,1)S(1)} %get-tuple-element.69), channel_id=1, source_target_pairs={{0,6},{2,0},{4,2},{6,4},{1,7},{3,1},{5,3},{7,5},{8,14},{10,8},{12,... | collective-permute-start | bytes 307208 | tf_op jit(solution)/shard_map/ppermute | solution.py:44
  71.4 4.8 %collective-permute-done.25.c1 = bf16[80,640]{1,0:T(8,128)(2,1)S(1)} collective-permute-done((bf16[80,640]{1,0:T(8,128)(2,1)S(1)}, bf16[80,640]{1,0:T(8,128)(2,1)S(1)}, u32[]{:S(2)}, u32[]{:S(2)}) %collective-permute-start.25) | collective-permute-done | bytes 102432 | tf_op jit(solution)/shard_map/ppermute | solution.py:44
  76.3 0.6 collective-permute-done.27.c3
  76.9 0.9 shard_map.120
  77.8 6.2 %all-to-all-start = ((bf16[8,20,640]{2,1,0:T(8,128)(2,1)}), bf16[8,20,640]{2,1,0:T(8,128)(2,1)S(1)}, u32[]{:S(2)}, u32[]{:S(2)}) async-start(bf16[8,20,640]{2,1,0:T(8,128)(2,1)} %shard_map.120), calls=%async_computation | async-start | bytes 491520 | tf_op jit(solution)/shard_map/all_to_all | solution.py:481
  84.0 3.8 %collective-permute-start.9 = (bf16[192,640]{1,0:T(8,128)(2,1)}, bf16[192,640]{1,0:T(8,128)(2,1)S(1)}, u32[]{:S(2)}, u32[]{:S(2)}) collective-permute-start(bf16[192,640]{1,0:T(8,128)(2,1)} %copy-done.5), channel_id=1, source_target_pairs={{0,24},{8,0},{16,8},{24,16},{1,25},{9,1},{17,9},{25,17},{2,26},{10... | collective-permute-start | bytes 737288 | tf_op jit(solution)/shard_map/ppermute | solution.py:44
  87.9 1.9 %collective-permute-start.10 = (bf16[40,640]{1,0:T(8,128)(2,1)S(1)}, bf16[40,640]{1,0:T(8,128)(2,1)S(1)}, u32[]{:S(2)}, u32[]{:S(2)}) collective-permute-start(bf16[40,640]{1,0:T(8,128)(2,1)S(1)} %get-tuple-element.45), channel_id=1, source_target_pairs={{0,32},{32,64},{64,96},{96,128},{128,160},{160,192},{192,224},{1,3... | collective-permute-start | bytes 153608 | tf_op jit(solution)/shard_map/ppermute | solution.py:363
  89.8 3.6 %collective-permute-start.11 = (bf16[40,640]{1,0:T(8,128)(2,1)S(1)}, bf16[40,640]{1,0:T(8,128)(2,1)S(1)}, u32[]{:S(2)}, u32[]{:S(2)}) collective-permute-start(bf16[40,640]{1,0:T(8,128)(2,1)S(1)} %get-tuple-element.46), channel_id=1, source_target_pairs={{32,0},{64,32},{96,64},{128,96},{160,128},{192,160},{224,192},{33,... | collective-permute-start | bytes 153608 | tf_op jit(solution)/shard_map/ppermute | solution.py:364
  93.4 1.7 %collective-permute-done.11.bottom = bf16[40,640]{1,0:T(8,128)(2,1)S(1)} collective-permute-done((bf16[40,640]{1,0:T(8,128)(2,1)S(1)}, bf16[40,640]{1,0:T(8,128)(2,1)S(1)}, u32[]{:S(2)}, u32[]{:S(2)}) %collective-permute-start.11) | collective-permute-done | bytes 51232 | tf_op jit(solution)/shard_map/ppermute | solution.py:364
  95.2 1.2 %collective-permute-done.9.right = bf16[192,640]{1,0:T(8,128)(2,1)S(1)} collective-permute-done((bf16[192,640]{1,0:T(8,128)(2,1)}, bf16[192,640]{1,0:T(8,128)(2,1)S(1)}, u32[]{:S(2)}, u32[]{:S(2)}) %collective-permute-start.9) | collective-permute-done | bytes 245792 | tf_op jit(solution)/shard_map/ppermute | solution.py:44
  96.4 6.8 %collective-permute-done.8.left = bf16[192,640]{1,0:T(8,128)(2,1)S(1)} collective-permute-done((bf16[192,640]{1,0:T(8,128)(2,1)}, bf16[192,640]{1,0:T(8,128)(2,1)S(1)}, u32[]{:S(2)}, u32[]{:S(2)}) %collective-permute-start.8) | collective-permute-done | bytes 245792 | tf_op jit(solution)/shard_map/ppermute | solution.py:44
  103.9 3.8 %collective-permute-start.13 = (bf16[64,640]{1,0:T(8,128)(2,1)S(1)}, bf16[64,640]{1,0:T(8,128)(2,1)S(1)}, u32[]{:S(2)}, u32[]{:S(2)}) collective-permute-start(bf16[64,640]{1,0:T(8,128)(2,1)S(1)} %get-tuple-element.48), channel_id=1, source_target_pairs={{0,24},{8,0},{16,8},{24,16},{1,25},{9,1},{17,9},{25,17},{2,26},{10... | collective-permute-start | bytes 245768 | tf_op jit(solution)/shard_map/ppermute | solution.py:44
  107.7 1.3 %shard_map.113 = bf16[192,640]{1,0:T(8,128)(2,1)} custom-call(bf16[192,1280]{1,0:T(8,128)(2,1)S(1)} %copy-done.3, bf16[192,1920]{1,0:T(8,128)(2,1)S(1)} %get-tuple-element.43.mine_mlp.mine, bf16[1280,640]{1,0:T(8,128)(2,1)S(1)} %copy-done), custom_call_target="tpu_custom_call" | custom-call | tf_op jit(solution)/shard_map/pallas_call | solution.py:349
  108.9 1.2 collective-permute-done.12.left_side
  110.1 4.5 %shard_map.115 = bf16[192,640]{1,0:T(8,128)(2,1)} custom-call(s32[5]{0:T(128)S(1)} %stack.23.place, bf16[192,640]{1,0:T(8,128)(2,1)S(1)} %copy-done.6, bf16[192,640]{1,0:T(8,128)(2,1)S(1)} %collective-permute-done.8.left, bf16[192,640]{1,0:T(8,128)(2,1)S(1)} %collective-permute-done.9.right, bf16[40,640]{1,0:T(8,128)(2,1)S(1)} %collective-permute-done.10.top, ...), custom_call_target="tpu_custom_call" | custom-call | tf_op jit(solution)/shard_map/pallas_call | solution.py:349
  114.6 0.6 shard_map.121
  (54 shorter events, 3.6 us)
Async XLA Ops:
  0.6 20.8 %copy-start.1 = (bf16[1,12,16,640]{3,2,1,0:T(8,128)(2,1)S(1)}, bf16[1,12,16,640]{3,2,1,0:T(8,128)(2,1)}, u32[]{:S(2)}) copy-start(bf16[1,12,16,640]{3,2,1,0:T(8,128)(2,1)} %param.13) | copy-start | bytes 737284
  0.6 20.8 %copy-start = (bf16[1280,640]{1,0:T(8,128)(2,1)S(1)}, bf16[1280,640]{1,0:T(8,128)(2,1)}, u32[]{:S(2)}) copy-start(bf16[1280,640]{1,0:T(8,128)(2,1)} %weight_out.3) | copy-start | bytes 4915204
  0.7 13.9 %collective-permute-start.1 = (bf16[192,640]{1,0:T(8,128)(2,1)}, bf16[192,640]{1,0:T(8,128)(2,1)S(1)}, u32[]{:S(2)}, u32[]{:S(2)}) collective-permute-start(bf16[192,640]{1,0:T(8,128)(2,1)} %bitcast.22), channel_id=1, source_target_pairs={{0,24},{8,0},{16,8},{24,16},{1,25},{9,1},{17,9},{25,17},{2,26},{10... | collective-permute-start | bytes 737288 | tf_op jit(solution)/shard_map/ppermute | solution.py:44
  5.4 11.4 %collective-permute-start = (bf16[192,640]{1,0:T(8,128)(2,1)}, bf16[192,640]{1,0:T(8,128)(2,1)S(1)}, u32[]{:S(2)}, u32[]{:S(2)}) collective-permute-start(bf16[192,640]{1,0:T(8,128)(2,1)} %bitcast.23), channel_id=1, source_target_pairs={{0,8},{8,16},{16,24},{24,0},{1,9},{9,17},{17,25},{25,1},{2,10},{10... | collective-permute-start | bytes 737288 | tf_op jit(solution)/shard_map/ppermute | solution.py:44
  6.2 7.7 %collective-permute-start.2 = (bf16[32,640]{1,0:T(8,128)(2,1)S(1)}, bf16[32,640]{1,0:T(8,128)(2,1)S(1)}, u32[]{:S(2)}, u32[]{:S(2)}) collective-permute-start(bf16[32,640]{1,0:T(8,128)(2,1)S(1)} %bitcast.31), channel_id=1, source_target_pairs={{0,32},{32,64},{64,96},{96,128},{128,160},{160,192},{192,224},{1,3... | collective-permute-start | bytes 122888 | tf_op jit(solution)/shard_map/ppermute | solution.py:363
  8.1 6.4 %collective-permute-start.3 = (bf16[32,640]{1,0:T(8,128)(2,1)S(1)}, bf16[32,640]{1,0:T(8,128)(2,1)S(1)}, u32[]{:S(2)}, u32[]{:S(2)}) collective-permute-start(bf16[32,640]{1,0:T(8,128)(2,1)S(1)} %bitcast.30), channel_id=1, source_target_pairs={{32,0},{64,32},{96,64},{128,96},{160,128},{192,160},{224,192},{33,... | collective-permute-start | bytes 122888 | tf_op jit(solution)/shard_map/ppermute | solution.py:364
  11.8 10.4 %collective-permute-start.7 = (bf16[192,640]{1,0:T(8,128)(2,1)}, bf16[192,640]{1,0:T(8,128)(2,1)S(1)}, u32[]{:S(2)}, u32[]{:S(2)}) collective-permute-start(bf16[192,640]{1,0:T(8,128)(2,1)} %bitcast.18), channel_id=1, source_target_pairs={{0,32},{32,0},{1,33},{33,1},{2,34},{34,2},{3,35},{35,3},{4,36},{36... | collective-permute-start | bytes 737288 | tf_op jit(solution)/shard_map/ppermute | solution.py:44
  13.9 8.3 %collective-permute-start.6 = (bf16[16,640]{1,0:T(8,128)(2,1)S(1)}, bf16[16,640]{1,0:T(8,128)(2,1)S(1)}, u32[]{:S(2)}, u32[]{:S(2)}) collective-permute-start(bf16[16,640]{1,0:T(8,128)(2,1)S(1)} %pad.4.rest_0_.own_e), channel_id=1, source_target_pairs={{0,16},{8,24},{16,0},{24,8},{1,17},{9,25},{17,1},{25,9},{2,18},{10... | collective-permute-start | bytes 61448 | tf_op jit(solution)/shard_map/ppermute | solution.py:44
  17.4 7.0 %collective-permute-start.4 = (bf16[80,640]{1,0:T(8,128)(2,1)S(1)}, bf16[80,640]{1,0:T(8,128)(2,1)S(1)}, u32[]{:S(2)}, u32[]{:S(2)}) collective-permute-start(bf16[80,640]{1,0:T(8,128)(2,1)S(1)} %get-tuple-element.39), channel_id=1, source_target_pairs={{0,8},{8,16},{16,24},{24,0},{1,9},{9,17},{17,25},{25,1},{2,10},{10... | collective-permute-start | bytes 307208 | tf_op jit(solution)/shard_map/ppermute | solution.py:44
  19.4 5.9 %collective-permute-start.5 = (bf16[80,640]{1,0:T(8,128)(2,1)S(1)}, bf16[80,640]{1,0:T(8,128)(2,1)S(1)}, u32[]{:S(2)}, u32[]{:S(2)}) collective-permute-start(bf16[80,640]{1,0:T(8,128)(2,1)S(1)} %get-tuple-element.40), channel_id=1, source_target_pairs={{0,24},{8,0},{16,8},{24,16},{1,25},{9,1},{17,9},{25,17},{2,26},{10... | collective-permute-start | bytes 307208 | tf_op jit(solution)/shard_map/ppermute | solution.py:44
  21.5 3.9 %copy-start.4 = (bf16[1,12,16,640]{3,2,1,0:T(8,128)(2,1)S(1)}, bf16[1,12,16,640]{3,2,1,0:T(8,128)(2,1)}, u32[]{:S(2)}) copy-start(bf16[1,12,16,640]{3,2,1,0:T(8,128)(2,1)} %param.7) | copy-start | bytes 737284
  22.2 0.7 copy-start.7
  24.4 8.7 %copy-start.8 = (bf16[192,640]{1,0:T(8,128)(2,1)S(1)}, bf16[192,640]{1,0:T(8,128)(2,1)}, u32[]{:S(2)}) copy-start(bf16[192,640]{1,0:T(8,128)(2,1)} %copy-done.7) | copy-start | bytes 737284
  30.8 12.8 %copy-start.2 = (bf16[192,1280]{1,0:T(8,128)(2,1)}, bf16[192,1280]{1,0:T(8,128)(2,1)S(1)}, u32[]{:S(2)}) copy-start(bf16[192,1280]{1,0:T(8,128)(2,1)S(1)} %get-tuple-element.42.hidden) | copy-start | bytes 1474564
  30.8 12.8 %copy-start.5 = (bf16[192,640]{1,0:T(8,128)(2,1)}, bf16[192,640]{1,0:T(8,128)(2,1)S(1)}, u32[]{:S(2)}) copy-start(bf16[192,640]{1,0:T(8,128)(2,1)S(1)} %get-tuple-element.44.tile) | copy-start | bytes 737284
  30.8 2.3 %collective-permute-start.14 = (bf16[192,1920]{1,0:T(8,128)(2,1)S(1)}, bf16[192,1920]{1,0:T(8,128)(2,1)S(1)}, u32[]{:S(2)}, u32[]{:S(2)}) collective-permute-start(bf16[192,1920]{1,0:T(8,128)(2,1)S(1)} %get-tuple-element.49), channel_id=1, source_target_pairs={{0,32},{32,0},{1,33},{33,1},{2,34},{34,2},{3,35},{35,3},{4,36},{36... | collective-permute-start | bytes 2211848 | tf_op jit(solution)/shard_map/ppermute | solution.py:44
  30.9 10.8 %collective-permute-start.21 = (bf16[192,2176]{1,0:T(8,128)(2,1)S(1)}, bf16[192,2176]{1,0:T(8,128)(2,1)S(1)}, u32[]{:S(2)}, u32[]{:S(2)}) collective-permute-start(bf16[192,2176]{1,0:T(8,128)(2,1)S(1)} %get-tuple-element.61), channel_id=1, source_target_pairs={{0,32},{32,0},{1,33},{33,1},{2,34},{34,2},{3,35},{35,3},{4,36},{36... | collective-permute-start | bytes 2506760 | tf_op jit(solution)/shard_map/ppermute | solution.py:44
  36.0 12.8 %collective-permute-start.15 = (bf16[320,640]{1,0:T(8,128)(2,1)S(1)}, bf16[320,640]{1,0:T(8,128)(2,1)S(1)}, u32[]{:S(2)}, u32[]{:S(2)}) collective-permute-start(bf16[320,640]{1,0:T(8,128)(2,1)S(1)} %get-tuple-element.53), channel_id=1, source_target_pairs={{0,2},{2,4},{4,6},{6,0},{1,3},{3,5},{5,7},{7,1},{8,10},{10,12},{12... | collective-permute-start | bytes 1228808 | tf_op jit(solution)/shard_map/ppermute | solution.py:44
  37.5 21.0 %collective-permute-start.16 = (bf16[320,640]{1,0:T(8,128)(2,1)S(1)}, bf16[320,640]{1,0:T(8,128)(2,1)S(1)}, u32[]{:S(2)}, u32[]{:S(2)}) collective-permute-start(bf16[320,640]{1,0:T(8,128)(2,1)S(1)} %get-tuple-element.54), channel_id=1, source_target_pairs={{0,4},{2,6},{4,0},{6,2},{1,5},{3,7},{5,1},{7,3},{8,12},{10,14},{12... | collective-permute-start | bytes 1228808 | tf_op jit(solution)/shard_map/ppermute | solution.py:44
  40.3 18.3 %collective-permute-start.17 = (bf16[320,640]{1,0:T(8,128)(2,1)S(1)}, bf16[320,640]{1,0:T(8,128)(2,1)S(1)}, u32[]{:S(2)}, u32[]{:S(2)}) collective-permute-start(bf16[320,640]{1,0:T(8,128)(2,1)S(1)} %get-tuple-element.55), channel_id=1, source_target_pairs={{0,6},{2,0},{4,2},{6,4},{1,7},{3,1},{5,3},{7,5},{8,14},{10,8},{12,... | collective-permute-start | bytes 1228808 | tf_op jit(solution)/shard_map/ppermute | solution.py:44
  43.6 18.4 %collective-permute-start.22 = (bf16[320,640]{1,0:T(8,128)(2,1)S(1)}, bf16[320,640]{1,0:T(8,128)(2,1)S(1)}, u32[]{:S(2)}, u32[]{:S(2)}) collective-permute-start(bf16[320,640]{1,0:T(8,128)(2,1)S(1)} %get-tuple-element.63), channel_id=1, source_target_pairs={{0,64},{64,128},{128,192},{192,0},{1,65},{65,129},{129,193},{193,1... | collective-permute-start | bytes 1228808 | tf_op jit(solution)/shard_map/ppermute | solution.py:44
  45.3 19.2 %collective-permute-start.23 = (bf16[320,640]{1,0:T(8,128)(2,1)S(1)}, bf16[320,640]{1,0:T(8,128)(2,1)S(1)}, u32[]{:S(2)}, u32[]{:S(2)}) collective-permute-start(bf16[320,640]{1,0:T(8,128)(2,1)S(1)} %get-tuple-element.64), channel_id=1, source_target_pairs={{0,128},{64,192},{128,0},{192,64},{1,129},{65,193},{129,1},{193,65... | collective-permute-start | bytes 1228808 | tf_op jit(solution)/shard_map/ppermute | solution.py:44
  48.8 18.4 %collective-permute-start.24 = (bf16[320,640]{1,0:T(8,128)(2,1)S(1)}, bf16[320,640]{1,0:T(8,128)(2,1)S(1)}, u32[]{:S(2)}, u32[]{:S(2)}) collective-permute-start(bf16[320,640]{1,0:T(8,128)(2,1)S(1)} %get-tuple-element.65), channel_id=1, source_target_pairs={{0,192},{64,0},{128,64},{192,128},{1,193},{65,1},{129,65},{193,129... | collective-permute-start | bytes 1228808 | tf_op jit(solution)/shard_map/ppermute | solution.py:44
  59.4 9.8 %collective-permute-start.18 = (bf16[80,640]{1,0:T(8,128)(2,1)S(1)}, bf16[80,640]{1,0:T(8,128)(2,1)S(1)}, u32[]{:S(2)}, u32[]{:S(2)}) collective-permute-start(bf16[80,640]{1,0:T(8,128)(2,1)S(1)} %get-tuple-element.57), channel_id=1, source_target_pairs={{0,64},{64,128},{128,192},{192,0},{1,65},{65,129},{129,193},{193,1... | collective-permute-start | bytes 307208 | tf_op jit(solution)/shard_map/ppermute | solution.py:44
  61.1 10.3 %collective-permute-start.19 = (bf16[80,640]{1,0:T(8,128)(2,1)S(1)}, bf16[80,640]{1,0:T(8,128)(2,1)S(1)}, u32[]{:S(2)}, u32[]{:S(2)}) collective-permute-start(bf16[80,640]{1,0:T(8,128)(2,1)S(1)} %get-tuple-element.58), channel_id=1, source_target_pairs={{0,128},{64,192},{128,0},{192,64},{1,129},{65,193},{129,1},{193,65... | collective-permute-start | bytes 307208 | tf_op jit(solution)/shard_map/ppermute | solution.py:44
  62.0 9.5 %collective-permute-start.20 = (bf16[80,640]{1,0:T(8,128)(2,1)S(1)}, bf16[80,640]{1,0:T(8,128)(2,1)S(1)}, u32[]{:S(2)}, u32[]{:S(2)}) collective-permute-start(bf16[80,640]{1,0:T(8,128)(2,1)S(1)} %get-tuple-element.59), channel_id=1, source_target_pairs={{0,192},{64,0},{128,64},{192,128},{1,193},{65,1},{129,65},{193,129... | collective-permute-start | bytes 307208 | tf_op jit(solution)/shard_map/ppermute | solution.py:44
  68.1 39.6 %copy-start.3 = (bf16[192,1280]{1,0:T(8,128)(2,1)S(1)}, bf16[192,1280]{1,0:T(8,128)(2,1)}, u32[]{:S(2)}) copy-start(bf16[192,1280]{1,0:T(8,128)(2,1)} %copy-done.2) | copy-start | bytes 1474564
  68.1 8.2 %collective-permute-start.25 = (bf16[80,640]{1,0:T(8,128)(2,1)S(1)}, bf16[80,640]{1,0:T(8,128)(2,1)S(1)}, u32[]{:S(2)}, u32[]{:S(2)}) collective-permute-start(bf16[80,640]{1,0:T(8,128)(2,1)S(1)} %get-tuple-element.67), channel_id=1, source_target_pairs={{0,2},{2,4},{4,6},{6,0},{1,3},{3,5},{5,7},{7,1},{8,10},{10,12},{12... | collective-permute-start | bytes 307208 | tf_op jit(solution)/shard_map/ppermute | solution.py:44
  68.7 7.6 %collective-permute-start.26 = (bf16[80,640]{1,0:T(8,128)(2,1)S(1)}, bf16[80,640]{1,0:T(8,128)(2,1)S(1)}, u32[]{:S(2)}, u32[]{:S(2)}) collective-permute-start(bf16[80,640]{1,0:T(8,128)(2,1)S(1)} %get-tuple-element.68), channel_id=1, source_target_pairs={{0,4},{2,6},{4,0},{6,2},{1,5},{3,7},{5,1},{7,3},{8,12},{10,14},{12... | collective-permute-start | bytes 307208 | tf_op jit(solution)/shard_map/ppermute | solution.py:44
  69.3 7.7 %collective-permute-start.27 = (bf16[80,640]{1,0:T(8,128)(2,1)S(1)}, bf16[80,640]{1,0:T(8,128)(2,1)S(1)}, u32[]{:S(2)}, u32[]{:S(2)}) collective-permute-start(bf16[80,640]{1,0:T(8,128)(2,1)S(1)} %get-tuple-element.69), channel_id=1, source_target_pairs={{0,6},{2,0},{4,2},{6,4},{1,7},{3,1},{5,3},{7,5},{8,14},{10,8},{12,... | collective-permute-start | bytes 307208 | tf_op jit(solution)/shard_map/ppermute | solution.py:44
  77.8 36.8 %all-to-all-start = ((bf16[8,20,640]{2,1,0:T(8,128)(2,1)}), bf16[8,20,640]{2,1,0:T(8,128)(2,1)S(1)}, u32[]{:S(2)}, u32[]{:S(2)}) async-start(bf16[8,20,640]{2,1,0:T(8,128)(2,1)} %shard_map.120), calls=%async_computation | async-start | bytes 491520 | tf_op jit(solution)/shard_map/all_to_all | solution.py:481
  84.0 12.4 %collective-permute-start.9 = (bf16[192,640]{1,0:T(8,128)(2,1)}, bf16[192,640]{1,0:T(8,128)(2,1)S(1)}, u32[]{:S(2)}, u32[]{:S(2)}) collective-permute-start(bf16[192,640]{1,0:T(8,128)(2,1)} %copy-done.5), channel_id=1, source_target_pairs={{0,24},{8,0},{16,8},{24,16},{1,25},{9,1},{17,9},{25,17},{2,26},{10... | collective-permute-start | bytes 737288 | tf_op jit(solution)/shard_map/ppermute | solution.py:44
  87.9 15.3 %collective-permute-start.8 = (bf16[192,640]{1,0:T(8,128)(2,1)}, bf16[192,640]{1,0:T(8,128)(2,1)S(1)}, u32[]{:S(2)}, u32[]{:S(2)}) collective-permute-start(bf16[192,640]{1,0:T(8,128)(2,1)} %copy-done.5), channel_id=1, source_target_pairs={{0,8},{8,16},{16,24},{24,0},{1,9},{9,17},{17,25},{25,1},{2,10},{10... | collective-permute-start | bytes 737288 | tf_op jit(solution)/shard_map/ppermute | solution.py:44
  87.9 5.6 %collective-permute-start.10 = (bf16[40,640]{1,0:T(8,128)(2,1)S(1)}, bf16[40,640]{1,0:T(8,128)(2,1)S(1)}, u32[]{:S(2)}, u32[]{:S(2)}) collective-permute-start(bf16[40,640]{1,0:T(8,128)(2,1)S(1)} %get-tuple-element.45), channel_id=1, source_target_pairs={{0,32},{32,64},{64,96},{96,128},{128,160},{160,192},{192,224},{1,3... | collective-permute-start | bytes 153608 | tf_op jit(solution)/shard_map/ppermute | solution.py:363
  89.8 5.4 %collective-permute-start.11 = (bf16[40,640]{1,0:T(8,128)(2,1)S(1)}, bf16[40,640]{1,0:T(8,128)(2,1)S(1)}, u32[]{:S(2)}, u32[]{:S(2)}) collective-permute-start(bf16[40,640]{1,0:T(8,128)(2,1)S(1)} %get-tuple-element.46), channel_id=1, source_target_pairs={{32,0},{64,32},{96,64},{128,96},{160,128},{192,160},{224,192},{33,... | collective-permute-start | bytes 153608 | tf_op jit(solution)/shard_map/ppermute | solution.py:364
  103.8 6.3 %copy-start.6 = (bf16[192,640]{1,0:T(8,128)(2,1)S(1)}, bf16[192,640]{1,0:T(8,128)(2,1)}, u32[]{:S(2)}) copy-start(bf16[192,640]{1,0:T(8,128)(2,1)} %copy-done.5) | copy-start | bytes 737284
  103.8 6.3 %collective-permute-start.12 = (bf16[64,640]{1,0:T(8,128)(2,1)S(1)}, bf16[64,640]{1,0:T(8,128)(2,1)S(1)}, u32[]{:S(2)}, u32[]{:S(2)}) collective-permute-start(bf16[64,640]{1,0:T(8,128)(2,1)S(1)} %get-tuple-element.47), channel_id=1, source_target_pairs={{0,8},{8,16},{16,24},{24,0},{1,9},{9,17},{17,25},{25,1},{2,10},{10... | collective-permute-start | bytes 245768 | tf_op jit(solution)/shard_map/ppermute | solution.py:44
  103.9 6.2 %collective-permute-start.13 = (bf16[64,640]{1,0:T(8,128)(2,1)S(1)}, bf16[64,640]{1,0:T(8,128)(2,1)S(1)}, u32[]{:S(2)}, u32[]{:S(2)}) collective-permute-start(bf16[64,640]{1,0:T(8,128)(2,1)S(1)} %get-tuple-element.48), channel_id=1, source_target_pairs={{0,24},{8,0},{16,8},{24,16},{1,25},{9,1},{17,9},{25,17},{2,26},{10... | collective-permute-start | bytes 245768 | tf_op jit(solution)/shard_map/ppermute | solution.py:44
